TPU v7x, 128 devices: a whole 4x4x4 slice. The times are simulated.
128 devices in a mesh: gx: 4 (over z), gy: 32 (over x, y, core).
Axes of the slice: x: 4, y: 4, z: 4, core: 2. Of those that a mesh axis runs over, the one named last changes fastest.
Arguments:
- operator_blocks: bfloat16 [1024, 6, 256, 256], P(('gx', 'gy')), may hold values from -0.15625 to 0.15625
- local_columns: int32 [1024, 2], P(('gx', 'gy')), may hold values from 0 to 7
- remote_columns: int32 [1024, 4], P(('gx', 'gy')), may hold values from 8 to 41
- match_slots: int32 [1024, 6, 2], P(('gx', 'gy')), may hold values from 0 to 2
- tentative: bfloat16 [1024, 2, 256, 256], P(('gx', 'gy')), may hold values from -1.5 to 1.5
- inverse_diagonal: bfloat16 [1024, 256, 256], P(('gx', 'gy')), may hold values from -0.375 to 0.375
- peer_sends: int32 [128, 32], P(('gx', 'gy')), may hold values from 0 to 7
- slab_sends: int32 [128, 2], P(('gx', 'gy')), may hold values from 0 to 7
- coarse_slots: int32 [1024, 2, 2], P(('gx', 'gy')), may hold values from 0 to 63, as said below
Outputs:
- smoothed: bfloat16 [1024, 2, 256, 256], P(('gx', 'gy'))
- coarse_operator: bfloat16 [256, 256, 256], P(('gx', 'gy'))
Inputs may be any that keep to these rules, and one draw needn't show every extreme that they name: `match_slots`: the value 2 stands for no matching block. `coarse_slots`: no two partial blocks of one device name the same coarse block; coarse block c of a slab belongs to the device of gy index c // 2.
All inputs are finite; a program needn't handle non-finite values.
Results may differ from a plain program's by a relative error of at most 0.012.
Values may be sent and summed in bfloat16 or wider, within the bound.
No kernel may reach another device: no remote copies, remote signals or barrier semaphores. Data moves between devices by JAX's collectives and lax.ppermute only.
A program may use at most 128 MiB of HBM per device.

v0:
```python
import jax
import jax.numpy as jnp
from jax import lax
from jax.sharding import PartitionSpec as P

KP = 2
H = 1


def from_behind(value, axis, steps):
    count = lax.axis_size(axis)
    leading, last = (max(0, -steps), min(count, count - steps))
    return lax.ppermute(value, axis, [(source, source + steps) for source in range(leading, last)])


def select_blocks(picked, matches):
    selected = []
    for out_block in range(matches.shape[2]):
        chosen = jnp.zeros_like(picked[:, :, 0])
        for in_block in range(picked.shape[2]):
            matched = (matches[:, :, out_block] == in_block)[:, :, None, None]
            chosen = jnp.where(matched, picked[:, :, in_block], chosen)
        selected.append(chosen)
    return jnp.stack(selected, axis=2)


def block_product(blocks, lookup, columns, matches):
    chosen = select_blocks(lookup[columns], matches)
    return jnp.einsum("rkab,rknbc->rnac", blocks, chosen, preferred_element_type=jnp.float32)


def fetch_remote(fine_rows, peer_list, slab_list):
    outgoing = fine_rows[peer_list]
    from_peers = lax.all_to_all(outgoing, "gy", split_axis=0, concat_axis=0, tiled=True)
    from_below = from_behind(fine_rows[slab_list[:H]], "gx", 1)
    from_above = from_behind(fine_rows[slab_list[H:]], "gx", -1)
    return jnp.concatenate([from_peers, from_below, from_above], axis=0)


def apply_operator(
    operator_blocks, fine_rows, local_columns, remote_columns, match_slots, peer_list, slab_list
):
    lookup = jnp.concatenate([fine_rows, fetch_remote(fine_rows, peer_list, slab_list)], axis=0)
    columns = jnp.concatenate([local_columns, remote_columns], axis=1)
    return block_product(operator_blocks, lookup, columns, match_slots)


def body(
    operator_blocks,
    local_columns,
    remote_columns,
    match_slots,
    tentative,
    inverse_diagonal,
    peer_sends,
    slab_sends,
    coarse_slots,
):
    peer_list = peer_sends.reshape(-1)
    slab_list = slab_sends.reshape(-1)
    width = tentative.shape[-1]
    group_size = lax.axis_size("gy")
    owned_slots = (3 * tentative.shape[0] * KP * KP // 2 + group_size - 1) // group_size
    fine_rows = tentative
    for smooth_pass in range(2):
        product = apply_operator(
            operator_blocks,
            fine_rows,
            local_columns,
            remote_columns,
            match_slots,
            peer_list,
            slab_list,
        )
        image = product.astype(jnp.bfloat16)
        update = jnp.einsum(
            "rab,rnbc->rnac", inverse_diagonal, image, preferred_element_type=jnp.float32
        )
        fine_rows = (fine_rows.astype(jnp.float32) - update).astype(jnp.bfloat16)
    final_image = apply_operator(
        operator_blocks, fine_rows, local_columns, remote_columns, match_slots, peer_list, slab_list
    ).astype(jnp.bfloat16)
    partial_value = jnp.einsum(
        "rnab,rmac->rnmbc", fine_rows, final_image, preferred_element_type=jnp.float32
    )
    partial_value = partial_value.astype(jnp.bfloat16).reshape(-1, width, width)
    slot_blocks = (
        jnp.zeros((group_size * owned_slots, width, width), jnp.bfloat16)
        .at[coarse_slots.reshape(-1)]
        .set(partial_value)
    )
    received = lax.all_to_all(slot_blocks, "gy", split_axis=0, concat_axis=0, tiled=True)
    coarse = jnp.sum(
        received.reshape(group_size, owned_slots, width, width), axis=0, dtype=jnp.float32
    )
    return (fine_rows, coarse.astype(jnp.bfloat16))


def solution(mesh):
    placed = (
        P(("gx", "gy"), None, None, None),
        P(("gx", "gy"), None),
        P(("gx", "gy"), None),
        P(("gx", "gy"), None, None),
        P(("gx", "gy"), None, None, None),
        P(("gx", "gy"), None, None),
        P(("gx", "gy"), None),
        P(("gx", "gy"), None),
        P(("gx", "gy"), None, None),
    )
    return jax.shard_map(
        body,
        mesh=mesh,
        in_specs=placed,
        out_specs=(P(("gx", "gy"), None, None, None), P(("gx", "gy"), None, None)),
        check_vma=False,
    )
```

profile of v0, /device:TPU:0, one launch (start us, length us, event | category | flops | bytes accessed | tf_op | source)
XLA Modules:
  0.0 706.4 jit_solution(11862035279081874423)
XLA Ops:
  0.6 0.0 copy-start
  0.6 0.9 copy.51
  1.5 0.1 reshape.187
  1.6 0.7 fusion.59
  2.3 6.6 gather_fusion
  8.8 0.0 copy-start.4
  8.8 7.7 %all-to-all-start = ((bf16[32,2,256,256]{3,2,1,0:T(8,128)(2,1)}), bf16[32,2,256,256]{3,2,1,0:T(8,128)(2,1)}, u32[]{:S(2)}, u32[]{:S(2)}) async-start(bf16[32,2,256,256]{3,2,1,0:T(8,128)(2,1)} %gather_fusion), calls=%async_computation | async-start | bytes 16777216 | tf_op jit(solution)/shard_map/all_to_all | solution.py:34
  16.6 0.0 copy-done.6
  16.6 0.6 fusion.69
  21.0 0.0 copy-done.2
  21.1 0.8 constant_dynamic-slice_fusion.5
  21.9 3.8 collective-permute-start
  25.7 1.3 collective-permute-start.1
  27.0 0.0 copy-done.7
  27.0 0.1 copy.43
  27.1 0.0 copy-done.5
  27.1 0.1 copy.44
  27.2 0.1 compare_select_fusion
  27.3 0.1 reshape.340
  27.4 2.4 copy.41
  29.8 0.1 copy.71
  29.8 0.1 copy.74
  29.9 2.0 collective-permute-done
  31.9 4.2 collective-permute-done.1
  36.1 94.1 %all-to-all-done = bf16[32,2,256,256]{3,2,1,0:T(8,128)(2,1)} async-done(((bf16[32,2,256,256]{3,2,1,0:T(8,128)(2,1)}), bf16[32,2,256,256]{3,2,1,0:T(8,128)(2,1)}, u32[]{:S(2)}, u32[]{:S(2)}) %all-to-all-start) | async-done | bytes 8388640 | tf_op jit(solution)/shard_map/all_to_all | solution.py:34
  130.3 9.3 %pad_maximum_fusion = bf16[42,2,256,256]{3,2,1,0:T(8,128)(2,1)} fusion(bf16[1,2,256,256]{3,2,1,0:T(8,128)(2,1)} %collective-permute-done.1, bf16[1,2,256,256]{3,2,1,0:T(8,128)(2,1)S(1)} %collective-permute-done, bf16[32,2,256,256]{3,2,1,0:T(8,128)(2,1)} %all-to-all-done, bf16[8,2,256,256]{3,2,1,0:T(8,128)(2,1)S(1)} %copy-done.2), kind=kLoop, calls=%fused_computation.19 | loop fusion | flops 16515072 | bytes 22020096 | tf_op jit(solution)/shard_map/concatenate | solution.py:43
  139.6 10.4 %gather_fusion.1 = bf16[48,2,256,256]{3,2,1,0:T(8,128)(2,1)} fusion(bf16[42,2,256,256]{3,2,1,0:T(8,128)(2,1)} %pad_maximum_fusion, s32[1024]{0:T(1024)S(1)} %pad_clamp_fusion), kind=kCustom, calls=%fused_computation.1 | custom fusion | bytes 25166016 | tf_op jit(solution)/shard_map/gather | solution.py:28
  150.0 10.4 %fusion.67 = (bf16[8,6,1,256,256]{4,3,2,1,0:T(8,128)(2,1)}, bf16[8,6,1,256,256]{4,3,2,1,0:T(8,128)(2,1)}) fusion(bf16[8,6,2,256,256]{4,3,2,1,0:T(8,128)(2,1)} %bitcast.138), kind=kLoop, calls=%fused_computation.69 | loop fusion | bytes 25165824 | tf_op jit(solution)/shard_map/slice | solution.py:22
  160.4 8.6 %copy.72 = bf16[8,6,1,256,256]{3,4,1,2,0:T(8,128)(2,1)} copy(bf16[8,6,1,256,256]{4,3,2,1,0:T(8,128)(2,1)} %get-tuple-element.83) | data formatting | bytes 12582912
  169.1 8.6 %copy.73 = bf16[8,6,1,256,256]{3,4,1,2,0:T(8,128)(2,1)} copy(bf16[8,6,1,256,256]{4,3,2,1,0:T(8,128)(2,1)} %get-tuple-element.82) | data formatting | bytes 12582912
  177.7 10.3 %select_select_fusion.5 = (bf16[8,6,1,256,256]{3,4,1,2,0:T(8,128)(2,1)}, bf16[8,6,1,256,256]{3,4,1,2,0:T(8,128)(2,1)}) fusion(bf16[8,6,1,256,256]{3,4,1,2,0:T(8,128)(2,1)} %copy.72, bf16[8,6,1,256,256]{3,4,1,2,0:T(8,128)(2,1)} %copy.73, pred[8,6]{1,0:T(8,128)(4,1)S(1)} %get-tuple-element.100, pred[8,6]{1,0:T(8,128)(4,1)S(1)} %get-tuple-element.101, ...), kind=kLoop, calls=%fused_computation.34 | loop fusion | flops 12582912 | bytes 25166016 | tf_op jit(solution)/shard_map/jit(_where)/select_n | solution.py:22
  188.0 0.0 copy-done
  188.0 9.1 %fusion.16 = bf16[8,2,256,256]{2,3,1,0:T(8,128)(2,1)S(1)} fusion(bf16[8,2,256,256]{2,3,1,0:T(8,128)(2,1)} %copy.41, bf16[8,6,256,256]{3,2,1,0:T(8,128)(2,1)} %param.9, bf16[8,6,1,256,256]{3,4,1,2,0:T(8,128)(2,1)} %get-tuple-element.81, bf16[8,6,1,256,256]{3,4,1,2,0:T(8,128)(2,1)} %get-tuple-element.80, bf16[8,256,256]{2,1,0:T(8,128)(2,1)S(1)} %copy-done), kind=kOutput, calls=%fused_computation.40 | convolution fusion | flops 3768582144 | bytes 24117248 | tf_op jit(solution)/shard_map/rab,rnbc->rnac/dot_general | solution.py:76
  197.1 0.0 copy-start.3
  197.1 5.0 gather_fusion.2
  202.1 16.4 %all-to-all-start.1 = ((bf16[32,2,256,256]{2,3,1,0:T(8,128)(2,1)}), bf16[32,2,256,256]{2,3,1,0:T(8,128)(2,1)}, u32[]{:S(2)}, u32[]{:S(2)}) async-start(bf16[32,2,256,256]{2,3,1,0:T(8,128)(2,1)} %gather_fusion.2), calls=%async_computation.1 | async-start | bytes 16777216 | tf_op jit(solution)/shard_map/all_to_all | solution.py:34
  218.5 3.8 collective-permute-start.2
  222.3 1.5 collective-permute-start.3
  223.8 4.4 collective-permute-done.2
  228.2 4.4 collective-permute-done.3
  232.6 99.6 %all-to-all-done.1 = bf16[32,2,256,256]{2,3,1,0:T(8,128)(2,1)} async-done(((bf16[32,2,256,256]{2,3,1,0:T(8,128)(2,1)}), bf16[32,2,256,256]{2,3,1,0:T(8,128)(2,1)}, u32[]{:S(2)}, u32[]{:S(2)}) %all-to-all-start.1) | async-done | bytes 8388640 | tf_op jit(solution)/shard_map/all_to_all | solution.py:34
  332.2 9.3 %pad_maximum_fusion.1 = bf16[42,2,256,256]{2,3,1,0:T(8,128)(2,1)} fusion(bf16[1,2,256,256]{2,3,1,0:T(8,128)(2,1)} %collective-permute-done.3, bf16[1,2,256,256]{2,3,1,0:T(8,128)(2,1)S(1)} %collective-permute-done.2, bf16[32,2,256,256]{2,3,1,0:T(8,128)(2,1)} %all-to-all-done.1, bf16[8,2,256,256]{2,3,1,0:T(8,128)(2,1)S(1)} %fusion.16), kind=kLoop, calls=%fused_computation.20 | loop fusion | flops 16515072 | bytes 22020096 | tf_op jit(solution)/shard_map/concatenate | solution.py:43
  341.5 10.4 %gather_fusion.3 = bf16[48,2,256,256]{2,3,1,0:T(8,128)(2,1)} fusion(bf16[42,2,256,256]{2,3,1,0:T(8,128)(2,1)} %pad_maximum_fusion.1, s32[1024]{0:T(1024)S(1)} %pad_clamp_fusion), kind=kCustom, calls=%fused_computation.3 | custom fusion | bytes 25166016 | tf_op jit(solution)/shard_map/gather | solution.py:28
  351.9 10.3 %select_select_fusion.3 = (bf16[8,6,1,256,256]{3,4,1,2,0:T(8,128)(2,1)}, bf16[8,6,1,256,256]{3,4,1,2,0:T(8,128)(2,1)}) fusion(pred[8,6]{1,0:T(8,128)(4,1)S(1)} %get-tuple-element.100, pred[8,6]{1,0:T(8,128)(4,1)S(1)} %get-tuple-element.101, bf16[8,6,2,256,256]{3,4,2,1,0:T(8,128)(2,1)} %bitcast.140, pred[8,6]{1,0:T(8,128)(4,1)S(1)} %get-tuple-element.95, ...), kind=kLoop, calls=%fused_computation.32 | loop fusion | flops 12582912 | bytes 25166016 | tf_op jit(solution)/shard_map/jit(_where)/select_n | solution.py:22
  362.3 9.1 %fusion.15 = bf16[8,2,256,256]{2,3,1,0:T(8,128)(2,1)S(1)} fusion(bf16[8,2,256,256]{2,3,1,0:T(8,128)(2,1)} %copy-done.3, bf16[8,6,256,256]{3,2,1,0:T(8,128)(2,1)} %param.9, bf16[8,6,1,256,256]{3,4,1,2,0:T(8,128)(2,1)} %get-tuple-element.79, bf16[8,6,1,256,256]{3,4,1,2,0:T(8,128)(2,1)} %get-tuple-element.78, bf16[8,256,256]{2,1,0:T(8,128)(2,1)S(1)} %copy-done), kind=kOutput, calls=%fused_computation.37 | convolution fusion | flops 3768582144 | bytes 24117248 | tf_op jit(solution)/shard_map/rab,rnbc->rnac/dot_general | solution.py:76
  371.3 5.0 gather_fusion.4
  376.3 16.4 %all-to-all-start.2 = ((bf16[32,2,256,256]{2,3,1,0:T(8,128)(2,1)}), bf16[32,2,256,256]{2,3,1,0:T(8,128)(2,1)}, u32[]{:S(2)}, u32[]{:S(2)}) async-start(bf16[32,2,256,256]{2,3,1,0:T(8,128)(2,1)} %gather_fusion.4), calls=%async_computation.2 | async-start | bytes 16777216 | tf_op jit(solution)/shard_map/all_to_all | solution.py:34
  392.7 3.7 collective-permute-start.4
  396.4 1.3 collective-permute-start.5
  397.7 4.6 collective-permute-done.4
  402.3 4.4 collective-permute-done.5
  406.7 99.7 %all-to-all-done.2 = bf16[32,2,256,256]{2,3,1,0:T(8,128)(2,1)} async-done(((bf16[32,2,256,256]{2,3,1,0:T(8,128)(2,1)}), bf16[32,2,256,256]{2,3,1,0:T(8,128)(2,1)}, u32[]{:S(2)}, u32[]{:S(2)}) %all-to-all-start.2) | async-done | bytes 8388640 | tf_op jit(solution)/shard_map/all_to_all | solution.py:34
  506.4 11.5 %pad_maximum_fusion.2 = bf16[42,2,256,256]{2,3,1,0:T(8,128)(2,1)} fusion(bf16[1,2,256,256]{2,3,1,0:T(8,128)(2,1)S(1)} %collective-permute-done.5, bf16[1,2,256,256]{2,3,1,0:T(8,128)(2,1)S(1)} %collective-permute-done.4, bf16[32,2,256,256]{2,3,1,0:T(8,128)(2,1)} %all-to-all-done.2, bf16[8,2,256,256]{2,3,1,0:T(8,128)(2,1)S(1)} %fusion.15), kind=kLoop, calls=%fused_computation.21 | loop fusion | flops 16515072 | bytes 22020096 | tf_op jit(solution)/shard_map/concatenate | solution.py:43
  517.8 10.4 %gather_fusion.5 = bf16[48,2,256,256]{2,3,1,0:T(8,128)(2,1)} fusion(bf16[42,2,256,256]{2,3,1,0:T(8,128)(2,1)} %pad_maximum_fusion.2, s32[1024]{0:T(1024)S(1)} %pad_clamp_fusion), kind=kCustom, calls=%fused_computation.5 | custom fusion | bytes 25166016 | tf_op jit(solution)/shard_map/gather | solution.py:28
  528.3 10.3 %select_select_fusion.1 = (bf16[8,6,1,256,256]{3,4,1,2,0:T(8,128)(2,1)}, bf16[8,6,1,256,256]{3,4,1,2,0:T(8,128)(2,1)}) fusion(pred[8,6]{1,0:T(8,128)(4,1)S(1)} %get-tuple-element.100, pred[8,6]{1,0:T(8,128)(4,1)S(1)} %get-tuple-element.101, bf16[8,6,2,256,256]{3,4,2,1,0:T(8,128)(2,1)} %bitcast.139, pred[8,6]{1,0:T(8,128)(4,1)S(1)} %get-tuple-element.95, ...), kind=kLoop, calls=%fused_computation.30 | loop fusion | flops 12582912 | bytes 25166016 | tf_op jit(solution)/shard_map/jit(_where)/select_n | solution.py:22
  538.6 10.1 %convert_bitcast_fusion = bf16[8,2,2,256,256]{3,4,1,2,0:T(8,128)(2,1)} fusion(bf16[8,2,256,256]{2,3,1,0:T(8,128)(2,1)S(1)} %fusion.15, bf16[8,6,256,256]{3,2,1,0:T(8,128)(2,1)} %param.9, bf16[8,6,1,256,256]{3,4,1,2,0:T(8,128)(2,1)} %get-tuple-element.77, bf16[8,6,1,256,256]{3,4,1,2,0:T(8,128)(2,1)} %get-tuple-element.76), kind=kOutput, calls=%fused_computation.42 | convolution fusion | flops 4304404480 | bytes 25165824 | tf_op jit(solution)/shard_map/rnab,rmac->rnmbc/dot_general | solution.py:83
  548.8 6.4 copy.56
  555.2 4.3 broadcast_in_dim.85
  559.5 11.4 %scatter_fusion = bf16[64,256,256]{2,1,0:T(8,128)(2,1)} fusion(bf16[64,256,256]{2,1,0:T(8,128)(2,1)} %broadcast_in_dim.85, s32[32]{0:T(128)S(1)} %get-tuple-element.99, bf16[32,256,256]{2,1,0:T(8,128)(2,1)} %bitcast.141), kind=kCustom, calls=%fused_computation.6 | custom fusion | bytes 12583040 | tf_op jit(solution)/shard_map/scatter | solution.py:90
  570.9 16.3 %all-to-all-start.3 = ((bf16[64,256,256]{2,1,0:T(8,128)(2,1)}), bf16[64,256,256]{2,1,0:T(8,128)(2,1)}, u32[]{:S(2)}, u32[]{:S(2)}) async-start(bf16[64,256,256]{2,1,0:T(8,128)(2,1)} %scatter_fusion), calls=%async_computation.3 | async-start | bytes 16777216 | tf_op jit(solution)/shard_map/all_to_all | solution.py:92
  587.2 0.0 copy-start.1
  587.2 2.4 copy.57
  589.6 111.3 %all-to-all-done.3 = bf16[64,256,256]{2,1,0:T(8,128)(2,1)} async-done(((bf16[64,256,256]{2,1,0:T(8,128)(2,1)}), bf16[64,256,256]{2,1,0:T(8,128)(2,1)}, u32[]{:S(2)}, u32[]{:S(2)}) %all-to-all-start.3) | async-done | bytes 8388640 | tf_op jit(solution)/shard_map/all_to_all | solution.py:92
  700.9 5.5 reduce_sum.12
  (13 shorter events, 0.1 us)
Async XLA Ops:
  0.6 187.4 %copy-start = (bf16[8,256,256]{2,1,0:T(8,128)(2,1)S(1)}, bf16[8,256,256]{2,1,0:T(8,128)(2,1)}, u32[]{:S(2)}) copy-start(bf16[8,256,256]{2,1,0:T(8,128)(2,1)} %param.14) | copy-start | bytes 3145732
  8.8 7.7 %copy-start.6 = (s32[1,2]{1,0:T(1,128)S(1)}, s32[1,2]{1,0:T(1,128)}, u32[]{:S(2)}) copy-start(s32[1,2]{1,0:T(1,128)} %param.16) | copy-start | bytes 28
  8.8 12.2 %copy-start.2 = (bf16[8,2,256,256]{3,2,1,0:T(8,128)(2,1)S(1)}, bf16[8,2,256,256]{3,2,1,0:T(8,128)(2,1)}, u32[]{:S(2)}) copy-start(bf16[8,2,256,256]{3,2,1,0:T(8,128)(2,1)} %param.13) | copy-start | bytes 6291460
  8.8 18.2 %copy-start.7 = (s32[8,2]{0,1:T(2,128)S(1)}, s32[8,2]{0,1:T(2,128)}, u32[]{:S(2)}) copy-start(s32[8,2]{0,1:T(2,128)} %param.10) | copy-start | bytes 196
  8.8 18.3 %copy-start.5 = (s32[8,4]{0,1:T(4,128)S(1)}, s32[8,4]{0,1:T(4,128)}, u32[]{:S(2)}) copy-start(s32[8,4]{0,1:T(4,128)} %param.11) | copy-start | bytes 388
  8.8 18.5 %copy-start.4 = (s32[8,6,2]{0,2,1:T(2,128)S(1)}, s32[8,6,2]{0,2,1:T(2,128)}, u32[]{:S(2)}) copy-start(s32[8,6,2]{0,2,1:T(2,128)} %param.12) | copy-start | bytes 1156
  8.8 121.4 %all-to-all-start = ((bf16[32,2,256,256]{3,2,1,0:T(8,128)(2,1)}), bf16[32,2,256,256]{3,2,1,0:T(8,128)(2,1)}, u32[]{:S(2)}, u32[]{:S(2)}) async-start(bf16[32,2,256,256]{3,2,1,0:T(8,128)(2,1)} %gather_fusion), calls=%async_computation | async-start | bytes 16777216 | tf_op jit(solution)/shard_map/all_to_all | solution.py:34
  21.9 10.0 %collective-permute-start = (bf16[1,2,256,256]{3,2,1,0:T(8,128)(2,1)}, bf16[1,2,256,256]{3,2,1,0:T(8,128)(2,1)S(1)}, u32[]{:S(2)}, u32[]{:S(2)}) collective-permute-start(bf16[1,2,256,256]{3,2,1,0:T(8,128)(2,1)} %get-tuple-element.88), channel_id=1, source_target_pairs={{0,32},{32,64},{64,96},{1,33},{33,65},{65,97},{2,34},{34,66},{66,9... | collective-permute-start | bytes 786440 | tf_op jit(solution)/shard_map/ppermute | solution.py:13
  25.7 10.4 %collective-permute-start.1 = (bf16[1,2,256,256]{3,2,1,0:T(8,128)(2,1)}, bf16[1,2,256,256]{3,2,1,0:T(8,128)(2,1)}, u32[]{:S(2)}, u32[]{:S(2)}) collective-permute-start(bf16[1,2,256,256]{3,2,1,0:T(8,128)(2,1)} %get-tuple-element.89), channel_id=1, source_target_pairs={{32,0},{64,32},{96,64},{33,1},{65,33},{97,65},{34,2},{66,34},{98,6... | collective-permute-start | bytes 786440 | tf_op jit(solution)/shard_map/ppermute | solution.py:13
  197.1 135.0 %copy-start.3 = (bf16[8,2,256,256]{2,3,1,0:T(8,128)(2,1)}, bf16[8,2,256,256]{2,3,1,0:T(8,128)(2,1)S(1)}, u32[]{:S(2)}) copy-start(bf16[8,2,256,256]{2,3,1,0:T(8,128)(2,1)S(1)} %fusion.16) | copy-start | bytes 6291460
  202.1 130.1 %all-to-all-start.1 = ((bf16[32,2,256,256]{2,3,1,0:T(8,128)(2,1)}), bf16[32,2,256,256]{2,3,1,0:T(8,128)(2,1)}, u32[]{:S(2)}, u32[]{:S(2)}) async-start(bf16[32,2,256,256]{2,3,1,0:T(8,128)(2,1)} %gather_fusion.2), calls=%async_computation.1 | async-start | bytes 16777216 | tf_op jit(solution)/shard_map/all_to_all | solution.py:34
  218.5 9.7 %collective-permute-start.2 = (bf16[1,2,256,256]{2,3,1,0:T(8,128)(2,1)S(1)}, bf16[1,2,256,256]{2,3,1,0:T(8,128)(2,1)S(1)}, u32[]{:S(2)}, u32[]{:S(2)}) collective-permute-start(bf16[1,2,256,256]{2,3,1,0:T(8,128)(2,1)S(1)} %get-tuple-element.86), channel_id=1, source_target_pairs={{0,32},{32,64},{64,96},{1,33},{33,65},{65,97},{2,34},{34,66},{66,9... | collective-permute-start | bytes 786440 | tf_op jit(solution)/shard_map/ppermute | solution.py:13
  222.3 10.3 %collective-permute-start.3 = (bf16[1,2,256,256]{2,3,1,0:T(8,128)(2,1)S(1)}, bf16[1,2,256,256]{2,3,1,0:T(8,128)(2,1)}, u32[]{:S(2)}, u32[]{:S(2)}) collective-permute-start(bf16[1,2,256,256]{2,3,1,0:T(8,128)(2,1)S(1)} %get-tuple-element.87), channel_id=1, source_target_pairs={{32,0},{64,32},{96,64},{33,1},{65,33},{97,65},{34,2},{66,34},{98,6... | collective-permute-start | bytes 786440 | tf_op jit(solution)/shard_map/ppermute | solution.py:13
  376.3 130.1 %all-to-all-start.2 = ((bf16[32,2,256,256]{2,3,1,0:T(8,128)(2,1)}), bf16[32,2,256,256]{2,3,1,0:T(8,128)(2,1)}, u32[]{:S(2)}, u32[]{:S(2)}) async-start(bf16[32,2,256,256]{2,3,1,0:T(8,128)(2,1)} %gather_fusion.4), calls=%async_computation.2 | async-start | bytes 16777216 | tf_op jit(solution)/shard_map/all_to_all | solution.py:34
  392.7 9.6 %collective-permute-start.4 = (bf16[1,2,256,256]{2,3,1,0:T(8,128)(2,1)S(1)}, bf16[1,2,256,256]{2,3,1,0:T(8,128)(2,1)S(1)}, u32[]{:S(2)}, u32[]{:S(2)}) collective-permute-start(bf16[1,2,256,256]{2,3,1,0:T(8,128)(2,1)S(1)} %get-tuple-element.84), channel_id=1, source_target_pairs={{0,32},{32,64},{64,96},{1,33},{33,65},{65,97},{2,34},{34,66},{66,9... | collective-permute-start | bytes 786440 | tf_op jit(solution)/shard_map/ppermute | solution.py:13
  396.4 10.3 %collective-permute-start.5 = (bf16[1,2,256,256]{2,3,1,0:T(8,128)(2,1)S(1)}, bf16[1,2,256,256]{2,3,1,0:T(8,128)(2,1)S(1)}, u32[]{:S(2)}, u32[]{:S(2)}) collective-permute-start(bf16[1,2,256,256]{2,3,1,0:T(8,128)(2,1)S(1)} %get-tuple-element.85), channel_id=1, source_target_pairs={{32,0},{64,32},{96,64},{33,1},{65,33},{97,65},{34,2},{66,34},{98,6... | collective-permute-start | bytes 786440 | tf_op jit(solution)/shard_map/ppermute | solution.py:13
  570.9 130.0 %all-to-all-start.3 = ((bf16[64,256,256]{2,1,0:T(8,128)(2,1)}), bf16[64,256,256]{2,1,0:T(8,128)(2,1)}, u32[]{:S(2)}, u32[]{:S(2)}) async-start(bf16[64,256,256]{2,1,0:T(8,128)(2,1)} %scatter_fusion), calls=%async_computation.3 | async-start | bytes 16777216 | tf_op jit(solution)/shard_map/all_to_all | solution.py:92
  587.2 119.2 %copy-start.1 = (bf16[8,256,256]{2,1,0:T(8,128)(2,1)S(1)}, bf16[8,256,256]{2,1,0:T(8,128)(2,1)}, u32[]{:S(2)}) copy-start(bf16[8,256,256]{2,1,0:T(8,128)(2,1)} %param.14) | copy-start | bytes 3145732
where the time goes:
time: 719 us; the launch traced here: 706 us
  waiting for transfers between devices  429 us (60%)
  local copies, waits for them, and re-layouts  105 us (15%)
  starting transfers between devices  72 us (10%)
  other arithmetic  67.4 us (9%)
  matrix products  28.3 us (4%)
    all_to_all x3, waiting for transfers between devices, fetch_remote(): lax.all_to_all(outgoing, 'gy', split_axis=0, concat_axis=0, tiled=True)  293 us
    all_to_all x1, waiting for transfers between devices, body(): lax.all_to_all(slot_blocks, 'gy', split_axis=0, concat_axis=0, tiled=True)  111 us
    all_to_all x3, starting transfers between devices, fetch_remote(): lax.all_to_all(outgoing, 'gy', split_axis=0, concat_axis=0, tiled=True)  40.4 us
    gather x3, local copies, waits for them, and re-layouts, block_product(): chosen = select_blocks(lookup[columns], matches)  31.3 us
    select_n x3, other arithmetic, select_blocks(): chosen = jnp.where(matched, picked[:, :, in_block], chosen)  31 us
    concatenate x3, other arithmetic, apply_operator(): jnp.concatenate([fine_rows, fetch_remote(fine_rows, peer_list, slab_list)...  30.1 us
    ppermute x6, waiting for transfers between devices, from_behind(): lax.ppermute(value, axis, [(source, source + steps) for source in range(l...  24 us
    unnamed x23, local copies, waits for them, and re-layouts  23.1 us
  transfers between devices with their start and end apart: 10, of which 10 were waited for; matrix products, arithmetic and copies ran while one was open for 1% of the time, Pallas kernels for 0%

commit v1 on v0

v1 whole, which is shorter than its diff:
```python
import functools

import jax
import jax.numpy as jnp
from jax import lax
from jax.experimental import pallas as pl
from jax.experimental.pallas import tpu as pltpu
from jax.sharding import Mesh
from jax.sharding import PartitionSpec as P

AXES = ("gx", "x", "y", "c")
GY = ("x", "y", "c")


def shifted(value, axis, steps):
    count = lax.axis_size(axis)
    first, last = (max(0, -steps), min(count, count - steps))
    return lax.ppermute(value, axis, [(source, source + steps) for source in range(first, last)])


def send_rows(peer_ref, slab_ref, rows_ref, out_ref, up_ref, down_ref, sems):
    copies = []
    for q in range(out_ref.shape[0]):
        copies.append(pltpu.make_async_copy(rows_ref.at[peer_ref[q]], out_ref.at[q], sems.at[q]))
    copies.append(pltpu.make_async_copy(rows_ref.at[slab_ref[0]], up_ref.at[0], sems.at[len(copies)]))
    copies.append(pltpu.make_async_copy(rows_ref.at[slab_ref[1]], down_ref.at[0], sems.at[len(copies)]))
    for copy in copies:
        copy.start()
    for copy in copies:
        copy.wait()


def outgoing_shapes(peers, blocks, width):
    one = jax.ShapeDtypeStruct((1, blocks, width, width), jnp.bfloat16)
    return (jax.ShapeDtypeStruct((peers, blocks, width, width), jnp.bfloat16), one, one)


def pack_kernel(peer_ref, slab_ref, rows_ref, out_ref, up_ref, down_ref, sems):
    send_rows(peer_ref, slab_ref, rows_ref, out_ref, up_ref, down_ref, sems)


def pack(peer_list, slab_list, rows):
    count, blocks, width, _ = rows.shape
    peers = peer_list.shape[0]
    anywhere = pl.BlockSpec(memory_space=pl.ANY)
    return pl.pallas_call(
        pack_kernel,
        grid_spec=pltpu.PrefetchScalarGridSpec(
            num_scalar_prefetch=2,
            grid=(1,),
            in_specs=[pl.BlockSpec(rows.shape, lambda i, *refs: (0, 0, 0, 0))],
            out_specs=[anywhere] * 3,
            scratch_shapes=[pltpu.SemaphoreType.DMA((peers + 2,))],
        ),
        out_shape=outgoing_shapes(peers, blocks, width),
        name="pack_rows",
    )(peer_list, slab_list, rows)


def gather_operand(columns, matches, own_ref, peers, low_ref, high_ref, rhs, i, own_count, peer_count):
    width = own_ref.shape[-1]
    local = 2
    for k in range(rhs.shape[0] // width):
        column = columns[i * 6 + k]
        for n in range(2):
            match = matches[(i * 6 + k) * 2 + n]
            there = jnp.minimum(match, 1)
            place = (pl.ds(k * width, width), pl.ds(n * width, width))

            @pl.when(match > 1)
            def _():
                rhs[place] = jnp.zeros((width, width), rhs.dtype)

            if k < local:

                @pl.when(match < 2)
                def _():
                    rhs[place] = own_ref[column, there]
            else:
                peer_ref = peers[k - local]

                @pl.when((match < 2) & (column < own_count + peer_count))
                def _():
                    rhs[place] = peer_ref[0, there]

                @pl.when((match < 2) & (column == own_count + peer_count))
                def _():
                    rhs[place] = low_ref[0, there]

                @pl.when((match < 2) & (column > own_count + peer_count))
                def _():
                    rhs[place] = high_ref[0, there]


def row_image(a_ref, rhs):
    lhs = jnp.concatenate([a_ref[0, k] for k in range(a_ref.shape[1])], axis=1)
    return jnp.dot(lhs, rhs[...], preferred_element_type=jnp.float32).astype(jnp.bfloat16)


def smooth_kernel(
    columns, matches, peer_list, slab_list,
    a_ref, d_ref, own_ref, r0, r1, r2, r3, low_ref, high_ref,
    rows_out, out_ref, up_ref, down_ref,
    rhs, kept, sems,
):
    i = pl.program_id(0)
    width = own_ref.shape[-1]
    gather_operand(columns, matches, own_ref, (r0, r1, r2, r3), low_ref, high_ref, rhs, i, own_ref.shape[0], out_ref.shape[0])
    image = row_image(a_ref, rhs)
    update = jnp.dot(d_ref[0], image, preferred_element_type=jnp.float32)
    for n in range(2):
        new = own_ref[i, n].astype(jnp.float32) - update[:, n * width : (n + 1) * width]
        new = new.astype(jnp.bfloat16)
        rows_out[0, n] = new
        kept[i, n] = new

    @pl.when(i == pl.num_programs(0) - 1)
    def _():
        send_rows(peer_list, slab_list, kept, out_ref, up_ref, down_ref, sems)


def final_kernel(
    columns, matches, slots, core,
    a_ref, own_ref, r0, r1, r2, r3, low_ref, high_ref,
    keep_ref, swap_ref,
    rhs,
):
    i = pl.program_id(0)
    width = own_ref.shape[-1]

    @pl.when(i == 0)
    def _():
        keep_ref[...] = jnp.zeros_like(keep_ref)
        swap_ref[...] = jnp.zeros_like(swap_ref)

    gather_operand(columns, matches, own_ref, (r0, r1, r2, r3), low_ref, high_ref, rhs, i, own_ref.shape[0], 32)
    image = row_image(a_ref, rhs)
    mine = jnp.concatenate([own_ref[i, n] for n in range(2)], axis=1)
    partial = lax.dot_general(mine, image, (((0,), (0,)), ((), ())), preferred_element_type=jnp.float32)
    partial = partial.astype(jnp.bfloat16)
    for n1 in range(2):
        for n2 in range(2):
            slot = slots[(i * 2 + n1) * 2 + n2]
            owner = slot // 2
            place = (owner // 2) * 2 + slot % 2
            block = partial[n1 * width : (n1 + 1) * width, n2 * width : (n2 + 1) * width]

            @pl.when(owner % 2 == core[0])
            def _():
                keep_ref[place] = block

            @pl.when(owner % 2 != core[0])
            def _():
                swap_ref[place] = block


def operand_specs(rows, blocks, width, inner, peers):
    def peer_spec(k):
        def index(i, columns, *refs):
            return (jnp.clip(columns[i * inner + k] - rows, 0, peers - 1), 0, 0, 0)

        return pl.BlockSpec((1, blocks, width, width), index)

    whole = pl.BlockSpec((rows, blocks, width, width), lambda i, *refs: (0, 0, 0, 0))
    single = pl.BlockSpec((1, blocks, width, width), lambda i, *refs: (0, 0, 0, 0))
    return [whole, *[peer_spec(k) for k in range(2, inner)], single, single]


def smooth(tables, peer_list, slab_list, operator, inverse, rows, received, low, high):
    count, inner, width, _ = operator.shape
    blocks = rows.shape[1]
    peers = received.shape[0]
    anywhere = pl.BlockSpec(memory_space=pl.ANY)
    outs = outgoing_shapes(peers, blocks, width)
    return pl.pallas_call(
        smooth_kernel,
        grid_spec=pltpu.PrefetchScalarGridSpec(
            num_scalar_prefetch=4,
            grid=(count,),
            in_specs=[
                pl.BlockSpec((1, inner, width, width), lambda i, *refs: (i, 0, 0, 0)),
                pl.BlockSpec((1, width, width), lambda i, *refs: (i, 0, 0)),
                *operand_specs(count, blocks, width, inner, peers),
            ],
            out_specs=[pl.BlockSpec((1, blocks, width, width), lambda i, *refs: (i, 0, 0, 0)), anywhere, anywhere, anywhere],
            scratch_shapes=[
                pltpu.VMEM((inner * width, blocks * width), jnp.bfloat16),
                pltpu.VMEM((count, blocks, width, width), jnp.bfloat16),
                pltpu.SemaphoreType.DMA((peers + 2,)),
            ],
        ),
        out_shape=(jax.ShapeDtypeStruct(rows.shape, jnp.bfloat16), *outs),
        compiler_params=pltpu.CompilerParams(vmem_limit_bytes=40 << 20),
        name="smooth_rows",
    )(*tables, peer_list, slab_list, operator, inverse, rows, received, received, received, received, low, high)


def galerkin(tables, slots, core, operator, rows, received, low, high):
    count, inner, width, _ = operator.shape
    blocks = rows.shape[1]
    peers = received.shape[0]
    half = jax.ShapeDtypeStruct((peers, width, width), jnp.bfloat16)
    half_spec = pl.BlockSpec((peers, width, width), lambda i, *refs: (0, 0, 0))
    return pl.pallas_call(
        final_kernel,
        grid_spec=pltpu.PrefetchScalarGridSpec(
            num_scalar_prefetch=4,
            grid=(count,),
            in_specs=[
                pl.BlockSpec((1, inner, width, width), lambda i, *refs: (i, 0, 0, 0)),
                *operand_specs(count, blocks, width, inner, peers),
            ],
            out_specs=[half_spec, half_spec],
            scratch_shapes=[pltpu.VMEM((inner * width, blocks * width), jnp.bfloat16)],
        ),
        out_shape=(half, half),
        compiler_params=pltpu.CompilerParams(vmem_limit_bytes=48 << 20),
        name="galerkin_rows",
    )(*tables, slots, core, operator, rows, received, received, received, received, low, high)


def body(
    operator_blocks,
    local_columns,
    remote_columns,
    match_slots,
    tentative,
    inverse_diagonal,
    peer_sends,
    slab_sends,
    coarse_slots,
):
    peer_list = peer_sends.reshape(-1)
    slab_list = slab_sends.reshape(-1)
    columns = jnp.concatenate([local_columns, remote_columns], axis=1).reshape(-1)
    tables = (columns, match_slots.reshape(-1))
    core = lax.axis_index("c").reshape(1).astype(jnp.int32)

    def exchange(outgoing, up, down):
        received = lax.all_to_all(outgoing, GY, split_axis=0, concat_axis=0, tiled=True)
        return received, shifted(up, "gx", 1), shifted(down, "gx", -1)

    rows = tentative
    outgoing = pack(peer_list, slab_list, rows)
    for smooth_pass in range(2):
        arrived = exchange(*outgoing)
        rows, *outgoing = smooth(tables, peer_list, slab_list, operator_blocks, inverse_diagonal, rows, *arrived)
    arrived = exchange(*outgoing)
    keep, swap = galerkin(tables, coarse_slots.reshape(-1), core, operator_blocks, rows, *arrived)
    other = lax.ppermute(swap, "c", [(0, 1), (1, 0)])
    chip = (keep.astype(jnp.float32) + other.astype(jnp.float32)).astype(jnp.bfloat16)
    width = chip.shape[-1]
    received = lax.all_to_all(chip, ("x", "y"), split_axis=0, concat_axis=0, tiled=True)
    coarse = jnp.sum(received.reshape(-1, 2, width, width), axis=0, dtype=jnp.float32)
    return (rows, coarse.astype(jnp.bfloat16))


def solution(mesh):
    fine = Mesh(mesh.devices.reshape(4, 4, 4, 2), AXES)
    placed = tuple(P(AXES, *[None] * extra) for extra in (3, 1, 1, 2, 3, 2, 1, 1, 2))
    return jax.shard_map(
        body,
        mesh=fine,
        in_specs=placed,
        out_specs=(P(AXES, None, None, None), P(AXES, None, None)),
        check_vma=False,
    )
```

time: 719 us -> 530 us (0.74); the launches traced: 706 us -> 529 us
  waiting for transfers between devices: 429 us -> 332 us
  local copies, waits for them, and re-layouts: 105 us -> 12 us
  blocking collectives: 0 us -> 67.2 us
  other arithmetic: 67.4 us -> 7.24 us
  Pallas kernels: 0 us -> 53.4 us
  matrix products: 28.3 us -> 0 us
  starting transfers between devices: 72 us -> 56.5 us
    all_to_all x4 -> x3, waiting for transfers between devices: 405 us -> 298 us  [exchange(): lax.all_to_all(outgoing, GY, split_axis=0, concat_axis=0, tiled=True)]
    all_to_all x0 -> x1, blocking collectives: none -> 67.2 us  [body(): lax.all_to_all(chip, ('x', 'y'), split_axis=0, concat_axis=0, tiled=True)]
    pallas_call x0 -> x4, Pallas kernels: none -> 53.4 us  [the longest x2 30.4 us: smooth(): pl.pallas_call(smooth_kernel, grid_spec=pltpu.PrefetchScalarGridSpec(num_...]
    gather x9 -> x0, local copies, waits for them, and re-layouts: 48.7 us -> none  [the longest x3 31.3 us: block_product(): chosen = select_blocks(lookup[columns], matches)]
    select_n x5 -> x0, other arithmetic: 31.7 us -> none  [the longest x3 31 us: select_blocks(): chosen = jnp.where(matched, picked[:, :, in_block], chosen)]
    concatenate x3 -> x1, other arithmetic: 30.1 us -> 0.01 us  [body(): jnp.concatenate([local_columns, remote_columns], axis=1).reshape(-1)]
    dot_general x3 -> x0, matrix products: 28.3 us -> none  [the longest x2 18.2 us: body(): jnp.einsum('rab,rnbc->rnac', inverse_diagonal, image, preferred_element_t...]
    all_to_all x4 -> x3, starting transfers between devices: 56.7 us -> 41 us  [exchange(): lax.all_to_all(outgoing, GY, split_axis=0, concat_axis=0, tiled=True)]
  transfers between devices with their start and end apart: 10 -> 10, of which waited for: 10 -> 10; matrix products, arithmetic and copies ran while one was open for 1% -> 0% of each run, Pallas kernels for 0% -> 0%
where the time goes in v1:
time: 530 us; the launch traced here: 529 us
  waiting for transfers between devices  332 us (63%)
  blocking collectives  67.2 us (13%)
  starting transfers between devices  56.5 us (11%)
  Pallas kernels  53.4 us (10%)
  local copies, waits for them, and re-layouts  12 us (2%)
  other arithmetic  7.24 us (1%)
    all_to_all x3, waiting for transfers between devices, exchange(): lax.all_to_all(outgoing, GY, split_axis=0, concat_axis=0, tiled=True)  298 us
    all_to_all x1, blocking collectives, body(): lax.all_to_all(chip, ('x', 'y'), split_axis=0, concat_axis=0, tiled=True)  67.2 us
    all_to_all x3, starting transfers between devices, exchange(): lax.all_to_all(outgoing, GY, split_axis=0, concat_axis=0, tiled=True)  41 us
    pallas_call x2, Pallas kernels, smooth(): pl.pallas_call(smooth_kernel, grid_spec=pltpu.PrefetchScalarGridSpec(num_...  30.4 us
    ppermute x6, waiting for transfers between devices, shifted(): lax.ppermute(value, axis, [(source, source + steps) for source in range(f...  26.4 us
    pallas_call x1, Pallas kernels, galerkin(): pl.pallas_call(final_kernel, grid_spec=pltpu.PrefetchScalarGridSpec(num_s...  17.1 us
    ppermute x6, starting transfers between devices, shifted(): lax.ppermute(value, axis, [(source, source + steps) for source in range(f...  15.5 us
    unnamed x44, local copies, waits for them, and re-layouts  11.6 us
  transfers between devices with their start and end apart: 10, of which 10 were waited for; matrix products, arithmetic and copies ran while one was open for 0% of the time, Pallas kernels for 0%

profile of v1, /device:TPU:0, one launch (start us, length us, event | category | flops | bytes accessed | tf_op | source)
XLA Modules:
  0.0 528.8 jit_solution(5169929088925006798)
XLA Ops:
  0.6 6.0 %pack_rows.1 = (bf16[32,2,256,256]{3,2,1,0:T(8,128)(2,1)}, bf16[1,2,256,256]{3,2,1,0:T(8,128)(2,1)}, bf16[1,2,256,256]{3,2,1,0:T(8,128)(2,1)}) custom-call(s32[32]{0:T(128)} %bitcast.4, s32[2]{0:T(128)} %bitcast.7, bf16[8,2,256,256]{3,2,1,0:T(8,128)(2,1)} %own_ref.1), custom_call_target="tpu_custom_call" | custom-call | tf_op jit(solution)/shard_map/pack_rows/pallas_call | solution.py:46
  6.6 0.0 copy-start.17
  6.6 0.0 copy-start.18
  6.6 0.0 copy-start.20
  6.6 0.0 copy-start.2
  6.7 0.0 copy-start.3
  6.7 0.0 copy-start.9
  6.7 0.0 copy-start.10
  6.7 7.8 %all-to-all-start = ((bf16[32,2,256,256]{3,2,1,0:T(8,128)(2,1)}), bf16[32,2,256,256]{3,2,1,0:T(8,128)(2,1)}, u32[]{:S(2)}, u32[]{:S(2)}) async-start(bf16[32,2,256,256]{3,2,1,0:T(8,128)(2,1)} %get-tuple-element.15), calls=%async_computation | async-start | bytes 16777216 | tf_op jit(solution)/shard_map/all_to_all | solution.py:240
  14.5 3.8 collective-permute-start
  18.4 1.3 collective-permute-start.1
  19.7 0.0 copy-done.17
  19.7 0.1 copy.15
  19.8 0.1 reshape.26.matches
  19.9 0.0 copy-done.18
  19.9 0.0 copy-done.20
  19.9 0.1 copy.14
  20.0 0.1 reshape.25.columns
  20.1 4.5 collective-permute-done.low_ref
  24.6 4.3 collective-permute-done.1.high_ref
  28.9 99.3 %all-to-all-done.r0.r1.r2.r3 = bf16[32,2,256,256]{3,2,1,0:T(8,128)(2,1)} async-done(((bf16[32,2,256,256]{3,2,1,0:T(8,128)(2,1)}), bf16[32,2,256,256]{3,2,1,0:T(8,128)(2,1)}, u32[]{:S(2)}, u32[]{:S(2)}) %all-to-all-start) | async-done | bytes 8388640 | tf_op jit(solution)/shard_map/all_to_all | solution.py:240
  128.2 0.0 copy-done.2
  128.2 0.0 copy-done.3
  128.2 0.0 copy-done.9
  128.2 0.0 copy-done.10
  128.2 0.0 copy-start
  128.2 2.8 copy-done
  131.0 14.8 %smooth_rows.2 = (bf16[8,2,256,256]{3,2,1,0:T(8,128)(2,1)S(1)}, bf16[32,2,256,256]{3,2,1,0:T(8,128)(2,1)}, bf16[1,2,256,256]{3,2,1,0:T(8,128)(2,1)S(1)}, bf16[1,2,256,256]{3,2,1,0:T(8,128)(2,1)S(1)}) custom-call(s32[48]{0:T(128)S(1)} %reshape.25.columns, s32[96]{0:T(128)S(1)} %reshape.26.matches, s32[32]{0:T(128)S(1)} %bitcast.5, s32[2]{0:T(128)S(1)} %bitcast.8, ...), custom_call_target="tpu_custom_call" | custom-call | tf_op jit(solution)/shard_map/smooth_rows/pallas_call | solution.py:175
  145.8 0.0 copy-start.4
  145.9 1.3 copy-done.4
  147.2 0.7 copy-done.15
  147.9 0.7 copy-done.16
  148.6 16.5 %all-to-all-start.1 = ((bf16[32,2,256,256]{3,2,1,0:T(8,128)(2,1)}), bf16[32,2,256,256]{3,2,1,0:T(8,128)(2,1)}, u32[]{:S(2)}, u32[]{:S(2)}) async-start(bf16[32,2,256,256]{3,2,1,0:T(8,128)(2,1)} %get-tuple-element.19), calls=%async_computation.1 | async-start | bytes 16777216 | tf_op jit(solution)/shard_map/all_to_all | solution.py:240
  165.1 3.8 collective-permute-start.2
  168.9 1.3 collective-permute-start.3
  170.2 4.9 collective-permute-done.2.low_ref
  175.1 4.2 collective-permute-done.3.high_ref
  179.3 0.7 copy-done.7
  180.0 98.8 %all-to-all-done.1.r0.r1.r2.r3 = bf16[32,2,256,256]{3,2,1,0:T(8,128)(2,1)} async-done(((bf16[32,2,256,256]{3,2,1,0:T(8,128)(2,1)}), bf16[32,2,256,256]{3,2,1,0:T(8,128)(2,1)}, u32[]{:S(2)}, u32[]{:S(2)}) %all-to-all-start.1) | async-done | bytes 8388640 | tf_op jit(solution)/shard_map/all_to_all | solution.py:240
  278.8 0.0 copy-done.5
  278.8 2.8 copy-done.1
  281.6 0.9 copy-done.8
  282.5 15.5 %smooth_rows.3 = (bf16[8,2,256,256]{3,2,1,0:T(8,128)(2,1)}, bf16[32,2,256,256]{3,2,1,0:T(8,128)(2,1)}, bf16[1,2,256,256]{3,2,1,0:T(8,128)(2,1)S(1)}, bf16[1,2,256,256]{3,2,1,0:T(8,128)(2,1)S(1)}) custom-call(s32[48]{0:T(128)S(1)} %reshape.25.columns, s32[96]{0:T(128)S(1)} %reshape.26.matches, s32[32]{0:T(128)S(1)} %bitcast.6, s32[2]{0:T(128)S(1)} %bitcast.9, ...), custom_call_target="tpu_custom_call" | custom-call | tf_op jit(solution)/shard_map/smooth_rows/pallas_call | solution.py:175
  298.1 0.0 copy-start.11
  298.1 0.7 copy-done.11
  298.8 0.7 copy-done.13
  299.5 16.7 %all-to-all-start.2 = ((bf16[32,2,256,256]{3,2,1,0:T(8,128)(2,1)}), bf16[32,2,256,256]{3,2,1,0:T(8,128)(2,1)}, u32[]{:S(2)}, u32[]{:S(2)}) async-start(bf16[32,2,256,256]{3,2,1,0:T(8,128)(2,1)} %get-tuple-element.23), calls=%async_computation.2 | async-start | bytes 16777216 | tf_op jit(solution)/shard_map/all_to_all | solution.py:240
  316.2 0.0 copy-done.14
  316.2 4.0 collective-permute-start.4
  320.2 0.0 copy-done.12
  320.2 1.3 collective-permute-start.5
  321.5 0.0 copy-done.19
  321.5 0.1 copy.16
  321.6 0.1 reshape.29.slots
  321.7 4.4 collective-permute-done.4.low_ref
  326.1 4.1 collective-permute-done.5.high_ref
  330.2 99.7 %all-to-all-done.2.r0.r1.r2.r3 = bf16[32,2,256,256]{3,2,1,0:T(8,128)(2,1)} async-done(((bf16[32,2,256,256]{3,2,1,0:T(8,128)(2,1)}), bf16[32,2,256,256]{3,2,1,0:T(8,128)(2,1)}, u32[]{:S(2)}, u32[]{:S(2)}) %all-to-all-start.2) | async-done | bytes 8388640 | tf_op jit(solution)/shard_map/all_to_all | solution.py:240
  429.9 0.0 copy-done.6
  429.9 17.1 %galerkin_rows.1 = (bf16[32,256,256]{2,1,0:T(8,128)(2,1)}, bf16[32,256,256]{2,1,0:T(8,128)(2,1)}) custom-call(s32[48]{0:T(128)S(1)} %reshape.25.columns, s32[96]{0:T(128)S(1)} %reshape.26.matches, s32[32]{0:T(128)S(1)} %reshape.29.slots, s32[1]{0:T(128)} %bitcast.2.core, bf16[8,6,256,256]{3,2,1,0:T(8,128)(2,1)} %a_ref.5, ...), custom_call_target="tpu_custom_call" | custom-call | tf_op jit(solution)/shard_map/galerkin_rows/pallas_call | solution.py:204
  446.9 0.0 collective-permute-start.6
  446.9 7.4 %collective-permute-done.6 = bf16[32,256,256]{2,1,0:T(8,128)(2,1)S(1)} collective-permute-done((bf16[32,256,256]{2,1,0:T(8,128)(2,1)}, bf16[32,256,256]{2,1,0:T(8,128)(2,1)S(1)}, u32[]{:S(2)}, u32[]{:S(2)}) %collective-permute-start.6) | collective-permute-done | bytes 4194336 | tf_op jit(solution)/shard_map/ppermute | solution.py:250
  454.3 3.7 add_convert_fusion
  458.0 67.2 %all_to_all.20 = bf16[32,256,256]{2,1,0:T(8,128)(2,1)} all-to-all(bf16[32,256,256]{2,1,0:T(8,128)(2,1)S(1)} %add_convert_fusion), channel_id=1, replica_groups=mesh['gx'=4,'x'=4,'y'=4,'c'=2] {'x','y'}, dimensions={0} | all-to-all | bytes 8388608 | tf_op jit(solution)/shard_map/all_to_all | solution.py:253
  525.2 3.6 reduce_sum.12
  (12 shorter events, 0.0 us)
Async XLA Ops:
  6.6 13.0 %copy-start.17 = (s32[8,6,2]{0,2,1:T(2,128)S(1)}, s32[8,6,2]{0,2,1:T(2,128)}, u32[]{:S(2)}) copy-start(s32[8,6,2]{0,2,1:T(2,128)} %param.12) | copy-start | bytes 1156
  6.6 13.3 %copy-start.18 = (s32[8,4]{0,1:T(4,128)S(1)}, s32[8,4]{0,1:T(4,128)}, u32[]{:S(2)}) copy-start(s32[8,4]{0,1:T(4,128)} %param.11) | copy-start | bytes 388
  6.6 13.3 %copy-start.20 = (s32[8,2]{0,1:T(2,128)S(1)}, s32[8,2]{0,1:T(2,128)}, u32[]{:S(2)}) copy-start(s32[8,2]{0,1:T(2,128)} %param.10) | copy-start | bytes 196
  6.6 121.6 %copy-start.2 = (bf16[8,2,256,256]{3,2,1,0:T(8,128)(2,1)S(1)}, bf16[8,2,256,256]{3,2,1,0:T(8,128)(2,1)}, u32[]{:S(2)}) copy-start(bf16[8,2,256,256]{3,2,1,0:T(8,128)(2,1)} %own_ref.1) | copy-start | bytes 6291460
  6.7 121.6 %copy-start.3 = (bf16[8,256,256]{2,1,0:T(8,128)(2,1)S(1)}, bf16[8,256,256]{2,1,0:T(8,128)(2,1)}, u32[]{:S(2)}) copy-start(bf16[8,256,256]{2,1,0:T(8,128)(2,1)} %d_ref.3) | copy-start | bytes 3145732
  6.7 121.5 %copy-start.9 = (s32[1,32]{1,0:T(1,128)S(1)}, s32[1,32]{1,0:T(1,128)}, u32[]{:S(2)}) copy-start(s32[1,32]{1,0:T(1,128)} %param.15) | copy-start | bytes 388
  6.7 121.5 %copy-start.10 = (s32[1,2]{1,0:T(1,128)S(1)}, s32[1,2]{1,0:T(1,128)}, u32[]{:S(2)}) copy-start(s32[1,2]{1,0:T(1,128)} %param.16) | copy-start | bytes 28
  6.7 121.5 %all-to-all-start = ((bf16[32,2,256,256]{3,2,1,0:T(8,128)(2,1)}), bf16[32,2,256,256]{3,2,1,0:T(8,128)(2,1)}, u32[]{:S(2)}, u32[]{:S(2)}) async-start(bf16[32,2,256,256]{3,2,1,0:T(8,128)(2,1)} %get-tuple-element.15), calls=%async_computation | async-start | bytes 16777216 | tf_op jit(solution)/shard_map/all_to_all | solution.py:240
  14.5 10.1 %collective-permute-start = (bf16[1,2,256,256]{3,2,1,0:T(8,128)(2,1)}, bf16[1,2,256,256]{3,2,1,0:T(8,128)(2,1)S(1)}, u32[]{:S(2)}, u32[]{:S(2)}) collective-permute-start(bf16[1,2,256,256]{3,2,1,0:T(8,128)(2,1)} %get-tuple-element.16), channel_id=1, source_target_pairs={{0,32},{32,64},{64,96},{1,33},{33,65},{65,97},{2,34},{34,66},{66,9... | collective-permute-start | bytes 786440 | tf_op jit(solution)/shard_map/ppermute | solution.py:18
  18.4 10.5 %collective-permute-start.1 = (bf16[1,2,256,256]{3,2,1,0:T(8,128)(2,1)}, bf16[1,2,256,256]{3,2,1,0:T(8,128)(2,1)}, u32[]{:S(2)}, u32[]{:S(2)}) collective-permute-start(bf16[1,2,256,256]{3,2,1,0:T(8,128)(2,1)} %get-tuple-element.17), channel_id=1, source_target_pairs={{32,0},{64,32},{96,64},{33,1},{65,33},{97,65},{34,2},{66,34},{98,6... | collective-permute-start | bytes 786440 | tf_op jit(solution)/shard_map/ppermute | solution.py:18
  128.2 2.8 copy-start
  145.8 1.3 copy-start.4
  147.2 0.7 copy-start.15
  147.9 0.7 copy-start.16
  148.6 130.2 %copy-start.5 = (bf16[8,2,256,256]{3,2,1,0:T(8,128)(2,1)S(1)}, bf16[8,2,256,256]{3,2,1,0:T(8,128)(2,1)}, u32[]{:S(2)}) copy-start(bf16[8,2,256,256]{3,2,1,0:T(8,128)(2,1)} %copy-done.4) | copy-start | bytes 6291460
  148.6 130.2 %all-to-all-start.1 = ((bf16[32,2,256,256]{3,2,1,0:T(8,128)(2,1)}), bf16[32,2,256,256]{3,2,1,0:T(8,128)(2,1)}, u32[]{:S(2)}, u32[]{:S(2)}) async-start(bf16[32,2,256,256]{3,2,1,0:T(8,128)(2,1)} %get-tuple-element.19), calls=%async_computation.1 | async-start | bytes 16777216 | tf_op jit(solution)/shard_map/all_to_all | solution.py:240
  165.1 10.0 %collective-permute-start.2 = (bf16[1,2,256,256]{3,2,1,0:T(8,128)(2,1)}, bf16[1,2,256,256]{3,2,1,0:T(8,128)(2,1)S(1)}, u32[]{:S(2)}, u32[]{:S(2)}) collective-permute-start(bf16[1,2,256,256]{3,2,1,0:T(8,128)(2,1)} %copy-done.16), channel_id=1, source_target_pairs={{0,32},{32,64},{64,96},{1,33},{33,65},{65,97},{2,34},{34,66},{66,9... | collective-permute-start | bytes 786440 | tf_op jit(solution)/shard_map/ppermute | solution.py:18
  168.9 10.4 %collective-permute-start.3 = (bf16[1,2,256,256]{3,2,1,0:T(8,128)(2,1)}, bf16[1,2,256,256]{3,2,1,0:T(8,128)(2,1)S(1)}, u32[]{:S(2)}, u32[]{:S(2)}) collective-permute-start(bf16[1,2,256,256]{3,2,1,0:T(8,128)(2,1)} %copy-done.15), channel_id=1, source_target_pairs={{32,0},{64,32},{96,64},{33,1},{65,33},{97,65},{34,2},{66,34},{98,6... | collective-permute-start | bytes 786440 | tf_op jit(solution)/shard_map/ppermute | solution.py:18
  179.3 0.7 copy-start.7
  278.8 2.8 copy-start.1
  281.6 0.9 copy-start.8
  298.1 0.7 copy-start.11
  298.8 0.7 copy-start.13
  299.5 16.7 %copy-start.14 = (bf16[1,2,256,256]{3,2,1,0:T(8,128)(2,1)S(1)}, bf16[1,2,256,256]{3,2,1,0:T(8,128)(2,1)}, u32[]{:S(2)}) copy-start(bf16[1,2,256,256]{3,2,1,0:T(8,128)(2,1)} %copy-done.13) | copy-start | bytes 786436
  299.5 20.7 %copy-start.12 = (bf16[1,2,256,256]{3,2,1,0:T(8,128)(2,1)S(1)}, bf16[1,2,256,256]{3,2,1,0:T(8,128)(2,1)}, u32[]{:S(2)}) copy-start(bf16[1,2,256,256]{3,2,1,0:T(8,128)(2,1)} %copy-done.11) | copy-start | bytes 786436
  299.5 22.0 %copy-start.19 = (s32[8,2,2]{0,2,1:T(2,128)S(1)}, s32[8,2,2]{0,2,1:T(2,128)}, u32[]{:S(2)}) copy-start(s32[8,2,2]{0,2,1:T(2,128)} %param.17) | copy-start | bytes 388
  299.5 130.4 %copy-start.6 = (bf16[8,2,256,256]{3,2,1,0:T(8,128)(2,1)S(1)}, bf16[8,2,256,256]{3,2,1,0:T(8,128)(2,1)}, u32[]{:S(2)}) copy-start(bf16[8,2,256,256]{3,2,1,0:T(8,128)(2,1)} %get-tuple-element.13.own_ref) | copy-start | bytes 6291460
  299.5 130.4 %all-to-all-start.2 = ((bf16[32,2,256,256]{3,2,1,0:T(8,128)(2,1)}), bf16[32,2,256,256]{3,2,1,0:T(8,128)(2,1)}, u32[]{:S(2)}, u32[]{:S(2)}) async-start(bf16[32,2,256,256]{3,2,1,0:T(8,128)(2,1)} %get-tuple-element.23), calls=%async_computation.2 | async-start | bytes 16777216 | tf_op jit(solution)/shard_map/all_to_all | solution.py:240
  316.2 9.9 %collective-permute-start.4 = (bf16[1,2,256,256]{3,2,1,0:T(8,128)(2,1)S(1)}, bf16[1,2,256,256]{3,2,1,0:T(8,128)(2,1)S(1)}, u32[]{:S(2)}, u32[]{:S(2)}) collective-permute-start(bf16[1,2,256,256]{3,2,1,0:T(8,128)(2,1)S(1)} %copy-done.14), channel_id=1, source_target_pairs={{0,32},{32,64},{64,96},{1,33},{33,65},{65,97},{2,34},{34,66},{66,9... | collective-permute-start | bytes 786440 | tf_op jit(solution)/shard_map/ppermute | solution.py:18
  320.2 10.0 %collective-permute-start.5 = (bf16[1,2,256,256]{3,2,1,0:T(8,128)(2,1)S(1)}, bf16[1,2,256,256]{3,2,1,0:T(8,128)(2,1)S(1)}, u32[]{:S(2)}, u32[]{:S(2)}) collective-permute-start(bf16[1,2,256,256]{3,2,1,0:T(8,128)(2,1)S(1)} %copy-done.12), channel_id=1, source_target_pairs={{32,0},{64,32},{96,64},{33,1},{65,33},{97,65},{34,2},{66,34},{98,6... | collective-permute-start | bytes 786440 | tf_op jit(solution)/shard_map/ppermute | solution.py:18
  446.9 7.4 %collective-permute-start.6 = (bf16[32,256,256]{2,1,0:T(8,128)(2,1)}, bf16[32,256,256]{2,1,0:T(8,128)(2,1)S(1)}, u32[]{:S(2)}, u32[]{:S(2)}) collective-permute-start(bf16[32,256,256]{2,1,0:T(8,128)(2,1)} %get-tuple-element.27), channel_id=1, source_target_pairs={{0,1},{1,0},{2,3},{3,2},{4,5},{5,4},{6,7},{7,6},{8,9},{9,8},{10,11... | collective-permute-start | bytes 12582920 | tf_op jit(solution)/shard_map/ppermute | solution.py:250

commit v2 on v1

v2 whole, which is shorter than its diff:
```python
import jax
import jax.numpy as jnp
from jax import lax
from jax.experimental import pallas as pl
from jax.experimental.pallas import tpu as pltpu
from jax.sharding import Mesh
from jax.sharding import PartitionSpec as P

AXES = ("gx", "x", "y", "c")
GY = ("x", "y", "c")
LINKS = 6
LOCAL = 2


def shifted(value, axis, steps):
    count = lax.axis_size(axis)
    first, last = (max(0, -steps), min(count, count - steps))
    return lax.ppermute(value, axis, [(source, source + steps) for source in range(first, last)])


def pack_kernel(peer_ref, rows_ref, out_ref, sems):
    copies = []
    for q in range(out_ref.shape[0]):
        copies.append(pltpu.make_async_copy(rows_ref.at[peer_ref[q]], out_ref.at[q], sems.at[q]))
    for copy in copies:
        copy.start()
    for copy in copies:
        copy.wait()


def pack(peer_list, rows):
    count, blocks, width, _ = rows.shape
    peers = peer_list.shape[0]
    size = 2 * blocks * width * width
    return pl.pallas_call(
        pack_kernel,
        grid_spec=pltpu.PrefetchScalarGridSpec(
            num_scalar_prefetch=1,
            grid=(1,),
            in_specs=[pl.BlockSpec(rows.shape, lambda i, *refs: (0, 0, 0, 0))],
            out_specs=pl.BlockSpec(memory_space=pl.ANY),
            scratch_shapes=[pltpu.SemaphoreType.DMA((peers,))],
        ),
        out_shape=jax.ShapeDtypeStruct((peers, blocks, width, width), jnp.bfloat16),
        cost_estimate=pl.CostEstimate(flops=0, transcendentals=0, bytes_accessed=(count + 2 * peers) * size),
        compiler_params=pltpu.CompilerParams(vmem_limit_bytes=56 << 20),
        name="pack_rows",
    )(peer_list, rows)


def fetch_rows(columns, i, slot, peers_ref, low_ref, high_ref, far, sems, first, count):
    for k in range(far.shape[1]):
        column = columns[i * LINKS + LOCAL + k]
        place = (far.at[slot, k], sems.at[slot, k])

        @pl.when(column < first + count)
        def _():
            pltpu.make_async_copy(peers_ref.at[jnp.maximum(column - first, 0)], *place).start()

        @pl.when(column == first + count)
        def _():
            pltpu.make_async_copy(low_ref.at[0], *place).start()

        @pl.when(column > first + count)
        def _():
            pltpu.make_async_copy(high_ref.at[0], *place).start()


def row_image(columns, matches, a_ref, own_ref, peers_ref, low_ref, high_ref, rhs, lhs, far, sems):
    i = pl.program_id(0)
    slot = lax.rem(i, 2)
    width = own_ref.shape[-1]
    arrays = (peers_ref, low_ref, high_ref, far, sems, own_ref.shape[0], peers_ref.shape[0])

    @pl.when(i == 0)
    def _():
        fetch_rows(columns, i, slot, *arrays)

    @pl.when(i + 1 < pl.num_programs(0))
    def _():
        fetch_rows(columns, i + 1, 1 - slot, *arrays)

    for k in range(far.shape[1]):
        pltpu.make_async_copy(peers_ref.at[0], far.at[slot, k], sems.at[slot, k]).wait()
    for k in range(LINKS):
        lhs[:, k * width : (k + 1) * width] = a_ref[0, k]
        for n in range(2):
            match = matches[(i * LINKS + k) * 2 + n]
            there = jnp.minimum(match, 1)
            if k < LOCAL:
                block = own_ref[columns[i * LINKS + k], there]
            else:
                block = far[slot, k - LOCAL, there]
            block = jnp.where(match < 2, block, jnp.zeros_like(block))
            rhs[k * width : (k + 1) * width, n * width : (n + 1) * width] = block
    return jnp.dot(lhs[...], rhs[...], preferred_element_type=jnp.float32).astype(jnp.bfloat16)


def smooth_kernel(
    columns, matches, slab_list,
    a_ref, d_ref, own_ref, peers_ref, low_ref, high_ref,
    rows_out, up_ref, down_ref,
    rhs, lhs, far, kept, sems, out_sems,
):
    i = pl.program_id(0)
    width = own_ref.shape[-1]
    image = row_image(columns, matches, a_ref, own_ref, peers_ref, low_ref, high_ref, rhs, lhs, far, sems)
    update = jnp.dot(d_ref[0], image, preferred_element_type=jnp.float32)
    for n in range(2):
        new = own_ref[i, n].astype(jnp.float32) - update[:, n * width : (n + 1) * width]
        new = new.astype(jnp.bfloat16)
        rows_out[0, n] = new
        kept[i, n] = new

    @pl.when(i == pl.num_programs(0) - 1)
    def _():
        up = pltpu.make_async_copy(kept.at[slab_list[0]], up_ref.at[0], out_sems.at[0])
        down = pltpu.make_async_copy(kept.at[slab_list[1]], down_ref.at[0], out_sems.at[1])
        up.start()
        down.start()
        up.wait()
        down.wait()


def final_kernel(
    columns, matches, slots, core,
    a_ref, own_ref, peers_ref, low_ref, high_ref,
    keep_ref, swap_ref,
    rhs, lhs, far, sems,
):
    i = pl.program_id(0)
    width = own_ref.shape[-1]

    @pl.when(i == 0)
    def _():
        keep_ref[...] = jnp.zeros_like(keep_ref)
        swap_ref[...] = jnp.zeros_like(swap_ref)

    image = row_image(columns, matches, a_ref, own_ref, peers_ref, low_ref, high_ref, rhs, lhs, far, sems)
    mine = jnp.concatenate([own_ref[i, n] for n in range(2)], axis=1)
    partial = lax.dot_general(mine, image, (((0,), (0,)), ((), ())), preferred_element_type=jnp.float32)
    partial = partial.astype(jnp.bfloat16)
    for n1 in range(2):
        for n2 in range(2):
            slot = slots[(i * 2 + n1) * 2 + n2]
            owner = slot // 2
            place = (owner // 2) * 2 + slot % 2
            block = partial[n1 * width : (n1 + 1) * width, n2 * width : (n2 + 1) * width]

            @pl.when(owner % 2 == core[0])
            def _():
                keep_ref[place] = block

            @pl.when(owner % 2 != core[0])
            def _():
                swap_ref[place] = block


def gather_scratch(blocks, width):
    return [
        pltpu.VMEM((LINKS * width, blocks * width), jnp.bfloat16),
        pltpu.VMEM((width, LINKS * width), jnp.bfloat16),
        pltpu.VMEM((2, LINKS - LOCAL, blocks, width, width), jnp.bfloat16),
    ]


def smooth(tables, slab_list, operator, inverse, rows, received, low, high):
    count, inner, width, _ = operator.shape
    blocks = rows.shape[1]
    anywhere = pl.BlockSpec(memory_space=pl.ANY)
    one = jax.ShapeDtypeStruct((1, blocks, width, width), jnp.bfloat16)
    return pl.pallas_call(
        smooth_kernel,
        grid_spec=pltpu.PrefetchScalarGridSpec(
            num_scalar_prefetch=3,
            grid=(count,),
            in_specs=[
                pl.BlockSpec((1, inner, width, width), lambda i, *refs: (i, 0, 0, 0)),
                pl.BlockSpec((1, width, width), lambda i, *refs: (i, 0, 0)),
                pl.BlockSpec(rows.shape, lambda i, *refs: (0, 0, 0, 0)),
                anywhere,
                anywhere,
                anywhere,
            ],
            out_specs=[pl.BlockSpec((1, blocks, width, width), lambda i, *refs: (i, 0, 0, 0)), anywhere, anywhere],
            scratch_shapes=[
                *gather_scratch(blocks, width),
                pltpu.VMEM((count, blocks, width, width), jnp.bfloat16),
                pltpu.SemaphoreType.DMA((2, LINKS - LOCAL)),
                pltpu.SemaphoreType.DMA((2,)),
            ],
        ),
        out_shape=(jax.ShapeDtypeStruct(rows.shape, jnp.bfloat16), one, one),
        compiler_params=pltpu.CompilerParams(vmem_limit_bytes=56 << 20),
        name="smooth_rows",
    )(*tables, slab_list, operator, inverse, rows, received, low, high)


def galerkin(tables, slots, core, operator, rows, received, low, high):
    count, inner, width, _ = operator.shape
    blocks = rows.shape[1]
    peers = received.shape[0]
    anywhere = pl.BlockSpec(memory_space=pl.ANY)
    half = jax.ShapeDtypeStruct((peers, width, width), jnp.bfloat16)
    half_spec = pl.BlockSpec((peers, width, width), lambda i, *refs: (0, 0, 0))
    return pl.pallas_call(
        final_kernel,
        grid_spec=pltpu.PrefetchScalarGridSpec(
            num_scalar_prefetch=4,
            grid=(count,),
            in_specs=[
                pl.BlockSpec((1, inner, width, width), lambda i, *refs: (i, 0, 0, 0)),
                pl.BlockSpec(rows.shape, lambda i, *refs: (0, 0, 0, 0)),
                anywhere,
                anywhere,
                anywhere,
            ],
            out_specs=[half_spec, half_spec],
            scratch_shapes=[*gather_scratch(blocks, width), pltpu.SemaphoreType.DMA((2, LINKS - LOCAL))],
        ),
        out_shape=(half, half),
        compiler_params=pltpu.CompilerParams(vmem_limit_bytes=56 << 20),
        name="galerkin_rows",
    )(*tables, slots, core, operator, rows, received, low, high)


def body(
    operator_blocks,
    local_columns,
    remote_columns,
    match_slots,
    tentative,
    inverse_diagonal,
    peer_sends,
    slab_sends,
    coarse_slots,
):
    peer_list = peer_sends.reshape(-1)
    slab_list = slab_sends.reshape(-1)
    columns = jnp.concatenate([local_columns, remote_columns], axis=1).reshape(-1)
    tables = (columns, match_slots.reshape(-1))
    core = lax.axis_index("c").reshape(1).astype(jnp.int32)

    slots = coarse_slots.reshape(-1)

    def exchange(rows, up, down):
        low, high = shifted(up, "gx", 1), shifted(down, "gx", -1)
        outgoing = pack(peer_list, rows)
        outgoing, low, high, *now = lax.optimization_barrier((outgoing, low, high, *tables, slab_list, slots, core, rows))
        received = lax.all_to_all(outgoing, GY, split_axis=0, concat_axis=0, tiled=True)
        return now, received, low, high

    up, down = tentative[slab_list[:1]], tentative[slab_list[1:]]
    rows = tentative
    for smooth_pass in range(2):
        (*tables, slab_list, slots, core, rows), *arrived = exchange(rows, up, down)
        rows, up, down = smooth(tables, slab_list, operator_blocks, inverse_diagonal, rows, *arrived)
    (*tables, slab_list, slots, core, rows), *arrived = exchange(rows, up, down)
    keep, swap = galerkin(tables, slots, core, operator_blocks, rows, *arrived)
    other = lax.ppermute(swap, "c", [(0, 1), (1, 0)])
    chip = (keep.astype(jnp.float32) + other.astype(jnp.float32)).astype(jnp.bfloat16)
    width = chip.shape[-1]
    received = lax.all_to_all(chip, ("x", "y"), split_axis=0, concat_axis=0, tiled=True)
    coarse = jnp.sum(received.reshape(-1, 2, width, width), axis=0, dtype=jnp.float32)
    return (rows, coarse.astype(jnp.bfloat16))


def solution(mesh):
    fine = Mesh(mesh.devices.reshape(4, 4, 4, 2), AXES)
    placed = tuple(P(AXES, *[None] * extra) for extra in (3, 1, 1, 2, 3, 2, 1, 1, 2))
    return jax.shard_map(
        body,
        mesh=fine,
        in_specs=placed,
        out_specs=(P(AXES, None, None, None), P(AXES, None, None)),
        check_vma=False,
    )
```

time: 530 us -> 472 us (0.89)
  waiting for transfers between devices: 332 us -> 13.8 us
  blocking collectives: 67.2 us -> 359 us
  starting transfers between devices: 56.5 us -> 16.4 us
  Pallas kernels: 53.4 us -> 63.2 us
  local copies, waits for them, and re-layouts: 12 us -> 5.89 us
    all_to_all x0 -> x3, blocking collectives: none -> 304 us  [exchange(): lax.all_to_all(outgoing, GY, split_axis=0, concat_axis=0, tiled=True)]
    all_to_all x3 -> x0, waiting for transfers between devices: 298 us -> none  [exchange(): lax.all_to_all(outgoing, GY, split_axis=0, concat_axis=0, tiled=True)]
    all_to_all x3 -> x0, starting transfers between devices: 41 us -> none  [exchange(): lax.all_to_all(outgoing, GY, split_axis=0, concat_axis=0, tiled=True)]
    ppermute x6, waiting for transfers between devices: 26.4 us -> 6.75 us  [shifted(): lax.ppermute(value, axis, [(source, source + steps) for source in range(f...]
    all_to_all x1, blocking collectives: 67.2 us -> 55 us  [body(): lax.all_to_all(chip, ('x', 'y'), split_axis=0, concat_axis=0, tiled=True)]
    pallas_call x1 -> x3, Pallas kernels: 5.98 us -> 17.3 us  [pack(): pl.pallas_call(pack_kernel, grid_spec=pltpu.PrefetchScalarGridSpec(num_sc...]
    unnamed x44 -> x14, local copies, waits for them, and re-layouts: 11.6 us -> 1.6 us
  transfers between devices with their start and end apart: 10 -> 7, of which waited for: 10 -> 3; matrix products, arithmetic and copies ran while one was open for 0% -> 1% of each run, Pallas kernels for 0% -> 4%
where the time goes in v2:
time: 472 us; the launch traced here: 471 us
  blocking collectives  359 us (76%)
  Pallas kernels  63.2 us (13%)
  starting transfers between devices  16.4 us (3%)
  waiting for transfers between devices  13.8 us (3%)
  other arithmetic  7.9 us (2%)
  local copies, waits for them, and re-layouts  5.89 us (1%)
    all_to_all x3, blocking collectives, exchange(): lax.all_to_all(outgoing, GY, split_axis=0, concat_axis=0, tiled=True)  304 us
    all_to_all x1, blocking collectives, body(): lax.all_to_all(chip, ('x', 'y'), split_axis=0, concat_axis=0, tiled=True)  55 us
    pallas_call x2, Pallas kernels, smooth(): pl.pallas_call(smooth_kernel, grid_spec=pltpu.PrefetchScalarGridSpec(num_...  28.8 us
    pallas_call x3, Pallas kernels, pack(): pl.pallas_call(pack_kernel, grid_spec=pltpu.PrefetchScalarGridSpec(num_sc...  17.3 us
    pallas_call x1, Pallas kernels, galerkin(): pl.pallas_call(final_kernel, grid_spec=pltpu.PrefetchScalarGridSpec(num_s...  17.1 us
    ppermute x6, starting transfers between devices, shifted(): lax.ppermute(value, axis, [(source, source + steps) for source in range(f...  16 us
  transfers between devices with their start and end apart: 7, of which 3 were waited for; matrix products, arithmetic and copies ran while one was open for 1% of the time, Pallas kernels for 4%

profile of v2, /device:TPU:0, one launch (start us, length us, event | category | flops | bytes accessed | tf_op | source)
XLA Modules:
  0.0 470.5 jit_solution(1059873598744114890)
XLA Ops:
  0.6 1.3 fusion
  5.8 1.1 constant_dynamic-slice_fusion
  6.9 1.3 collective-permute-start.1
  8.2 4.6 collective-permute-start
  12.8 0.7 pad_add_fusion
  13.5 0.1 copy.14
  13.6 0.6 reshape.28.columns
  14.2 0.8 copy.16
  14.9 0.6 reshape.31.slots
  15.5 0.8 copy.15
  16.3 0.6 reshape.29.matches
  17.0 5.8 %pack_rows.3 = bf16[32,2,256,256]{3,2,1,0:T(8,128)(2,1)} custom-call(s32[32]{0:T(128)} %bitcast.11, bf16[8,2,256,256]{3,2,1,0:T(8,128)(2,1)} %own_ref), custom_call_target="tpu_custom_call" | custom-call | bytes 18874368 | tf_op jit(solution)/shard_map/pack_rows/pallas_call | solution.py:35
  22.7 0.0 collective-permute-done.1.high_ref
  22.7 0.0 copy-start
  22.8 0.0 collective-permute-done.low_ref
  22.8 0.0 copy-start.1
  22.8 103.0 %all_to_all.20.peers_ref = bf16[32,2,256,256]{3,2,1,0:T(8,128)(2,1)} all-to-all(bf16[32,2,256,256]{3,2,1,0:T(8,128)(2,1)} %pack_rows.3), channel_id=1, replica_groups=mesh['gx'=4,'x'=4,'y'=4,'c'=2] {'x','y','c'}, dimensions={0} | all-to-all | bytes 16777216 | tf_op jit(solution)/shard_map/all_to_all | solution.py:250
  125.8 0.0 copy-done
  125.8 0.0 copy-done.1
  125.8 14.4 %smooth_rows.2 = (bf16[8,2,256,256]{3,2,1,0:T(8,128)(2,1)}, bf16[1,2,256,256]{3,2,1,0:T(8,128)(2,1)}, bf16[1,2,256,256]{3,2,1,0:T(8,128)(2,1)}) custom-call(s32[48]{0:T(128)} %reshape.28.columns, s32[96]{0:T(128)} %reshape.29.matches, s32[2]{0:T(128)} %bitcast.9, bf16[8,6,256,256]{3,2,1,0:T(8,128)(2,1)} %a_ref.5, bf16[8,256,256]{2,1,0:T(8,128)(2,1)} %d_ref.3, ...), custom_call_target="tpu_custom_call" | custom-call | tf_op jit(solution)/shard_map/smooth_rows/pallas_call | solution.py:172
  140.1 3.8 collective-permute-start.2
  144.0 1.3 collective-permute-start.3
  145.3 5.8 %pack_rows.4 = bf16[32,2,256,256]{3,2,1,0:T(8,128)(2,1)} custom-call(s32[32]{0:T(128)} %bitcast.12, bf16[8,2,256,256]{3,2,1,0:T(8,128)(2,1)} %get-tuple-element.51.rows_ref.own_ref), custom_call_target="tpu_custom_call" | custom-call | bytes 18874368 | tf_op jit(solution)/shard_map/pack_rows/pallas_call | solution.py:35
  151.1 0.0 collective-permute-done.2.low_ref
  151.1 0.0 copy-start.3
  151.1 3.5 collective-permute-done.3.high_ref
  154.6 0.0 copy-start.5
  154.6 100.4 %all_to_all.21.peers_ref = bf16[32,2,256,256]{3,2,1,0:T(8,128)(2,1)} all-to-all(bf16[32,2,256,256]{3,2,1,0:T(8,128)(2,1)} %pack_rows.4), channel_id=1, replica_groups=mesh['gx'=4,'x'=4,'y'=4,'c'=2] {'x','y','c'}, dimensions={0} | all-to-all | bytes 16777216 | tf_op jit(solution)/shard_map/all_to_all | solution.py:250
  254.9 0.0 copy-done.3
  254.9 0.0 copy-done.5
  255.0 14.4 %smooth_rows.3 = (bf16[8,2,256,256]{3,2,1,0:T(8,128)(2,1)}, bf16[1,2,256,256]{3,2,1,0:T(8,128)(2,1)}, bf16[1,2,256,256]{3,2,1,0:T(8,128)(2,1)}) custom-call(s32[48]{0:T(128)} %reshape.28.columns, s32[96]{0:T(128)} %reshape.29.matches, s32[2]{0:T(128)} %bitcast.10, bf16[8,6,256,256]{3,2,1,0:T(8,128)(2,1)} %a_ref.5, bf16[8,256,256]{2,1,0:T(8,128)(2,1)} %d_ref.3, ...), custom_call_target="tpu_custom_call" | custom-call | tf_op jit(solution)/shard_map/smooth_rows/pallas_call | solution.py:172
  269.3 3.7 collective-permute-start.4
  273.0 1.3 collective-permute-start.5
  274.3 5.8 %pack_rows.5 = bf16[32,2,256,256]{3,2,1,0:T(8,128)(2,1)} custom-call(s32[32]{0:T(128)} %bitcast.13, bf16[8,2,256,256]{3,2,1,0:T(8,128)(2,1)} %get-tuple-element.34.rows_ref.own_ref), custom_call_target="tpu_custom_call" | custom-call | bytes 18874368 | tf_op jit(solution)/shard_map/pack_rows/pallas_call | solution.py:35
  280.1 0.0 collective-permute-done.4.low_ref
  280.1 0.0 copy-start.2
  280.1 3.3 collective-permute-done.5.high_ref
  283.4 0.0 copy-start.4
  283.4 100.4 %all_to_all.22.peers_ref = bf16[32,2,256,256]{3,2,1,0:T(8,128)(2,1)} all-to-all(bf16[32,2,256,256]{3,2,1,0:T(8,128)(2,1)} %pack_rows.5), channel_id=1, replica_groups=mesh['gx'=4,'x'=4,'y'=4,'c'=2] {'x','y','c'}, dimensions={0} | all-to-all | bytes 16777216 | tf_op jit(solution)/shard_map/all_to_all | solution.py:250
  383.8 0.0 copy-done.2
  383.8 0.0 copy-done.4
  383.8 17.1 %galerkin_rows.1 = (bf16[32,256,256]{2,1,0:T(8,128)(2,1)}, bf16[32,256,256]{2,1,0:T(8,128)(2,1)}) custom-call(s32[48]{0:T(128)} %reshape.28.columns, s32[96]{0:T(128)} %reshape.29.matches, s32[32]{0:T(128)} %reshape.31.slots, s32[1]{0:T(128)} %bitcast.6.core, bf16[8,6,256,256]{3,2,1,0:T(8,128)(2,1)} %a_ref.5, ...), custom_call_target="tpu_custom_call" | custom-call | tf_op jit(solution)/shard_map/galerkin_rows/pallas_call | solution.py:206
  400.9 0.4 collective-permute-start.6
  401.3 7.0 %collective-permute-done.6 = bf16[32,256,256]{2,1,0:T(8,128)(2,1)S(1)} collective-permute-done((bf16[32,256,256]{2,1,0:T(8,128)(2,1)}, bf16[32,256,256]{2,1,0:T(8,128)(2,1)S(1)}, u32[]{:S(2)}, u32[]{:S(2)}) %collective-permute-start.6) | collective-permute-done | bytes 4194336 | tf_op jit(solution)/shard_map/ppermute | solution.py:260
  408.3 3.6 add_convert_fusion
  412.0 55.0 %all_to_all.23 = bf16[32,256,256]{2,1,0:T(8,128)(2,1)} all-to-all(bf16[32,256,256]{2,1,0:T(8,128)(2,1)S(1)} %add_convert_fusion), channel_id=1, replica_groups=mesh['gx'=4,'x'=4,'y'=4,'c'=2] {'x','y'}, dimensions={0} | all-to-all | bytes 8388608 | tf_op jit(solution)/shard_map/all_to_all | solution.py:263
  467.0 3.6 reduce_sum.12
Async XLA Ops:
  6.9 15.8 %collective-permute-start.1 = (bf16[1,2,256,256]{3,2,1,0:T(8,128)(2,1)S(1)}, bf16[1,2,256,256]{3,2,1,0:T(8,128)(2,1)S(1)}, u32[]{:S(2)}, u32[]{:S(2)}) collective-permute-start(bf16[1,2,256,256]{3,2,1,0:T(8,128)(2,1)S(1)} %get-tuple-element.92), channel_id=1, source_target_pairs={{32,0},{64,32},{96,64},{33,1},{65,33},{97,65},{34,2},{66,34},{98,6... | collective-permute-start | bytes 786440 | tf_op jit(solution)/shard_map/ppermute | solution.py:18
  8.2 14.6 %collective-permute-start = (bf16[1,2,256,256]{3,2,1,0:T(8,128)(2,1)S(1)}, bf16[1,2,256,256]{3,2,1,0:T(8,128)(2,1)S(1)}, u32[]{:S(2)}, u32[]{:S(2)}) collective-permute-start(bf16[1,2,256,256]{3,2,1,0:T(8,128)(2,1)S(1)} %get-tuple-element.93), channel_id=1, source_target_pairs={{0,32},{32,64},{64,96},{1,33},{33,65},{65,97},{2,34},{34,66},{66,9... | collective-permute-start | bytes 786440 | tf_op jit(solution)/shard_map/ppermute | solution.py:18
  22.7 103.0 %copy-start = (bf16[1,2,256,256]{3,2,1,0:T(8,128)(2,1)}, bf16[1,2,256,256]{3,2,1,0:T(8,128)(2,1)S(1)}, u32[]{:S(2)}) copy-start(bf16[1,2,256,256]{3,2,1,0:T(8,128)(2,1)S(1)} %collective-permute-done.1.high_ref) | copy-start | bytes 786436
  22.8 103.0 %copy-start.1 = (bf16[1,2,256,256]{3,2,1,0:T(8,128)(2,1)}, bf16[1,2,256,256]{3,2,1,0:T(8,128)(2,1)S(1)}, u32[]{:S(2)}) copy-start(bf16[1,2,256,256]{3,2,1,0:T(8,128)(2,1)S(1)} %collective-permute-done.low_ref) | copy-start | bytes 786436
  140.1 10.9 %collective-permute-start.2 = (bf16[1,2,256,256]{3,2,1,0:T(8,128)(2,1)}, bf16[1,2,256,256]{3,2,1,0:T(8,128)(2,1)S(1)}, u32[]{:S(2)}, u32[]{:S(2)}) collective-permute-start(bf16[1,2,256,256]{3,2,1,0:T(8,128)(2,1)} %get-tuple-element.44), channel_id=1, source_target_pairs={{0,32},{32,64},{64,96},{1,33},{33,65},{65,97},{2,34},{34,66},{66,9... | collective-permute-start | bytes 786440 | tf_op jit(solution)/shard_map/ppermute | solution.py:18
  144.0 10.6 %collective-permute-start.3 = (bf16[1,2,256,256]{3,2,1,0:T(8,128)(2,1)}, bf16[1,2,256,256]{3,2,1,0:T(8,128)(2,1)S(1)}, u32[]{:S(2)}, u32[]{:S(2)}) collective-permute-start(bf16[1,2,256,256]{3,2,1,0:T(8,128)(2,1)} %get-tuple-element.45), channel_id=1, source_target_pairs={{32,0},{64,32},{96,64},{33,1},{65,33},{97,65},{34,2},{66,34},{98,6... | collective-permute-start | bytes 786440 | tf_op jit(solution)/shard_map/ppermute | solution.py:18
  151.1 103.9 %copy-start.3 = (bf16[1,2,256,256]{3,2,1,0:T(8,128)(2,1)}, bf16[1,2,256,256]{3,2,1,0:T(8,128)(2,1)S(1)}, u32[]{:S(2)}) copy-start(bf16[1,2,256,256]{3,2,1,0:T(8,128)(2,1)S(1)} %collective-permute-done.2.low_ref) | copy-start | bytes 786436
  154.6 100.4 %copy-start.5 = (bf16[1,2,256,256]{3,2,1,0:T(8,128)(2,1)}, bf16[1,2,256,256]{3,2,1,0:T(8,128)(2,1)S(1)}, u32[]{:S(2)}) copy-start(bf16[1,2,256,256]{3,2,1,0:T(8,128)(2,1)S(1)} %collective-permute-done.3.high_ref) | copy-start | bytes 786436
  269.3 10.8 %collective-permute-start.4 = (bf16[1,2,256,256]{3,2,1,0:T(8,128)(2,1)}, bf16[1,2,256,256]{3,2,1,0:T(8,128)(2,1)S(1)}, u32[]{:S(2)}, u32[]{:S(2)}) collective-permute-start(bf16[1,2,256,256]{3,2,1,0:T(8,128)(2,1)} %get-tuple-element.56), channel_id=1, source_target_pairs={{0,32},{32,64},{64,96},{1,33},{33,65},{65,97},{2,34},{34,66},{66,9... | collective-permute-start | bytes 786440 | tf_op jit(solution)/shard_map/ppermute | solution.py:18
  273.0 10.4 %collective-permute-start.5 = (bf16[1,2,256,256]{3,2,1,0:T(8,128)(2,1)}, bf16[1,2,256,256]{3,2,1,0:T(8,128)(2,1)S(1)}, u32[]{:S(2)}, u32[]{:S(2)}) collective-permute-start(bf16[1,2,256,256]{3,2,1,0:T(8,128)(2,1)} %get-tuple-element.57), channel_id=1, source_target_pairs={{32,0},{64,32},{96,64},{33,1},{65,33},{97,65},{34,2},{66,34},{98,6... | collective-permute-start | bytes 786440 | tf_op jit(solution)/shard_map/ppermute | solution.py:18
  280.1 103.7 %copy-start.2 = (bf16[1,2,256,256]{3,2,1,0:T(8,128)(2,1)}, bf16[1,2,256,256]{3,2,1,0:T(8,128)(2,1)S(1)}, u32[]{:S(2)}) copy-start(bf16[1,2,256,256]{3,2,1,0:T(8,128)(2,1)S(1)} %collective-permute-done.4.low_ref) | copy-start | bytes 786436
  283.4 100.4 %copy-start.4 = (bf16[1,2,256,256]{3,2,1,0:T(8,128)(2,1)}, bf16[1,2,256,256]{3,2,1,0:T(8,128)(2,1)S(1)}, u32[]{:S(2)}) copy-start(bf16[1,2,256,256]{3,2,1,0:T(8,128)(2,1)S(1)} %collective-permute-done.5.high_ref) | copy-start | bytes 786436
  400.9 7.4 %collective-permute-start.6 = (bf16[32,256,256]{2,1,0:T(8,128)(2,1)}, bf16[32,256,256]{2,1,0:T(8,128)(2,1)S(1)}, u32[]{:S(2)}, u32[]{:S(2)}) collective-permute-start(bf16[32,256,256]{2,1,0:T(8,128)(2,1)} %get-tuple-element.69), channel_id=1, source_target_pairs={{0,1},{1,0},{2,3},{3,2},{4,5},{5,4},{6,7},{7,6},{8,9},{9,8},{10,11... | collective-permute-start | bytes 12582920 | tf_op jit(solution)/shard_map/ppermute | solution.py:260

commit v3 on v0

v3 whole, which is shorter than its diff:
```python
import jax
import jax.numpy as jnp
from jax import lax
from jax.experimental import pallas as pl
from jax.experimental.pallas import tpu as pltpu
from jax.sharding import Mesh
from jax.sharding import PartitionSpec as P

AXES = ("gx", "x", "y", "c")
GY = ("x", "y", "c")
LINKS = 6
LOCAL = 2
BLOCKS = 2
RING = 4
ANY = pl.BlockSpec(memory_space=pl.ANY)
SMEM = pl.BlockSpec(memory_space=pltpu.SMEM)
PARAMS = pltpu.CompilerParams(vmem_limit_bytes=56 << 20)


def shifted(value, axis, steps):
    count = lax.axis_size(axis)
    first, last = (max(0, -steps), min(count, count - steps))
    return lax.ppermute(value, axis, [(source, source + steps) for source in range(first, last)])


def around(value, axis, steps):
    count = lax.axis_size(axis)
    return lax.ppermute(value, axis, [(source, (source + steps) % count) for source in range(count)])


def shape(*sizes):
    return jax.ShapeDtypeStruct(sizes, jnp.bfloat16)


def pick_kernel(slab, rows_ref, up_ref, down_ref, held, sems):
    arrivals = [pltpu.make_async_copy(rows_ref.at[slab[0, j]], held.at[j], sems.at[j]) for j in range(2)]
    copies = [pltpu.make_async_copy(held.at[j], out.at[0], sems.at[2 + j]) for j, out in enumerate((up_ref, down_ref))]
    for copy in arrivals:
        copy.start()
    for arrival, copy in zip(arrivals, copies):
        arrival.wait()
        copy.start()
    for copy in copies:
        copy.wait()


def pick(slab, rows):
    one = shape(1, *rows.shape[1:])
    return pl.pallas_call(
        pick_kernel,
        in_specs=[SMEM, ANY],
        out_specs=[ANY, ANY],
        out_shape=(one, one),
        scratch_shapes=[pltpu.VMEM((2, *rows.shape[1:]), jnp.bfloat16), pltpu.SemaphoreType.DMA((4,))],
        compiler_params=PARAMS,
        name="pick_rows",
    )(slab, rows)


def pack_kernel(peer, rows_ref, out_ref, own, in_sems, sems):
    arrivals = [pltpu.make_async_copy(rows_ref.at[j], own.at[j], in_sems.at[j]) for j in range(own.shape[0])]
    for copy in arrivals:
        copy.start()
    for copy in arrivals:
        copy.wait()
    copies = [pltpu.make_async_copy(own.at[peer[0, q]], out_ref.at[q], sems.at[q]) for q in range(out_ref.shape[0])]
    for copy in copies:
        copy.start()
    for copy in copies:
        copy.wait()


def pack(peer, rows):
    peers = peer.shape[1]
    return pl.pallas_call(
        pack_kernel,
        in_specs=[SMEM, ANY],
        out_specs=ANY,
        out_shape=shape(peers, *rows.shape[1:]),
        scratch_shapes=[
            pltpu.VMEM(rows.shape, jnp.bfloat16),
            pltpu.SemaphoreType.DMA((rows.shape[0],)),
            pltpu.SemaphoreType.DMA((peers,)),
        ],
        cost_estimate=pl.CostEstimate(flops=0, transcendentals=0, bytes_accessed=10 << 20),
        compiler_params=PARAMS,
        name="pack_rows",
    )(peer, rows)


def start_row(remote, i, a_hbm, peers_hbm, low_hbm, high_hbm, a_buf, far, sems, first, count):
    pltpu.make_async_copy(a_hbm.at[i], a_buf.at[i], sems.at[i, 0]).start()
    for k in range(LINKS - LOCAL):
        column = remote[k, i]
        place = (far.at[i, k], sems.at[i, 1 + k])

        @pl.when(column < first + count)
        def _():
            pltpu.make_async_copy(peers_hbm.at[jnp.maximum(column - first, 0)], *place).start()

        @pl.when(column == first + count)
        def _():
            pltpu.make_async_copy(low_hbm.at[0], *place).start()

        @pl.when(column > first + count)
        def _():
            pltpu.make_async_copy(high_hbm.at[0], *place).start()


def wait_row(i, a_hbm, peers_hbm, a_buf, far, sems):
    pltpu.make_async_copy(a_hbm.at[i], a_buf.at[i], sems.at[i, 0]).wait()
    for k in range(LINKS - LOCAL):
        pltpu.make_async_copy(peers_hbm.at[0], far.at[i, k], sems.at[i, 1 + k]).wait()


def row_image(local, match, i, a_buf, own, far, rhs):
    width = own.shape[-1]
    for k in range(LINKS):
        for n in range(BLOCKS):
            wanted = match[k, n, i]
            there = jnp.minimum(wanted, BLOCKS - 1)
            if k < LOCAL:
                block = own[local[k, i], there]
            else:
                block = far[i, k - LOCAL, there]
            block = jnp.where(wanted < BLOCKS, block, jnp.zeros_like(block))
            rhs[k * width : (k + 1) * width, n * width : (n + 1) * width] = block
    lhs = jnp.concatenate([a_buf[i, k] for k in range(LINKS)], axis=1)
    return jnp.dot(lhs, rhs[...], preferred_element_type=jnp.float32).astype(jnp.bfloat16)


def smooth_kernel(
    local, remote, match, peer, slab,
    a_hbm, d_hbm, own_hbm, peers_hbm, low_hbm, high_hbm,
    rows_hbm, out_hbm, up_hbm, down_hbm,
    a_buf, d_buf, own, far, new, rhs,
    sems, own_sems, d_sem, rows_sem, out_sem, slab_sems,
):
    count, width = own.shape[0], own.shape[-1]
    peers = out_hbm.shape[0]
    arrays = (a_hbm, peers_hbm, low_hbm, high_hbm, a_buf, far, sems, count, peers)
    own_copy = pltpu.make_async_copy(own_hbm, own, own_sems.at[0])
    d_copy = pltpu.make_async_copy(d_hbm, d_buf, d_sem.at[0])
    own_copy.start()
    start_row(remote, 0, *arrays)
    d_copy.start()

    @pl.loop(1, count)
    def _(i):
        start_row(remote, i, *arrays)

    own_copy.wait()

    @pl.loop(0, count)
    def _(i):
        wait_row(i, a_hbm, peers_hbm, a_buf, far, sems)
        image = row_image(local, match, i, a_buf, own, far, rhs)

        @pl.when(i == 0)
        def _():
            d_copy.wait()

        update = jnp.dot(d_buf[i], image, preferred_element_type=jnp.float32)
        for n in range(BLOCKS):
            value = own[i, n].astype(jnp.float32) - update[:, n * width : (n + 1) * width]
            new[i, n] = value.astype(jnp.bfloat16)
        pltpu.make_async_copy(new.at[i], rows_hbm.at[i], rows_sem.at[0]).start()
        for q in range(peers):

            @pl.when(peer[0, q] == i)
            def _():
                pltpu.make_async_copy(new.at[i], out_hbm.at[q], out_sem.at[0]).start()

    up = pltpu.make_async_copy(new.at[slab[0, 0]], up_hbm.at[0], slab_sems.at[0])
    down = pltpu.make_async_copy(new.at[slab[0, 1]], down_hbm.at[0], slab_sems.at[1])
    up.start()
    down.start()
    pltpu.make_async_copy(rows_hbm, rows_hbm, rows_sem.at[0]).wait()
    pltpu.make_async_copy(out_hbm, out_hbm, out_sem.at[0]).wait()
    up.wait()
    down.wait()


def row_scratch(count, width):
    return [
        pltpu.VMEM((count, LINKS, width, width), jnp.bfloat16),
        pltpu.VMEM((count, BLOCKS, width, width), jnp.bfloat16),
        pltpu.VMEM((count, LINKS - LOCAL, BLOCKS, width, width), jnp.bfloat16),
        pltpu.VMEM((LINKS * width, BLOCKS * width), jnp.bfloat16),
        pltpu.SemaphoreType.DMA((count, 1 + LINKS - LOCAL)),
        pltpu.SemaphoreType.DMA((1,)),
    ]


def smooth(tables, peer, slab, operator, inverse, rows, received, low, high):
    count, _, width, _ = operator.shape
    one = shape(1, *rows.shape[1:])
    a_buf, own, far, rhs, sems, single = row_scratch(count, width)
    return pl.pallas_call(
        smooth_kernel,
        in_specs=[SMEM] * 5 + [ANY] * 6,
        out_specs=[ANY] * 4,
        out_shape=(shape(*rows.shape), shape(*received.shape), one, one),
        scratch_shapes=[
            a_buf, pltpu.VMEM(inverse.shape, jnp.bfloat16), own, far, own, rhs,
            sems, single, single, single, single, pltpu.SemaphoreType.DMA((2,)),
        ],
        compiler_params=PARAMS,
        name="smooth_rows",
    )(*tables, peer, slab, operator, inverse, rows, received, low, high)


def galerkin_kernel(
    local, remote, match, slots, here,
    a_hbm, own_hbm, peers_hbm, low_hbm, high_hbm,
    keep_hbm, swap_hbm,
    a_buf, own, far, rhs, result, zero, named,
    sems, own_sems, keep_sem, swap_sem,
):
    count, width = own.shape[0], own.shape[-1]
    peers = peers_hbm.shape[0]
    half = keep_hbm.shape[0]
    arrays = (a_hbm, peers_hbm, low_hbm, high_hbm, a_buf, far, sems, count, peers)
    own_copy = pltpu.make_async_copy(own_hbm, own, own_sems.at[0])
    own_copy.start()

    @pl.loop(0, count)
    def _(i):
        start_row(remote, i, *arrays)

    zero[...] = jnp.zeros_like(zero)

    def send(block, slot):
        owner = slot // 2
        chip = owner // 2
        dx = (chip // RING - here[0] + RING) % RING
        dy = (chip % RING - here[1] + RING) % RING
        second = slot % 2
        place = jnp.where(second == 0, dx * RING + dy, RING * RING + dy * RING + dx)

        @pl.when(owner % 2 == here[2])
        def _():
            pltpu.make_async_copy(block, keep_hbm.at[place], keep_sem.at[0]).start()

        @pl.when(owner % 2 != here[2])
        def _():
            pltpu.make_async_copy(block, swap_hbm.at[place], swap_sem.at[0]).start()

    @pl.loop(0, 2 * half)
    def _(slot):
        named[slot] = 0

    @pl.loop(0, count)
    def _(i):
        for n1 in range(BLOCKS):
            for n2 in range(BLOCKS):
                named[slots[n1, n2, i]] = 1

    @pl.loop(0, 2 * half)
    def _(slot):
        @pl.when(named[slot] == 0)
        def _():
            send(zero, slot)

    own_copy.wait()

    @pl.loop(0, count)
    def _(i):
        wait_row(i, a_hbm, peers_hbm, a_buf, far, sems)
        image = row_image(local, match, i, a_buf, own, far, rhs)
        mine = jnp.concatenate([own[i, n] for n in range(BLOCKS)], axis=1)
        partial = lax.dot_general(mine, image, (((0,), (0,)), ((), ())), preferred_element_type=jnp.float32)
        for n1 in range(BLOCKS):
            for n2 in range(BLOCKS):
                block = partial[n1 * width : (n1 + 1) * width, n2 * width : (n2 + 1) * width]
                result[i, n1 * BLOCKS + n2] = block.astype(jnp.bfloat16)
                send(result.at[i, n1 * BLOCKS + n2], slots[n1, n2, i])

    pltpu.make_async_copy(keep_hbm, keep_hbm, keep_sem.at[0]).wait()
    pltpu.make_async_copy(swap_hbm, swap_hbm, swap_sem.at[0]).wait()


def galerkin(tables, slots, here, operator, rows, received, low, high):
    count, _, width, _ = operator.shape
    half = RING * RING * BLOCKS
    a_buf, own, far, rhs, sems, single = row_scratch(count, width)
    return pl.pallas_call(
        galerkin_kernel,
        in_specs=[SMEM] * 5 + [ANY] * 5,
        out_specs=[ANY] * 2,
        out_shape=(shape(half, width, width), shape(half, width, width)),
        scratch_shapes=[
            a_buf, own, far, rhs,
            pltpu.VMEM((count, BLOCKS * BLOCKS, width, width), jnp.bfloat16),
            pltpu.VMEM((width, width), jnp.bfloat16),
            pltpu.SMEM((2 * half,), jnp.int32),
            sems, single, single, single,
        ],
        compiler_params=PARAMS,
        name="galerkin_rows",
    )(*tables, slots, here, operator, rows, received, low, high)


def add(terms):
    total = terms[0].astype(jnp.float32)
    for term in terms[1:]:
        total = total + term.astype(jnp.float32)
    return total.astype(jnp.bfloat16)


def body(
    operator_blocks,
    local_columns,
    remote_columns,
    match_slots,
    tentative,
    inverse_diagonal,
    peer,
    slab,
    coarse_slots,
):
    tables = (local_columns.T, remote_columns.T, match_slots.transpose(1, 2, 0))
    slots = coarse_slots.transpose(1, 2, 0)
    here = jnp.stack([lax.axis_index("x"), lax.axis_index("y"), lax.axis_index("c")]).astype(jnp.int32)
    rows = tentative
    up, down = pick(slab, rows)
    low, high = shifted(up, "gx", 1), shifted(down, "gx", -1)
    outgoing = pack(peer, rows)
    outgoing, low, high, here = lax.optimization_barrier((outgoing, low, high, here))
    received = lax.all_to_all(outgoing, GY, split_axis=0, concat_axis=0, tiled=True)
    for smooth_pass in range(2):
        rows, outgoing, up, down = smooth(tables, peer, slab, operator_blocks, inverse_diagonal, rows, received, low, high)
        low, high = shifted(up, "gx", 1), shifted(down, "gx", -1)
        outgoing, low, high = lax.optimization_barrier((outgoing, low, high))
        received = lax.all_to_all(outgoing, GY, split_axis=0, concat_axis=0, tiled=True)
    keep, swap = galerkin(tables, slots, here, operator_blocks, rows, received, low, high)
    other = lax.ppermute(swap, "c", [(0, 1), (1, 0)])
    parts = [add((keep[RING * j : RING * j + RING], other[RING * j : RING * j + RING])) for j in range(2 * RING)]
    for axes in (("x", "y"), ("y", "x")):
        sums = []
        for axis, group in zip(axes, (parts[: len(parts) // 2], parts[len(parts) // 2 :])):
            terms = [group[0], *[around(group[s], axis, s) for s in range(1, RING)]]
            sums.append([add([term[j : j + 1] for term in terms]) for j in range(terms[0].shape[0])])
        parts = sums[0] + sums[1]
    return (rows, jnp.concatenate(parts, axis=0))


def solution(mesh):
    fine = Mesh(mesh.devices.reshape(4, 4, 4, 2), AXES)
    placed = tuple(P(AXES, *[None] * extra) for extra in (3, 1, 1, 2, 3, 2, 1, 1, 2))
    return jax.shard_map(
        body,
        mesh=fine,
        in_specs=placed,
        out_specs=(P(AXES, None, None, None), P(AXES, None, None)),
        check_vma=False,
    )
```

time: 719 us -> 451 us (0.63); the launches traced: 706 us -> 449 us
  waiting for transfers between devices: 429 us -> 47.4 us
  blocking collectives: 0 us -> 304 us
  local copies, waits for them, and re-layouts: 105 us -> 0.02 us
  other arithmetic: 67.4 us -> 4.91 us
  Pallas kernels: 0 us -> 48.9 us
  starting transfers between devices: 72 us -> 43.5 us
  matrix products: 28.3 us -> 0 us
    all_to_all x4 -> x0, waiting for transfers between devices: 405 us -> none  [the longest x3 293 us: fetch_remote(): lax.all_to_all(outgoing, 'gy', split_axis=0, concat_axis=0, tiled=True)]
    all_to_all x0 -> x3, blocking collectives: none -> 304 us  [body(): lax.all_to_all(outgoing, GY, split_axis=0, concat_axis=0, tiled=True)]
    all_to_all x4 -> x0, starting transfers between devices: 56.7 us -> none  [the longest x3 40.4 us: fetch_remote(): lax.all_to_all(outgoing, 'gy', split_axis=0, concat_axis=0, tiled=True)]
    pallas_call x0 -> x5, Pallas kernels: none -> 48.9 us  [the longest x2 26.9 us: smooth(): pl.pallas_call(smooth_kernel, in_specs=[SMEM] * 5 + [ANY] * 6, out_specs=...]
    gather x9 -> x0, local copies, waits for them, and re-layouts: 48.7 us -> none  [the longest x3 31.3 us: block_product(): chosen = select_blocks(lookup[columns], matches)]
    select_n x5 -> x0, other arithmetic: 31.7 us -> none  [the longest x3 31 us: select_blocks(): chosen = jnp.where(matched, picked[:, :, in_block], chosen)]
    concatenate x3 -> x1, other arithmetic: 30.1 us -> 0.73 us  [body(): return (rows, jnp.concatenate(parts, axis=0))]
    dot_general x3 -> x0, matrix products: 28.3 us -> none  [the longest x2 18.2 us: body(): jnp.einsum('rab,rnbc->rnac', inverse_diagonal, image, preferred_element_t...]
  transfers between devices with their start and end apart: 10 -> 19, of which waited for: 10 -> 11; matrix products, arithmetic and copies ran while one was open for 1% -> 0% of each run, Pallas kernels for 0% -> 1%
where the time goes in v3:
time: 451 us; the launch traced here: 449 us
  blocking collectives  304 us (67%)
  Pallas kernels  48.9 us (11%)
  waiting for transfers between devices  47.4 us (11%)
  starting transfers between devices  43.5 us (10%)
  other arithmetic  4.91 us (1%)
    all_to_all x3, blocking collectives, body(): lax.all_to_all(outgoing, GY, split_axis=0, concat_axis=0, tiled=True)  304 us
    ppermute x12, starting transfers between devices, around(): lax.ppermute(value, axis, [(source, (source + steps) % count) for source...  28 us
    pallas_call x2, Pallas kernels, smooth(): pl.pallas_call(smooth_kernel, in_specs=[SMEM] * 5 + [ANY] * 6, out_specs=...  26.9 us
    ppermute x6, waiting for transfers between devices, shifted(): lax.ppermute(value, axis, [(source, source + steps) for source in range(f...  20.7 us
    ppermute x12, waiting for transfers between devices, around(): lax.ppermute(value, axis, [(source, (source + steps) % count) for source...  19.7 us
    ppermute x6, starting transfers between devices, shifted(): lax.ppermute(value, axis, [(source, source + steps) for source in range(f...  15 us
    pallas_call x1, Pallas kernels, galerkin(): pl.pallas_call(galerkin_kernel, in_specs=[SMEM] * 5 + [ANY] * 5, out_spec...  13.7 us
  transfers between devices with their start and end apart: 19, of which 11 were waited for; matrix products, arithmetic and copies ran while one was open for 0% of the time, Pallas kernels for 1%

profile of v3, /device:TPU:0, one launch (start us, length us, event | category | flops | bytes accessed | tf_op | source)
XLA Modules:
  0.0 449.2 jit_solution(3367553509998134368)
XLA Ops:
  0.6 2.4 pick_rows.1
  3.1 4.0 collective-permute-start
  7.1 1.3 collective-permute-start.1
  8.4 5.8 %pack_rows.1 = bf16[32,2,256,256]{3,2,1,0:T(8,128)(2,1)} custom-call(s32[1,32]{1,0:T(1,128)} %peer.5, bf16[8,2,256,256]{3,2,1,0:T(8,128)(2,1)} %own_hbm.1), custom_call_target="tpu_custom_call" | custom-call | bytes 10485760 | tf_op jit(solution)/shard_map/pack_rows/pallas_call | solution.py:75
  14.2 0.7 pad_add_fusion.here
  14.9 0.0 collective-permute-done.low_hbm
  14.9 0.0 copy-start
  14.9 2.1 collective-permute-done.1.high_hbm
  17.0 0.0 copy-start.1
  17.0 102.9 %all_to_all.15.peers_hbm = bf16[32,2,256,256]{3,2,1,0:T(8,128)(2,1)} all-to-all(bf16[32,2,256,256]{3,2,1,0:T(8,128)(2,1)} %pack_rows.1), channel_id=1, replica_groups=mesh['gx'=4,'x'=4,'y'=4,'c'=2] {'x','y','c'}, dimensions={0} | all-to-all | bytes 16777216 | tf_op jit(solution)/shard_map/all_to_all | solution.py:330
  119.9 0.0 copy-done
  119.9 0.0 copy-done.1
  119.9 13.6 %smooth_rows.2 = (bf16[8,2,256,256]{3,2,1,0:T(8,128)(2,1)}, bf16[32,2,256,256]{3,2,1,0:T(8,128)(2,1)}, bf16[1,2,256,256]{3,2,1,0:T(8,128)(2,1)}, bf16[1,2,256,256]{3,2,1,0:T(8,128)(2,1)}) custom-call(s32[2,8]{1,0:T(2,128)} %bitcast.13, s32[4,8]{1,0:T(4,128)} %bitcast.10, s32[6,2,8]{2,1,0:T(2,128)} %bitcast.7, s32[1,32]{1,0:T(1,128)} %peer.5, s32[1,2]{1,0:T(1,128)} %slab.5, ...), custom_call_target="tpu_custom_call" | custom-call | tf_op jit(solution)/shard_map/smooth_rows/pallas_call | solution.py:199
  133.5 3.7 collective-permute-start.2
  137.2 1.3 collective-permute-start.3
  138.5 5.2 %collective-permute-done.2.low_hbm = bf16[1,2,256,256]{3,2,1,0:T(8,128)(2,1)S(1)} collective-permute-done((bf16[1,2,256,256]{3,2,1,0:T(8,128)(2,1)}, bf16[1,2,256,256]{3,2,1,0:T(8,128)(2,1)S(1)}, u32[]{:S(2)}, u32[]{:S(2)}) %collective-permute-start.2) | collective-permute-done | bytes 262176 | tf_op jit(solution)/shard_map/ppermute | solution.py:23
  143.7 0.0 copy-start.2
  143.7 4.0 collective-permute-done.3.high_hbm
  147.7 0.0 copy-start.4
  147.7 100.4 %all_to_all.16.peers_hbm = bf16[32,2,256,256]{3,2,1,0:T(8,128)(2,1)} all-to-all(bf16[32,2,256,256]{3,2,1,0:T(8,128)(2,1)} %get-tuple-element.33), channel_id=1, replica_groups=mesh['gx'=4,'x'=4,'y'=4,'c'=2] {'x','y','c'}, dimensions={0} | all-to-all | bytes 16777216 | tf_op jit(solution)/shard_map/all_to_all | solution.py:335
  248.1 0.0 copy-done.2
  248.1 0.0 copy-done.4
  248.1 13.3 %smooth_rows.3 = (bf16[8,2,256,256]{3,2,1,0:T(8,128)(2,1)}, bf16[32,2,256,256]{3,2,1,0:T(8,128)(2,1)}, bf16[1,2,256,256]{3,2,1,0:T(8,128)(2,1)}, bf16[1,2,256,256]{3,2,1,0:T(8,128)(2,1)}) custom-call(s32[2,8]{1,0:T(2,128)} %bitcast.14, s32[4,8]{1,0:T(4,128)} %bitcast.11, s32[6,2,8]{2,1,0:T(2,128)} %bitcast.8, s32[1,32]{1,0:T(1,128)} %peer.5, s32[1,2]{1,0:T(1,128)} %slab.5, ...), custom_call_target="tpu_custom_call" | custom-call | tf_op jit(solution)/shard_map/smooth_rows/pallas_call | solution.py:199
  261.4 3.4 collective-permute-start.4
  264.9 1.3 collective-permute-start.5
  266.2 5.4 %collective-permute-done.4.low_hbm = bf16[1,2,256,256]{3,2,1,0:T(8,128)(2,1)S(1)} collective-permute-done((bf16[1,2,256,256]{3,2,1,0:T(8,128)(2,1)}, bf16[1,2,256,256]{3,2,1,0:T(8,128)(2,1)S(1)}, u32[]{:S(2)}, u32[]{:S(2)}) %collective-permute-start.4) | collective-permute-done | bytes 262176 | tf_op jit(solution)/shard_map/ppermute | solution.py:23
  271.5 0.0 copy-start.3
  271.5 4.0 collective-permute-done.5.high_hbm
  275.6 100.4 %all_to_all.17.peers_hbm = bf16[32,2,256,256]{3,2,1,0:T(8,128)(2,1)} all-to-all(bf16[32,2,256,256]{3,2,1,0:T(8,128)(2,1)} %get-tuple-element.41), channel_id=1, replica_groups=mesh['gx'=4,'x'=4,'y'=4,'c'=2] {'x','y','c'}, dimensions={0} | all-to-all | bytes 16777216 | tf_op jit(solution)/shard_map/all_to_all | solution.py:335
  376.0 0.0 copy-done.3
  376.0 0.0 copy-done.5
  376.0 13.7 %galerkin_rows.1 = (bf16[32,256,256]{2,1,0:T(8,128)(2,1)}, bf16[32,256,256]{2,1,0:T(8,128)(2,1)}) custom-call(s32[2,8]{1,0:T(2,128)} %bitcast.15, s32[4,8]{1,0:T(4,128)} %bitcast.12, s32[6,2,8]{2,1,0:T(2,128)} %bitcast.9, s32[2,2,8]{2,1,0:T(2,128)} %bitcast.16, s32[3]{0:T(128)} %pad_add_fusion.here, bf16[8,6,256,256]{3,2,1,0:T(8,128)(2,1)} %a_hbm.5, ...), custom_call_target="tpu_custom_call" | custom-call | tf_op jit(solution)/shard_map/galerkin_rows/pallas_call | solution.py:287
  389.7 0.5 collective-permute-start.6
  390.2 7.0 %collective-permute-done.6 = bf16[32,256,256]{2,1,0:T(8,128)(2,1)S(1)} collective-permute-done((bf16[32,256,256]{2,1,0:T(8,128)(2,1)}, bf16[32,256,256]{2,1,0:T(8,128)(2,1)S(1)}, u32[]{:S(2)}, u32[]{:S(2)}) %collective-permute-start.6) | collective-permute-done | bytes 4194336 | tf_op jit(solution)/shard_map/ppermute | solution.py:337
  397.2 2.8 add_convert_fusion.7
  400.0 1.6 collective-permute-start.15
  401.6 1.4 collective-permute-start.14
  403.1 0.2 collective-permute-start.13
  403.2 1.3 collective-permute-start.9
  404.5 1.3 collective-permute-start.8
  405.8 9.0 %collective-permute-done.15 = bf16[4,256,256]{2,1,0:T(8,128)(2,1)S(1)} collective-permute-done((bf16[4,256,256]{2,1,0:T(8,128)(2,1)S(1)}, bf16[4,256,256]{2,1,0:T(8,128)(2,1)S(1)}, u32[]{:S(2)}, u32[]{:S(2)}) %collective-permute-start.15) | collective-permute-done | bytes 524320 | tf_op jit(solution)/shard_map/ppermute | solution.py:28
  414.8 10.6 %collective-permute-start.7 = (bf16[4,256,256]{2,1,0:T(8,128)(2,1)S(1)}, bf16[4,256,256]{2,1,0:T(8,128)(2,1)S(1)}, u32[]{:S(2)}, u32[]{:S(2)}) collective-permute-start(bf16[4,256,256]{2,1,0:T(8,128)(2,1)S(1)} %get-tuple-element.53), channel_id=1, source_target_pairs={{0,8},{8,16},{16,24},{24,0},{1,9},{9,17},{17,25},{25,1},{2,10},{10... | collective-permute-start | bytes 1572872 | tf_op jit(solution)/shard_map/ppermute | solution.py:28
  425.5 0.0 collective-permute-done.14
  425.5 2.8 collective-permute-done.13
  428.3 0.2 add_convert_fusion.11
  428.5 1.0 collective-permute-start.16
  429.4 2.3 collective-permute-start.18
  431.8 0.0 collective-permute-done.9
  431.8 0.0 collective-permute-start.17
  431.8 0.0 collective-permute-done.8
  431.8 3.0 collective-permute-done.7
  434.7 0.2 add_convert_fusion.16
  434.9 0.1 collective-permute-start.10
  435.0 6.8 %collective-permute-start.12 = (bf16[1,256,256]{2,1,0:T(8,128)(2,1)S(1)}, bf16[1,256,256]{2,1,0:T(8,128)(2,1)S(1)}, u32[]{:S(2)}, u32[]{:S(2)}) collective-permute-start(bf16[1,256,256]{2,1,0:T(8,128)(2,1)S(1)} %get-tuple-element.55), channel_id=1, source_target_pairs={{0,6},{2,0},{4,2},{6,4},{1,7},{3,1},{5,3},{7,5},{8,14},{10,8},{12,... | collective-permute-start | bytes 393224 | tf_op jit(solution)/shard_map/ppermute | solution.py:28
  441.9 0.0 collective-permute-done.16
  441.9 1.4 collective-permute-start.11
  443.2 0.0 collective-permute-done.18
  443.3 0.0 collective-permute-done.17
  443.3 0.1 add_convert_fusion.8
  443.4 2.3 collective-permute-done.10
  445.7 0.0 collective-permute-done.12
  445.7 2.7 collective-permute-done.11
  448.3 0.1 add_convert_fusion.13
  448.5 0.7 pad_maximum_fusion
  (1 shorter events, 0.0 us)
Async XLA Ops:
  3.1 11.8 %collective-permute-start = (bf16[1,2,256,256]{3,2,1,0:T(8,128)(2,1)}, bf16[1,2,256,256]{3,2,1,0:T(8,128)(2,1)S(1)}, u32[]{:S(2)}, u32[]{:S(2)}) collective-permute-start(bf16[1,2,256,256]{3,2,1,0:T(8,128)(2,1)} %get-tuple-element.24), channel_id=1, source_target_pairs={{0,32},{32,64},{64,96},{1,33},{33,65},{65,97},{2,34},{34,66},{66,9... | collective-permute-start | bytes 786440 | tf_op jit(solution)/shard_map/ppermute | solution.py:23
  7.1 9.9 %collective-permute-start.1 = (bf16[1,2,256,256]{3,2,1,0:T(8,128)(2,1)}, bf16[1,2,256,256]{3,2,1,0:T(8,128)(2,1)S(1)}, u32[]{:S(2)}, u32[]{:S(2)}) collective-permute-start(bf16[1,2,256,256]{3,2,1,0:T(8,128)(2,1)} %get-tuple-element.25), channel_id=1, source_target_pairs={{32,0},{64,32},{96,64},{33,1},{65,33},{97,65},{34,2},{66,34},{98,6... | collective-permute-start | bytes 786440 | tf_op jit(solution)/shard_map/ppermute | solution.py:23
  14.9 105.0 %copy-start = (bf16[1,2,256,256]{3,2,1,0:T(8,128)(2,1)}, bf16[1,2,256,256]{3,2,1,0:T(8,128)(2,1)S(1)}, u32[]{:S(2)}) copy-start(bf16[1,2,256,256]{3,2,1,0:T(8,128)(2,1)S(1)} %collective-permute-done.low_hbm) | copy-start | bytes 786436
  17.0 102.9 %copy-start.1 = (bf16[1,2,256,256]{3,2,1,0:T(8,128)(2,1)}, bf16[1,2,256,256]{3,2,1,0:T(8,128)(2,1)S(1)}, u32[]{:S(2)}) copy-start(bf16[1,2,256,256]{3,2,1,0:T(8,128)(2,1)S(1)} %collective-permute-done.1.high_hbm) | copy-start | bytes 786436
  133.5 10.2 %collective-permute-start.2 = (bf16[1,2,256,256]{3,2,1,0:T(8,128)(2,1)}, bf16[1,2,256,256]{3,2,1,0:T(8,128)(2,1)S(1)}, u32[]{:S(2)}, u32[]{:S(2)}) collective-permute-start(bf16[1,2,256,256]{3,2,1,0:T(8,128)(2,1)} %get-tuple-element.31), channel_id=1, source_target_pairs={{0,32},{32,64},{64,96},{1,33},{33,65},{65,97},{2,34},{34,66},{66,9... | collective-permute-start | bytes 786440 | tf_op jit(solution)/shard_map/ppermute | solution.py:23
  137.2 10.5 %collective-permute-start.3 = (bf16[1,2,256,256]{3,2,1,0:T(8,128)(2,1)}, bf16[1,2,256,256]{3,2,1,0:T(8,128)(2,1)S(1)}, u32[]{:S(2)}, u32[]{:S(2)}) collective-permute-start(bf16[1,2,256,256]{3,2,1,0:T(8,128)(2,1)} %get-tuple-element.32), channel_id=1, source_target_pairs={{32,0},{64,32},{96,64},{33,1},{65,33},{97,65},{34,2},{66,34},{98,6... | collective-permute-start | bytes 786440 | tf_op jit(solution)/shard_map/ppermute | solution.py:23
  143.7 104.4 %copy-start.2 = (bf16[1,2,256,256]{3,2,1,0:T(8,128)(2,1)}, bf16[1,2,256,256]{3,2,1,0:T(8,128)(2,1)S(1)}, u32[]{:S(2)}) copy-start(bf16[1,2,256,256]{3,2,1,0:T(8,128)(2,1)S(1)} %collective-permute-done.2.low_hbm) | copy-start | bytes 786436
  147.7 100.4 %copy-start.4 = (bf16[1,2,256,256]{3,2,1,0:T(8,128)(2,1)}, bf16[1,2,256,256]{3,2,1,0:T(8,128)(2,1)S(1)}, u32[]{:S(2)}) copy-start(bf16[1,2,256,256]{3,2,1,0:T(8,128)(2,1)S(1)} %collective-permute-done.3.high_hbm) | copy-start | bytes 786436
  261.4 10.1 %collective-permute-start.4 = (bf16[1,2,256,256]{3,2,1,0:T(8,128)(2,1)}, bf16[1,2,256,256]{3,2,1,0:T(8,128)(2,1)S(1)}, u32[]{:S(2)}, u32[]{:S(2)}) collective-permute-start(bf16[1,2,256,256]{3,2,1,0:T(8,128)(2,1)} %get-tuple-element.39), channel_id=1, source_target_pairs={{0,32},{32,64},{64,96},{1,33},{33,65},{65,97},{2,34},{34,66},{66,9... | collective-permute-start | bytes 786440 | tf_op jit(solution)/shard_map/ppermute | solution.py:23
  264.9 10.7 %collective-permute-start.5 = (bf16[1,2,256,256]{3,2,1,0:T(8,128)(2,1)}, bf16[1,2,256,256]{3,2,1,0:T(8,128)(2,1)S(1)}, u32[]{:S(2)}, u32[]{:S(2)}) collective-permute-start(bf16[1,2,256,256]{3,2,1,0:T(8,128)(2,1)} %get-tuple-element.40), channel_id=1, source_target_pairs={{32,0},{64,32},{96,64},{33,1},{65,33},{97,65},{34,2},{66,34},{98,6... | collective-permute-start | bytes 786440 | tf_op jit(solution)/shard_map/ppermute | solution.py:23
  271.5 104.4 %copy-start.3 = (bf16[1,2,256,256]{3,2,1,0:T(8,128)(2,1)}, bf16[1,2,256,256]{3,2,1,0:T(8,128)(2,1)S(1)}, u32[]{:S(2)}) copy-start(bf16[1,2,256,256]{3,2,1,0:T(8,128)(2,1)S(1)} %collective-permute-done.4.low_hbm) | copy-start | bytes 786436
  275.6 100.4 %copy-start.5 = (bf16[1,2,256,256]{3,2,1,0:T(8,128)(2,1)}, bf16[1,2,256,256]{3,2,1,0:T(8,128)(2,1)S(1)}, u32[]{:S(2)}) copy-start(bf16[1,2,256,256]{3,2,1,0:T(8,128)(2,1)S(1)} %collective-permute-done.5.high_hbm) | copy-start | bytes 786436
  389.7 7.4 %collective-permute-start.6 = (bf16[32,256,256]{2,1,0:T(8,128)(2,1)}, bf16[32,256,256]{2,1,0:T(8,128)(2,1)S(1)}, u32[]{:S(2)}, u32[]{:S(2)}) collective-permute-start(bf16[32,256,256]{2,1,0:T(8,128)(2,1)} %get-tuple-element.45), channel_id=1, source_target_pairs={{0,1},{1,0},{2,3},{3,2},{4,5},{5,4},{6,7},{7,6},{8,9},{9,8},{10,11... | collective-permute-start | bytes 12582920 | tf_op jit(solution)/shard_map/ppermute | solution.py:337
  400.0 14.8 %collective-permute-start.15 = (bf16[4,256,256]{2,1,0:T(8,128)(2,1)S(1)}, bf16[4,256,256]{2,1,0:T(8,128)(2,1)S(1)}, u32[]{:S(2)}, u32[]{:S(2)}) collective-permute-start(bf16[4,256,256]{2,1,0:T(8,128)(2,1)S(1)} %get-tuple-element.47), channel_id=1, source_target_pairs={{0,6},{2,0},{4,2},{6,4},{1,7},{3,1},{5,3},{7,5},{8,14},{10,8},{12,... | collective-permute-start | bytes 1572872 | tf_op jit(solution)/shard_map/ppermute | solution.py:28
  401.6 23.9 %collective-permute-start.14 = (bf16[4,256,256]{2,1,0:T(8,128)(2,1)S(1)}, bf16[4,256,256]{2,1,0:T(8,128)(2,1)S(1)}, u32[]{:S(2)}, u32[]{:S(2)}) collective-permute-start(bf16[4,256,256]{2,1,0:T(8,128)(2,1)S(1)} %get-tuple-element.48), channel_id=1, source_target_pairs={{0,4},{2,6},{4,0},{6,2},{1,5},{3,7},{5,1},{7,3},{8,12},{10,14},{12... | collective-permute-start | bytes 1572872 | tf_op jit(solution)/shard_map/ppermute | solution.py:28
  403.1 25.2 %collective-permute-start.13 = (bf16[4,256,256]{2,1,0:T(8,128)(2,1)S(1)}, bf16[4,256,256]{2,1,0:T(8,128)(2,1)S(1)}, u32[]{:S(2)}, u32[]{:S(2)}) collective-permute-start(bf16[4,256,256]{2,1,0:T(8,128)(2,1)S(1)} %get-tuple-element.49), channel_id=1, source_target_pairs={{0,2},{2,4},{4,6},{6,0},{1,3},{3,5},{5,7},{7,1},{8,10},{10,12},{12... | collective-permute-start | bytes 1572872 | tf_op jit(solution)/shard_map/ppermute | solution.py:28
  403.2 28.5 %collective-permute-start.9 = (bf16[4,256,256]{2,1,0:T(8,128)(2,1)S(1)}, bf16[4,256,256]{2,1,0:T(8,128)(2,1)S(1)}, u32[]{:S(2)}, u32[]{:S(2)}) collective-permute-start(bf16[4,256,256]{2,1,0:T(8,128)(2,1)S(1)} %get-tuple-element.51), channel_id=1, source_target_pairs={{0,24},{8,0},{16,8},{24,16},{1,25},{9,1},{17,9},{25,17},{2,26},{10... | collective-permute-start | bytes 1572872 | tf_op jit(solution)/shard_map/ppermute | solution.py:28
  404.5 27.3 %collective-permute-start.8 = (bf16[4,256,256]{2,1,0:T(8,128)(2,1)S(1)}, bf16[4,256,256]{2,1,0:T(8,128)(2,1)S(1)}, u32[]{:S(2)}, u32[]{:S(2)}) collective-permute-start(bf16[4,256,256]{2,1,0:T(8,128)(2,1)S(1)} %get-tuple-element.52), channel_id=1, source_target_pairs={{0,16},{8,24},{16,0},{24,8},{1,17},{9,25},{17,1},{25,9},{2,18},{10... | collective-permute-start | bytes 1572872 | tf_op jit(solution)/shard_map/ppermute | solution.py:28
  414.8 19.9 %collective-permute-start.7 = (bf16[4,256,256]{2,1,0:T(8,128)(2,1)S(1)}, bf16[4,256,256]{2,1,0:T(8,128)(2,1)S(1)}, u32[]{:S(2)}, u32[]{:S(2)}) collective-permute-start(bf16[4,256,256]{2,1,0:T(8,128)(2,1)S(1)} %get-tuple-element.53), channel_id=1, source_target_pairs={{0,8},{8,16},{16,24},{24,0},{1,9},{9,17},{17,25},{25,1},{2,10},{10... | collective-permute-start | bytes 1572872 | tf_op jit(solution)/shard_map/ppermute | solution.py:28
  428.5 13.4 %collective-permute-start.16 = (bf16[1,256,256]{2,1,0:T(8,128)(2,1)S(1)}, bf16[1,256,256]{2,1,0:T(8,128)(2,1)S(1)}, u32[]{:S(2)}, u32[]{:S(2)}) collective-permute-start(bf16[1,256,256]{2,1,0:T(8,128)(2,1)S(1)} %get-tuple-element.57), channel_id=1, source_target_pairs={{0,8},{8,16},{16,24},{24,0},{1,9},{9,17},{17,25},{25,1},{2,10},{10... | collective-permute-start | bytes 393224 | tf_op jit(solution)/shard_map/ppermute | solution.py:28
  429.4 13.8 %collective-permute-start.18 = (bf16[1,256,256]{2,1,0:T(8,128)(2,1)S(1)}, bf16[1,256,256]{2,1,0:T(8,128)(2,1)S(1)}, u32[]{:S(2)}, u32[]{:S(2)}) collective-permute-start(bf16[1,256,256]{2,1,0:T(8,128)(2,1)S(1)} %get-tuple-element.58), channel_id=1, source_target_pairs={{0,24},{8,0},{16,8},{24,16},{1,25},{9,1},{17,9},{25,17},{2,26},{10... | collective-permute-start | bytes 393224 | tf_op jit(solution)/shard_map/ppermute | solution.py:28
  431.8 11.5 %collective-permute-start.17 = (bf16[1,256,256]{2,1,0:T(8,128)(2,1)S(1)}, bf16[1,256,256]{2,1,0:T(8,128)(2,1)S(1)}, u32[]{:S(2)}, u32[]{:S(2)}) collective-permute-start(bf16[1,256,256]{2,1,0:T(8,128)(2,1)S(1)} %get-tuple-element.59), channel_id=1, source_target_pairs={{0,16},{8,24},{16,0},{24,8},{1,17},{9,25},{17,1},{25,9},{2,18},{10... | collective-permute-start | bytes 393224 | tf_op jit(solution)/shard_map/ppermute | solution.py:28
  434.9 10.7 %collective-permute-start.10 = (bf16[1,256,256]{2,1,0:T(8,128)(2,1)S(1)}, bf16[1,256,256]{2,1,0:T(8,128)(2,1)S(1)}, u32[]{:S(2)}, u32[]{:S(2)}) collective-permute-start(bf16[1,256,256]{2,1,0:T(8,128)(2,1)S(1)} %get-tuple-element.54), channel_id=1, source_target_pairs={{0,2},{2,4},{4,6},{6,0},{1,3},{3,5},{5,7},{7,1},{8,10},{10,12},{12... | collective-permute-start | bytes 393224 | tf_op jit(solution)/shard_map/ppermute | solution.py:28
  435.0 10.7 %collective-permute-start.12 = (bf16[1,256,256]{2,1,0:T(8,128)(2,1)S(1)}, bf16[1,256,256]{2,1,0:T(8,128)(2,1)S(1)}, u32[]{:S(2)}, u32[]{:S(2)}) collective-permute-start(bf16[1,256,256]{2,1,0:T(8,128)(2,1)S(1)} %get-tuple-element.55), channel_id=1, source_target_pairs={{0,6},{2,0},{4,2},{6,4},{1,7},{3,1},{5,3},{7,5},{8,14},{10,8},{12,... | collective-permute-start | bytes 393224 | tf_op jit(solution)/shard_map/ppermute | solution.py:28
  441.9 6.5 %collective-permute-start.11 = (bf16[1,256,256]{2,1,0:T(8,128)(2,1)S(1)}, bf16[1,256,256]{2,1,0:T(8,128)(2,1)S(1)}, u32[]{:S(2)}, u32[]{:S(2)}) collective-permute-start(bf16[1,256,256]{2,1,0:T(8,128)(2,1)S(1)} %get-tuple-element.56), channel_id=1, source_target_pairs={{0,4},{2,6},{4,0},{6,2},{1,5},{3,7},{5,1},{7,3},{8,12},{10,14},{12... | collective-permute-start | bytes 393224 | tf_op jit(solution)/shard_map/ppermute | solution.py:28

commit v4 on v3

--- a/solution.py
+++ b/solution.py
@@ -13,8 +13,9 @@
 BLOCKS = 2
 RING = 4
 ANY = pl.BlockSpec(memory_space=pl.ANY)
+VMEM = pl.BlockSpec(memory_space=pltpu.VMEM)
 SMEM = pl.BlockSpec(memory_space=pltpu.SMEM)
-PARAMS = pltpu.CompilerParams(vmem_limit_bytes=56 << 20)
+PARAMS = pltpu.CompilerParams(vmem_limit_bytes=40 << 20)
 
 
 def shifted(value, axis, steps):
@@ -23,9 +24,14 @@
     return lax.ppermute(value, axis, [(source, source + steps) for source in range(first, last)])
 
 
-def around(value, axis, steps):
-    count = lax.axis_size(axis)
-    return lax.ppermute(value, axis, [(source, (source + steps) % count) for source in range(count)])
+def around(value, steps, swapped):
+    pairs = []
+    for x in range(RING):
+        for y in range(RING):
+            for c in range(2):
+                to_x, to_y = ((x + steps) % RING, y) if c == swapped else (x, (y + steps) % RING)
+                pairs.append(((x * RING + y) * 2 + c, (to_x * RING + to_y) * 2 + c))
+    return lax.ppermute(value, GY, pairs)
 
 
 def shape(*sizes):
@@ -88,11 +94,10 @@
     )(peer, rows)
 
 
-def start_row(remote, i, a_hbm, peers_hbm, low_hbm, high_hbm, a_buf, far, sems, first, count):
-    pltpu.make_async_copy(a_hbm.at[i], a_buf.at[i], sems.at[i, 0]).start()
+def start_row(remote, i, peers_hbm, low_hbm, high_hbm, far, sems, first, count):
     for k in range(LINKS - LOCAL):
         column = remote[k, i]
-        place = (far.at[i, k], sems.at[i, 1 + k])
+        place = (far.at[i, k], sems.at[i, k])
 
         @pl.when(column < first + count)
         def _():
@@ -107,10 +112,9 @@
             pltpu.make_async_copy(high_hbm.at[0], *place).start()
 
 
-def wait_row(i, a_hbm, peers_hbm, a_buf, far, sems):
-    pltpu.make_async_copy(a_hbm.at[i], a_buf.at[i], sems.at[i, 0]).wait()
+def wait_row(i, peers_hbm, far, sems):
     for k in range(LINKS - LOCAL):
-        pltpu.make_async_copy(peers_hbm.at[0], far.at[i, k], sems.at[i, 1 + k]).wait()
+        pltpu.make_async_copy(peers_hbm.at[0], far.at[i, k], sems.at[i, k]).wait()
 
 
 def row_image(local, match, i, a_buf, own, far, rhs):
@@ -131,34 +135,23 @@
 
 def smooth_kernel(
     local, remote, match, peer, slab,
-    a_hbm, d_hbm, own_hbm, peers_hbm, low_hbm, high_hbm,
+    a_buf, d_buf, own, peers_hbm, low_hbm, high_hbm,
     rows_hbm, out_hbm, up_hbm, down_hbm,
-    a_buf, d_buf, own, far, new, rhs,
-    sems, own_sems, d_sem, rows_sem, out_sem, slab_sems,
+    far, new, rhs,
+    sems, rows_sem, out_sem, slab_sems,
 ):
     count, width = own.shape[0], own.shape[-1]
     peers = out_hbm.shape[0]
-    arrays = (a_hbm, peers_hbm, low_hbm, high_hbm, a_buf, far, sems, count, peers)
-    own_copy = pltpu.make_async_copy(own_hbm, own, own_sems.at[0])
-    d_copy = pltpu.make_async_copy(d_hbm, d_buf, d_sem.at[0])
-    own_copy.start()
-    start_row(remote, 0, *arrays)
-    d_copy.start()
-
-    @pl.loop(1, count)
+    arrays = (peers_hbm, low_hbm, high_hbm, far, sems, count, peers)
+
+    @pl.loop(0, count)
     def _(i):
         start_row(remote, i, *arrays)
 
-    own_copy.wait()
-
-    @pl.loop(0, count)
-    def _(i):
-        wait_row(i, a_hbm, peers_hbm, a_buf, far, sems)
+    @pl.loop(0, count)
+    def _(i):
+        wait_row(i, peers_hbm, far, sems)
         image = row_image(local, match, i, a_buf, own, far, rhs)
-
-        @pl.when(i == 0)
-        def _():
-            d_copy.wait()
 
         update = jnp.dot(d_buf[i], image, preferred_element_type=jnp.float32)
         for n in range(BLOCKS):
@@ -183,11 +176,9 @@
 
 def row_scratch(count, width):
     return [
-        pltpu.VMEM((count, LINKS, width, width), jnp.bfloat16),
-        pltpu.VMEM((count, BLOCKS, width, width), jnp.bfloat16),
         pltpu.VMEM((count, LINKS - LOCAL, BLOCKS, width, width), jnp.bfloat16),
         pltpu.VMEM((LINKS * width, BLOCKS * width), jnp.bfloat16),
-        pltpu.SemaphoreType.DMA((count, 1 + LINKS - LOCAL)),
+        pltpu.SemaphoreType.DMA((count, LINKS - LOCAL)),
         pltpu.SemaphoreType.DMA((1,)),
     ]
 
@@ -195,15 +186,15 @@
 def smooth(tables, peer, slab, operator, inverse, rows, received, low, high):
     count, _, width, _ = operator.shape
     one = shape(1, *rows.shape[1:])
-    a_buf, own, far, rhs, sems, single = row_scratch(count, width)
+    far, rhs, sems, single = row_scratch(count, width)
     return pl.pallas_call(
         smooth_kernel,
-        in_specs=[SMEM] * 5 + [ANY] * 6,
+        in_specs=[SMEM] * 5 + [VMEM] * 3 + [ANY] * 3,
         out_specs=[ANY] * 4,
         out_shape=(shape(*rows.shape), shape(*received.shape), one, one),
         scratch_shapes=[
-            a_buf, pltpu.VMEM(inverse.shape, jnp.bfloat16), own, far, own, rhs,
-            sems, single, single, single, single, pltpu.SemaphoreType.DMA((2,)),
+            far, pltpu.VMEM(rows.shape, jnp.bfloat16), rhs,
+            sems, single, single, pltpu.SemaphoreType.DMA((2,)),
         ],
         compiler_params=PARAMS,
         name="smooth_rows",
@@ -212,17 +203,15 @@
 
 def galerkin_kernel(
     local, remote, match, slots, here,
-    a_hbm, own_hbm, peers_hbm, low_hbm, high_hbm,
+    a_buf, own, peers_hbm, low_hbm, high_hbm,
     keep_hbm, swap_hbm,
-    a_buf, own, far, rhs, result, zero, named,
-    sems, own_sems, keep_sem, swap_sem,
+    far, rhs, result, zero, named,
+    sems, keep_sem, swap_sem,
 ):
     count, width = own.shape[0], own.shape[-1]
     peers = peers_hbm.shape[0]
     half = keep_hbm.shape[0]
-    arrays = (a_hbm, peers_hbm, low_hbm, high_hbm, a_buf, far, sems, count, peers)
-    own_copy = pltpu.make_async_copy(own_hbm, own, own_sems.at[0])
-    own_copy.start()
+    arrays = (peers_hbm, low_hbm, high_hbm, far, sems, count, peers)
 
     @pl.loop(0, count)
     def _(i):
@@ -236,13 +225,13 @@
         dx = (chip // RING - here[0] + RING) % RING
         dy = (chip % RING - here[1] + RING) % RING
         second = slot % 2
-        place = jnp.where(second == 0, dx * RING + dy, RING * RING + dy * RING + dx)
-
-        @pl.when(owner % 2 == here[2])
+        place = jnp.where(second == 0, dx * RING + dy, dy * RING + dx) * 2 + owner % 2
+
+        @pl.when(second == here[2])
         def _():
             pltpu.make_async_copy(block, keep_hbm.at[place], keep_sem.at[0]).start()
 
-        @pl.when(owner % 2 != here[2])
+        @pl.when(second != here[2])
         def _():
             pltpu.make_async_copy(block, swap_hbm.at[place], swap_sem.at[0]).start()
 
@@ -262,11 +251,9 @@
         def _():
             send(zero, slot)
 
-    own_copy.wait()
-
-    @pl.loop(0, count)
-    def _(i):
-        wait_row(i, a_hbm, peers_hbm, a_buf, far, sems)
+    @pl.loop(0, count)
+    def _(i):
+        wait_row(i, peers_hbm, far, sems)
         image = row_image(local, match, i, a_buf, own, far, rhs)
         mine = jnp.concatenate([own[i, n] for n in range(BLOCKS)], axis=1)
         partial = lax.dot_general(mine, image, (((0,), (0,)), ((), ())), preferred_element_type=jnp.float32)
@@ -283,18 +270,18 @@
 def galerkin(tables, slots, here, operator, rows, received, low, high):
     count, _, width, _ = operator.shape
     half = RING * RING * BLOCKS
-    a_buf, own, far, rhs, sems, single = row_scratch(count, width)
+    far, rhs, sems, single = row_scratch(count, width)
     return pl.pallas_call(
         galerkin_kernel,
-        in_specs=[SMEM] * 5 + [ANY] * 5,
+        in_specs=[SMEM] * 5 + [VMEM] * 2 + [ANY] * 3,
         out_specs=[ANY] * 2,
         out_shape=(shape(half, width, width), shape(half, width, width)),
         scratch_shapes=[
-            a_buf, own, far, rhs,
+            far, rhs,
             pltpu.VMEM((count, BLOCKS * BLOCKS, width, width), jnp.bfloat16),
             pltpu.VMEM((width, width), jnp.bfloat16),
             pltpu.SMEM((2 * half,), jnp.int32),
-            sems, single, single, single,
+            sems, single, single,
         ],
         compiler_params=PARAMS,
         name="galerkin_rows",
@@ -335,14 +322,18 @@
         received = lax.all_to_all(outgoing, GY, split_axis=0, concat_axis=0, tiled=True)
     keep, swap = galerkin(tables, slots, here, operator_blocks, rows, received, low, high)
     other = lax.ppermute(swap, "c", [(0, 1), (1, 0)])
-    parts = [add((keep[RING * j : RING * j + RING], other[RING * j : RING * j + RING])) for j in range(2 * RING)]
-    for axes in (("x", "y"), ("y", "x")):
-        sums = []
-        for axis, group in zip(axes, (parts[: len(parts) // 2], parts[len(parts) // 2 :])):
-            terms = [group[0], *[around(group[s], axis, s) for s in range(1, RING)]]
-            sums.append([add([term[j : j + 1] for term in terms]) for j in range(terms[0].shape[0])])
-        parts = sums[0] + sums[1]
-    return (rows, jnp.concatenate(parts, axis=0))
+    group = keep.shape[0] // RING
+    parts = [add((keep[group * j : group * j + group], other[group * j : group * j + group])) for j in range(RING)]
+    for swapped in range(2):
+        terms = [parts[0], *[around(parts[s], s, swapped) for s in range(1, RING)]]
+        group = max(terms[0].shape[0] // RING, 2)
+        parts = [add([term[j : j + group] for term in terms]) for j in range(0, terms[0].shape[0], group)]
+    total = parts[0]
+    core = lax.axis_index("c") == 0
+    mine = jnp.where(core, total[:1], total[1:])
+    theirs = lax.ppermute(jnp.where(core, total[1:], total[:1]), "c", [(0, 1), (1, 0)])
+    first, second = jnp.where(core, mine, theirs), jnp.where(core, theirs, mine)
+    return (rows, jnp.concatenate([first, second], axis=0))
 
 
 def solution(mesh):

time: 451 us -> 450 us (level)
  starting transfers between devices: 43.5 us -> 22.1 us
  waiting for transfers between devices: 47.4 us -> 66.3 us
    ppermute x12 -> x7, starting transfers between devices: 28 us -> 6.47 us  [the longest x6 6.38 us: around(): return lax.ppermute(value, GY, pairs)]
    ppermute x12 -> x7, waiting for transfers between devices: 19.7 us -> 35.5 us  [the longest x6 34.1 us: around(): return lax.ppermute(value, GY, pairs)]
  transfers between devices with their start and end apart: 19 -> 14, of which waited for: 11 -> 14; matrix products, arithmetic and copies ran while one was open for 0% -> 0% of each run, Pallas kernels for 1% -> 0%
where the time goes in v4:
time: 450 us; the launch traced here: 448 us
  blocking collectives  304 us (68%)
  waiting for transfers between devices  66.3 us (15%)
  Pallas kernels  47.5 us (11%)
  starting transfers between devices  22.1 us (5%)
  other arithmetic  4.67 us (1%)
    all_to_all x3, blocking collectives, body(): lax.all_to_all(outgoing, GY, split_axis=0, concat_axis=0, tiled=True)  304 us
    ppermute x6, waiting for transfers between devices, around(): return lax.ppermute(value, GY, pairs)  34.1 us
    pallas_call x1, Pallas kernels, galerkin(): pl.pallas_call(galerkin_kernel, in_specs=[SMEM] * 5 + [VMEM] * 2 + [ANY]...  25 us
    ppermute x6, waiting for transfers between devices, shifted(): lax.ppermute(value, axis, [(source, source + steps) for source in range(f...  24 us
    pallas_call x2, Pallas kernels, smooth(): pl.pallas_call(smooth_kernel, in_specs=[SMEM] * 5 + [VMEM] * 3 + [ANY] *...  20.1 us
    ppermute x6, starting transfers between devices, shifted(): lax.ppermute(value, axis, [(source, source + steps) for source in range(f...  15.2 us
  transfers between devices with their start and end apart: 14, of which 14 were waited for; matrix products, arithmetic and copies ran while one was open for 0% of the time, Pallas kernels for 0%

profile of v4, /device:TPU:0, one launch (start us, length us, event | category | flops | bytes accessed | tf_op | source)
XLA Modules:
  0.0 448.3 jit_solution(5019371298284019036)
XLA Ops:
  0.6 0.0 copy-start
  0.6 1.6 copy-done
  2.2 0.0 copy-start.7
  2.2 0.7 copy-done.7
  2.9 0.0 copy-start.1
  2.9 0.0 copy-start.9
  2.9 0.7 pick_rows.1
  3.5 3.9 collective-permute-start
  7.5 1.3 collective-permute-start.1
  8.8 0.0 copy-done.1
  8.8 0.0 copy-done.9
  8.8 0.0 slice-start
  8.8 1.8 pack_rows.1
  10.6 0.1 pad_add_fusion.here
  10.7 0.0 slice-start.1
  10.7 0.0 copy-start.2
  10.7 0.0 copy-start.6
  10.7 0.0 copy-start.8
  10.7 2.3 collective-permute-done.low_hbm
  13.0 4.3 collective-permute-done.1.high_hbm
  17.3 102.7 %all_to_all.15.peers_hbm = bf16[32,2,256,256]{3,2,1,0:T(8,128)(2,1)} all-to-all(bf16[32,2,256,256]{3,2,1,0:T(8,128)(2,1)S(1)} %pack_rows.1), channel_id=1, replica_groups=mesh['gx'=4,'x'=4,'y'=4,'c'=2] {'x','y','c'}, dimensions={0} | all-to-all | bytes 16777216 | tf_op jit(solution)/shard_map/all_to_all | solution.py:317
  120.0 0.0 slice-done
  120.0 0.0 slice-done.1
  120.0 0.0 copy-done.2
  120.0 0.0 copy-done.4
  120.0 0.0 copy-done.5
  120.0 0.0 copy-done.6
  120.0 0.0 copy-done.8
  120.0 10.0 %smooth_rows.2 = (bf16[8,2,256,256]{3,2,1,0:T(8,128)(2,1)S(1)}, bf16[32,2,256,256]{3,2,1,0:T(8,128)(2,1)}, bf16[1,2,256,256]{3,2,1,0:T(8,128)(2,1)S(1)}, bf16[1,2,256,256]{3,2,1,0:T(8,128)(2,1)S(1)}) custom-call(s32[2,8]{1,0:T(2,128)S(1)} %bitcast.15, s32[4,8]{1,0:T(4,128)S(1)} %bitcast.12, s32[6,2,8]{2,1,0:T(2,128)S(1)} %bitcast.9, s32[1,32]{1,0:T(1,128)S(1)} %copy-done.9, ...), custom_call_target="tpu_custom_call" | custom-call | tf_op jit(solution)/shard_map/smooth_rows/pallas_call | solution.py:190
  130.0 3.7 collective-permute-start.2
  133.7 1.3 collective-permute-start.3
  135.0 4.6 %collective-permute-done.2.low_hbm = bf16[1,2,256,256]{3,2,1,0:T(8,128)(2,1)S(1)} collective-permute-done((bf16[1,2,256,256]{3,2,1,0:T(8,128)(2,1)S(1)}, bf16[1,2,256,256]{3,2,1,0:T(8,128)(2,1)S(1)}, u32[]{:S(2)}, u32[]{:S(2)}) %collective-permute-start.2) | collective-permute-done | bytes 262176 | tf_op jit(solution)/shard_map/ppermute | solution.py:24
  139.6 4.1 collective-permute-done.3.high_hbm
  143.8 100.4 %all_to_all.16.peers_hbm = bf16[32,2,256,256]{3,2,1,0:T(8,128)(2,1)} all-to-all(bf16[32,2,256,256]{3,2,1,0:T(8,128)(2,1)} %get-tuple-element.33), channel_id=1, replica_groups=mesh['gx'=4,'x'=4,'y'=4,'c'=2] {'x','y','c'}, dimensions={0} | all-to-all | bytes 16777216 | tf_op jit(solution)/shard_map/all_to_all | solution.py:322
  244.2 10.1 %smooth_rows.3 = (bf16[8,2,256,256]{3,2,1,0:T(8,128)(2,1)}, bf16[32,2,256,256]{3,2,1,0:T(8,128)(2,1)}, bf16[1,2,256,256]{3,2,1,0:T(8,128)(2,1)S(1)}, bf16[1,2,256,256]{3,2,1,0:T(8,128)(2,1)S(1)}) custom-call(s32[2,8]{1,0:T(2,128)S(1)} %bitcast.16, s32[4,8]{1,0:T(4,128)S(1)} %bitcast.13, s32[6,2,8]{2,1,0:T(2,128)S(1)} %bitcast.10, s32[1,32]{1,0:T(1,128)S(1)} %copy-done.9, ...), custom_call_target="tpu_custom_call" | custom-call | tf_op jit(solution)/shard_map/smooth_rows/pallas_call | solution.py:190
  254.3 3.7 collective-permute-start.4
  258.0 1.3 collective-permute-start.5
  259.3 4.6 %collective-permute-done.4.low_hbm = bf16[1,2,256,256]{3,2,1,0:T(8,128)(2,1)S(1)} collective-permute-done((bf16[1,2,256,256]{3,2,1,0:T(8,128)(2,1)S(1)}, bf16[1,2,256,256]{3,2,1,0:T(8,128)(2,1)S(1)}, u32[]{:S(2)}, u32[]{:S(2)}) %collective-permute-start.4) | collective-permute-done | bytes 262176 | tf_op jit(solution)/shard_map/ppermute | solution.py:24
  263.8 4.1 collective-permute-done.5.high_hbm
  268.0 100.5 %all_to_all.17.peers_hbm = bf16[32,2,256,256]{3,2,1,0:T(8,128)(2,1)} all-to-all(bf16[32,2,256,256]{3,2,1,0:T(8,128)(2,1)} %get-tuple-element.41), channel_id=1, replica_groups=mesh['gx'=4,'x'=4,'y'=4,'c'=2] {'x','y','c'}, dimensions={0} | all-to-all | bytes 16777216 | tf_op jit(solution)/shard_map/all_to_all | solution.py:322
  368.5 0.0 copy-done.3
  368.5 0.0 copy-done.10
  368.5 25.0 %galerkin_rows.1 = (bf16[32,256,256]{2,1,0:T(8,128)(2,1)S(1)}, bf16[32,256,256]{2,1,0:T(8,128)(2,1)S(1)}) custom-call(s32[2,8]{1,0:T(2,128)S(1)} %bitcast.17, s32[4,8]{1,0:T(4,128)S(1)} %bitcast.14, s32[6,2,8]{2,1,0:T(2,128)S(1)} %bitcast.11, s32[2,2,8]{2,1,0:T(2,128)S(1)} %bitcast.18, s32[3]{0:T(128)S(1)} %pad_add_fusion.here, ...), custom_call_target="tpu_custom_call" | custom-call | tf_op jit(solution)/shard_map/galerkin_rows/pallas_call | solution.py:274
  393.5 0.4 collective-permute-start.6
  393.9 6.8 %collective-permute-done.6 = bf16[32,256,256]{2,1,0:T(8,128)(2,1)S(1)} collective-permute-done((bf16[32,256,256]{2,1,0:T(8,128)(2,1)S(1)}, bf16[32,256,256]{2,1,0:T(8,128)(2,1)S(1)}, u32[]{:S(2)}, u32[]{:S(2)}) %collective-permute-start.6) | collective-permute-done | bytes 4194336 | tf_op jit(solution)/shard_map/ppermute | solution.py:324
  400.7 1.3 add_convert_fusion.3
  402.0 1.6 collective-permute-start.9
  403.6 0.5 collective-permute-start.8
  404.1 0.9 collective-permute-start.7
  405.0 11.9 %collective-permute-done.9 = bf16[8,256,256]{2,1,0:T(8,128)(2,1)S(1)} collective-permute-done((bf16[8,256,256]{2,1,0:T(8,128)(2,1)S(1)}, bf16[8,256,256]{2,1,0:T(8,128)(2,1)S(1)}, u32[]{:S(2)}, u32[]{:S(2)}) %collective-permute-start.9) | collective-permute-done | bytes 1048608 | tf_op jit(solution)/shard_map/ppermute | solution.py:34
  416.9 3.1 collective-permute-done.8
  420.0 11.1 %collective-permute-done.7 = bf16[8,256,256]{2,1,0:T(8,128)(2,1)S(1)} collective-permute-done((bf16[8,256,256]{2,1,0:T(8,128)(2,1)S(1)}, bf16[8,256,256]{2,1,0:T(8,128)(2,1)S(1)}, u32[]{:S(2)}, u32[]{:S(2)}) %collective-permute-start.7) | collective-permute-done | bytes 1048608 | tf_op jit(solution)/shard_map/ppermute | solution.py:34
  431.1 1.0 copy-done.11
  432.1 1.2 add_convert_fusion.7
  433.3 0.0 collective-permute-start.10
  433.3 3.2 collective-permute-start.12
  436.5 0.2 collective-permute-start.11
  436.7 4.4 collective-permute-done.10
  441.1 2.5 collective-permute-done.12
  443.5 1.2 collective-permute-done.11
  444.7 1.3 add_convert_fusion.4
  446.1 0.1 collective-permute-start.13
  446.2 1.3 collective-permute-done.13
  447.5 0.7 pad_maximum_fusion
  (8 shorter events, 0.1 us)
Async XLA Ops:
  0.6 1.6 copy-start
  2.2 0.7 copy-start.7
  2.9 5.9 %copy-start.1 = (bf16[8,2,256,256]{3,2,1,0:T(8,128)(2,1)S(1)}, bf16[8,2,256,256]{3,2,1,0:T(8,128)(2,1)}, u32[]{:S(2)}) copy-start(bf16[8,2,256,256]{3,2,1,0:T(8,128)(2,1)} %own.1) | copy-start | bytes 6291460
  2.9 5.9 %copy-start.9 = (s32[1,32]{1,0:T(1,128)S(1)}, s32[1,32]{1,0:T(1,128)}, u32[]{:S(2)}) copy-start(s32[1,32]{1,0:T(1,128)} %peer.5) | copy-start | bytes 388
  3.5 9.5 %collective-permute-start = (bf16[1,2,256,256]{3,2,1,0:T(8,128)(2,1)S(1)}, bf16[1,2,256,256]{3,2,1,0:T(8,128)(2,1)S(1)}, u32[]{:S(2)}, u32[]{:S(2)}) collective-permute-start(bf16[1,2,256,256]{3,2,1,0:T(8,128)(2,1)S(1)} %get-tuple-element.24), channel_id=1, source_target_pairs={{0,32},{32,64},{64,96},{1,33},{33,65},{65,97},{2,34},{34,66},{66,9... | collective-permute-start | bytes 786440 | tf_op jit(solution)/shard_map/ppermute | solution.py:24
  7.5 9.8 %collective-permute-start.1 = (bf16[1,2,256,256]{3,2,1,0:T(8,128)(2,1)S(1)}, bf16[1,2,256,256]{3,2,1,0:T(8,128)(2,1)S(1)}, u32[]{:S(2)}, u32[]{:S(2)}) collective-permute-start(bf16[1,2,256,256]{3,2,1,0:T(8,128)(2,1)S(1)} %get-tuple-element.25), channel_id=1, source_target_pairs={{32,0},{64,32},{96,64},{33,1},{65,33},{97,65},{34,2},{66,34},{98,6... | collective-permute-start | bytes 786440 | tf_op jit(solution)/shard_map/ppermute | solution.py:24
  8.8 111.2 %slice-start = ((s8[6291456]{0:T(1024)(128)(4,1)}), s8[4194304]{0:T(1024)(128)(4,1)S(1)}, s32[]{:S(2)}) async-start(s8[6291456]{0:T(1024)(128)(4,1)} %bitcast.7), calls=%async_computation.3 | async-start | bytes 8388608
  10.7 109.3 %slice-start.1 = ((s8[6291456]{0:T(1024)(128)(4,1)}), s8[2097152]{0:T(1024)(128)(4,1)S(1)}, s32[]{:S(2)}) async-start(s8[6291456]{0:T(1024)(128)(4,1)} %bitcast.7), calls=%async_computation.4 | async-start | bytes 4194304
  10.7 109.3 %copy-start.2 = (bf16[8,256,256]{2,1,0:T(8,128)(2,1)S(1)}, bf16[8,256,256]{2,1,0:T(8,128)(2,1)}, u32[]{:S(2)}) copy-start(bf16[8,256,256]{2,1,0:T(8,128)(2,1)} %d_buf.3) | copy-start | bytes 3145732
  10.7 109.3 %copy-start.4 = (s32[8,6,2]{0,2,1:T(2,128)S(1)}, s32[8,6,2]{0,2,1:T(2,128)}, u32[]{:S(2)}) copy-start(s32[8,6,2]{0,2,1:T(2,128)} %param.12) | copy-start | bytes 1156
  10.7 109.3 %copy-start.5 = (s32[8,4]{0,1:T(4,128)S(1)}, s32[8,4]{0,1:T(4,128)}, u32[]{:S(2)}) copy-start(s32[8,4]{0,1:T(4,128)} %param.11) | copy-start | bytes 388
  10.7 109.3 %copy-start.6 = (s32[8,2]{0,1:T(2,128)S(1)}, s32[8,2]{0,1:T(2,128)}, u32[]{:S(2)}) copy-start(s32[8,2]{0,1:T(2,128)} %param.10) | copy-start | bytes 196
  10.7 109.3 %copy-start.8 = (s32[1,2]{1,0:T(1,128)S(1)}, s32[1,2]{1,0:T(1,128)}, u32[]{:S(2)}) copy-start(s32[1,2]{1,0:T(1,128)} %slab.5) | copy-start | bytes 28
  130.0 9.6 %collective-permute-start.2 = (bf16[1,2,256,256]{3,2,1,0:T(8,128)(2,1)S(1)}, bf16[1,2,256,256]{3,2,1,0:T(8,128)(2,1)S(1)}, u32[]{:S(2)}, u32[]{:S(2)}) collective-permute-start(bf16[1,2,256,256]{3,2,1,0:T(8,128)(2,1)S(1)} %get-tuple-element.31), channel_id=1, source_target_pairs={{0,32},{32,64},{64,96},{1,33},{33,65},{65,97},{2,34},{34,66},{66,9... | collective-permute-start | bytes 786440 | tf_op jit(solution)/shard_map/ppermute | solution.py:24
  133.7 10.0 %collective-permute-start.3 = (bf16[1,2,256,256]{3,2,1,0:T(8,128)(2,1)S(1)}, bf16[1,2,256,256]{3,2,1,0:T(8,128)(2,1)S(1)}, u32[]{:S(2)}, u32[]{:S(2)}) collective-permute-start(bf16[1,2,256,256]{3,2,1,0:T(8,128)(2,1)S(1)} %get-tuple-element.32), channel_id=1, source_target_pairs={{32,0},{64,32},{96,64},{33,1},{65,33},{97,65},{34,2},{66,34},{98,6... | collective-permute-start | bytes 786440 | tf_op jit(solution)/shard_map/ppermute | solution.py:24
  254.3 9.6 %collective-permute-start.4 = (bf16[1,2,256,256]{3,2,1,0:T(8,128)(2,1)S(1)}, bf16[1,2,256,256]{3,2,1,0:T(8,128)(2,1)S(1)}, u32[]{:S(2)}, u32[]{:S(2)}) collective-permute-start(bf16[1,2,256,256]{3,2,1,0:T(8,128)(2,1)S(1)} %get-tuple-element.39), channel_id=1, source_target_pairs={{0,32},{32,64},{64,96},{1,33},{33,65},{65,97},{2,34},{34,66},{66,9... | collective-permute-start | bytes 786440 | tf_op jit(solution)/shard_map/ppermute | solution.py:24
  258.0 10.0 %collective-permute-start.5 = (bf16[1,2,256,256]{3,2,1,0:T(8,128)(2,1)S(1)}, bf16[1,2,256,256]{3,2,1,0:T(8,128)(2,1)S(1)}, u32[]{:S(2)}, u32[]{:S(2)}) collective-permute-start(bf16[1,2,256,256]{3,2,1,0:T(8,128)(2,1)S(1)} %get-tuple-element.40), channel_id=1, source_target_pairs={{32,0},{64,32},{96,64},{33,1},{65,33},{97,65},{34,2},{66,34},{98,6... | collective-permute-start | bytes 786440 | tf_op jit(solution)/shard_map/ppermute | solution.py:24
  268.0 100.5 %copy-start.3 = (bf16[8,2,256,256]{3,2,1,0:T(8,128)(2,1)S(1)}, bf16[8,2,256,256]{3,2,1,0:T(8,128)(2,1)}, u32[]{:S(2)}) copy-start(bf16[8,2,256,256]{3,2,1,0:T(8,128)(2,1)} %get-tuple-element.22.own) | copy-start | bytes 6291460
  268.0 100.5 %copy-start.10 = (s32[8,2,2]{0,2,1:T(2,128)S(1)}, s32[8,2,2]{0,2,1:T(2,128)}, u32[]{:S(2)}) copy-start(s32[8,2,2]{0,2,1:T(2,128)} %param.17) | copy-start | bytes 388
  393.5 7.2 %collective-permute-start.6 = (bf16[32,256,256]{2,1,0:T(8,128)(2,1)S(1)}, bf16[32,256,256]{2,1,0:T(8,128)(2,1)S(1)}, u32[]{:S(2)}, u32[]{:S(2)}) collective-permute-start(bf16[32,256,256]{2,1,0:T(8,128)(2,1)S(1)} %get-tuple-element.45), channel_id=1, source_target_pairs={{0,1},{1,0},{2,3},{3,2},{4,5},{5,4},{6,7},{7,6},{8,9},{9,8},{10,11... | collective-permute-start | bytes 12582920 | tf_op jit(solution)/shard_map/ppermute | solution.py:324
  402.0 14.9 %collective-permute-start.9 = (bf16[8,256,256]{2,1,0:T(8,128)(2,1)S(1)}, bf16[8,256,256]{2,1,0:T(8,128)(2,1)S(1)}, u32[]{:S(2)}, u32[]{:S(2)}) collective-permute-start(bf16[8,256,256]{2,1,0:T(8,128)(2,1)S(1)} %get-tuple-element.47), channel_id=1, source_target_pairs={{0,24},{1,7},{2,26},{3,1},{4,28},{5,3},{6,30},{7,5},{8,0},{9,15},{... | collective-permute-start | bytes 3145736 | tf_op jit(solution)/shard_map/ppermute | solution.py:34
  403.6 16.4 %collective-permute-start.8 = (bf16[8,256,256]{2,1,0:T(8,128)(2,1)S(1)}, bf16[8,256,256]{2,1,0:T(8,128)(2,1)S(1)}, u32[]{:S(2)}, u32[]{:S(2)}) collective-permute-start(bf16[8,256,256]{2,1,0:T(8,128)(2,1)S(1)} %get-tuple-element.48), channel_id=1, source_target_pairs={{0,16},{1,5},{2,18},{3,7},{4,20},{5,1},{6,22},{7,3},{8,24},{9,13},... | collective-permute-start | bytes 3145736 | tf_op jit(solution)/shard_map/ppermute | solution.py:34
  404.1 27.1 %collective-permute-start.7 = (bf16[8,256,256]{2,1,0:T(8,128)(2,1)S(1)}, bf16[8,256,256]{2,1,0:T(8,128)(2,1)S(1)}, u32[]{:S(2)}, u32[]{:S(2)}) collective-permute-start(bf16[8,256,256]{2,1,0:T(8,128)(2,1)S(1)} %get-tuple-element.49), channel_id=1, source_target_pairs={{0,8},{1,3},{2,10},{3,5},{4,12},{5,7},{6,14},{7,1},{8,16},{9,11},{... | collective-permute-start | bytes 3145736 | tf_op jit(solution)/shard_map/ppermute | solution.py:34
  431.1 1.0 copy-start.11
  433.3 7.8 %collective-permute-start.10 = (bf16[2,256,256]{2,1,0:T(8,128)(2,1)}, bf16[2,256,256]{2,1,0:T(8,128)(2,1)S(1)}, u32[]{:S(2)}, u32[]{:S(2)}) collective-permute-start(bf16[2,256,256]{2,1,0:T(8,128)(2,1)} %get-tuple-element.50), channel_id=1, source_target_pairs={{0,2},{1,9},{2,4},{3,11},{4,6},{5,13},{6,0},{7,15},{8,10},{9,17},{... | collective-permute-start | bytes 786440 | tf_op jit(solution)/shard_map/ppermute | solution.py:34
  433.3 10.2 %collective-permute-start.12 = (bf16[2,256,256]{2,1,0:T(8,128)(2,1)}, bf16[2,256,256]{2,1,0:T(8,128)(2,1)}, u32[]{:S(2)}, u32[]{:S(2)}) collective-permute-start(bf16[2,256,256]{2,1,0:T(8,128)(2,1)} %get-tuple-element.51), channel_id=1, source_target_pairs={{0,6},{1,25},{2,0},{3,27},{4,2},{5,29},{6,4},{7,31},{8,14},{9,1},{... | collective-permute-start | bytes 786440 | tf_op jit(solution)/shard_map/ppermute | solution.py:34
  436.5 8.2 %collective-permute-start.11 = (bf16[2,256,256]{2,1,0:T(8,128)(2,1)}, bf16[2,256,256]{2,1,0:T(8,128)(2,1)}, u32[]{:S(2)}, u32[]{:S(2)}) collective-permute-start(bf16[2,256,256]{2,1,0:T(8,128)(2,1)} %get-tuple-element.52), channel_id=1, source_target_pairs={{0,4},{1,17},{2,6},{3,19},{4,0},{5,21},{6,2},{7,23},{8,12},{9,25},... | collective-permute-start | bytes 786440 | tf_op jit(solution)/shard_map/ppermute | solution.py:34
  446.1 1.4 collective-permute-start.13

commit v5 on v4

--- a/solution.py
+++ b/solution.py
@@ -94,10 +94,10 @@
     )(peer, rows)
 
 
-def start_row(remote, i, peers_hbm, low_hbm, high_hbm, far, sems, first, count):
+def start_row(remote, i, slot, peers_hbm, low_hbm, high_hbm, far, sems, first, count):
     for k in range(LINKS - LOCAL):
         column = remote[k, i]
-        place = (far.at[i, k], sems.at[i, k])
+        place = (far.at[slot, k], sems.at[slot, k])
 
         @pl.when(column < first + count)
         def _():
@@ -117,7 +117,7 @@
         pltpu.make_async_copy(peers_hbm.at[0], far.at[i, k], sems.at[i, k]).wait()
 
 
-def row_image(local, match, i, a_buf, own, far, rhs):
+def row_image(local, match, i, slot, a_buf, own, far, rhs):
     width = own.shape[-1]
     for k in range(LINKS):
         for n in range(BLOCKS):
@@ -126,37 +126,57 @@
             if k < LOCAL:
                 block = own[local[k, i], there]
             else:
-                block = far[i, k - LOCAL, there]
+                block = far[slot, k - LOCAL, there]
             block = jnp.where(wanted < BLOCKS, block, jnp.zeros_like(block))
             rhs[k * width : (k + 1) * width, n * width : (n + 1) * width] = block
     lhs = jnp.concatenate([a_buf[i, k] for k in range(LINKS)], axis=1)
     return jnp.dot(lhs, rhs[...], preferred_element_type=jnp.float32).astype(jnp.bfloat16)
 
 
+def new_row(local, match, i, slot, a_buf, d_buf, own, far, rhs):
+    width = own.shape[-1]
+    image = row_image(local, match, i, slot, a_buf, own, far, rhs)
+    update = jnp.dot(d_buf[i], image, preferred_element_type=jnp.float32)
+    halves = [update[:, n * width : (n + 1) * width] for n in range(BLOCKS)]
+    return [(own[i, n].astype(jnp.float32) - halves[n]).astype(jnp.bfloat16) for n in range(BLOCKS)]
+
+
+def slab_kernel(
+    local, remote, match, slab,
+    a_buf, d_buf, own, peers_hbm, low_hbm, high_hbm,
+    up, down,
+    far, rhs,
+    sems,
+):
+    arrays = (peers_hbm, low_hbm, high_hbm, far, sems, own.shape[0], peers_hbm.shape[0])
+    for j in range(2):
+        start_row(remote, slab[0, j], j, *arrays)
+    for j, out in enumerate((up, down)):
+        wait_row(j, peers_hbm, far, sems)
+        for n, value in enumerate(new_row(local, match, slab[0, j], j, a_buf, d_buf, own, far, rhs)):
+            out[0, n] = value
+
+
 def smooth_kernel(
-    local, remote, match, peer, slab,
+    local, remote, match, peer,
     a_buf, d_buf, own, peers_hbm, low_hbm, high_hbm,
-    rows_hbm, out_hbm, up_hbm, down_hbm,
+    rows_hbm, out_hbm,
     far, new, rhs,
-    sems, rows_sem, out_sem, slab_sems,
+    sems, rows_sem, out_sem,
 ):
-    count, width = own.shape[0], own.shape[-1]
+    count = own.shape[0]
     peers = out_hbm.shape[0]
     arrays = (peers_hbm, low_hbm, high_hbm, far, sems, count, peers)
 
     @pl.loop(0, count)
     def _(i):
-        start_row(remote, i, *arrays)
+        start_row(remote, i, i, *arrays)
 
     @pl.loop(0, count)
     def _(i):
         wait_row(i, peers_hbm, far, sems)
-        image = row_image(local, match, i, a_buf, own, far, rhs)
-
-        update = jnp.dot(d_buf[i], image, preferred_element_type=jnp.float32)
-        for n in range(BLOCKS):
-            value = own[i, n].astype(jnp.float32) - update[:, n * width : (n + 1) * width]
-            new[i, n] = value.astype(jnp.bfloat16)
+        for n, value in enumerate(new_row(local, match, i, i, a_buf, d_buf, own, far, rhs)):
+            new[i, n] = value
         pltpu.make_async_copy(new.at[i], rows_hbm.at[i], rows_sem.at[0]).start()
         for q in range(peers):
 
@@ -164,14 +184,8 @@
             def _():
                 pltpu.make_async_copy(new.at[i], out_hbm.at[q], out_sem.at[0]).start()
 
-    up = pltpu.make_async_copy(new.at[slab[0, 0]], up_hbm.at[0], slab_sems.at[0])
-    down = pltpu.make_async_copy(new.at[slab[0, 1]], down_hbm.at[0], slab_sems.at[1])
-    up.start()
-    down.start()
     pltpu.make_async_copy(rows_hbm, rows_hbm, rows_sem.at[0]).wait()
     pltpu.make_async_copy(out_hbm, out_hbm, out_sem.at[0]).wait()
-    up.wait()
-    down.wait()
 
 
 def row_scratch(count, width):
@@ -183,88 +197,79 @@
     ]
 
 
-def smooth(tables, peer, slab, operator, inverse, rows, received, low, high):
+def slab_rows(tables, slab, operator, inverse, rows, received, low, high):
+    width = operator.shape[-1]
+    one = shape(1, *rows.shape[1:])
+    return pl.pallas_call(
+        slab_kernel,
+        in_specs=[SMEM] * 4 + [VMEM] * 3 + [ANY] * 3,
+        out_specs=[VMEM] * 2,
+        out_shape=(one, one),
+        scratch_shapes=row_scratch(2, width)[:3],
+        compiler_params=PARAMS,
+        name="slab_rows",
+    )(*tables, slab, operator, inverse, rows, received, low, high)
+
+
+def smooth(tables, peer, operator, inverse, rows, received, low, high):
     count, _, width, _ = operator.shape
-    one = shape(1, *rows.shape[1:])
     far, rhs, sems, single = row_scratch(count, width)
+    flops = 2 * count * (LINKS + 1) * BLOCKS * width**3
     return pl.pallas_call(
         smooth_kernel,
-        in_specs=[SMEM] * 5 + [VMEM] * 3 + [ANY] * 3,
-        out_specs=[ANY] * 4,
-        out_shape=(shape(*rows.shape), shape(*received.shape), one, one),
-        scratch_shapes=[
-            far, pltpu.VMEM(rows.shape, jnp.bfloat16), rhs,
-            sems, single, single, pltpu.SemaphoreType.DMA((2,)),
-        ],
+        in_specs=[SMEM] * 4 + [VMEM] * 3 + [ANY] * 3,
+        out_specs=[ANY] * 2,
+        out_shape=(shape(*rows.shape), shape(*received.shape)),
+        scratch_shapes=[far, pltpu.VMEM(rows.shape, jnp.bfloat16), rhs, sems, single, single],
+        cost_estimate=pl.CostEstimate(flops=flops, transcendentals=0, bytes_accessed=28 << 20),
         compiler_params=PARAMS,
         name="smooth_rows",
-    )(*tables, peer, slab, operator, inverse, rows, received, low, high)
+    )(*tables, peer, operator, inverse, rows, received, low, high)
 
 
 def galerkin_kernel(
     local, remote, match, slots, here,
     a_buf, own, peers_hbm, low_hbm, high_hbm,
-    keep_hbm, swap_hbm,
-    far, rhs, result, zero, named,
-    sems, keep_sem, swap_sem,
+    keep, swap,
+    far, rhs,
+    sems,
 ):
     count, width = own.shape[0], own.shape[-1]
     peers = peers_hbm.shape[0]
-    half = keep_hbm.shape[0]
     arrays = (peers_hbm, low_hbm, high_hbm, far, sems, count, peers)
 
     @pl.loop(0, count)
     def _(i):
-        start_row(remote, i, *arrays)
-
-    zero[...] = jnp.zeros_like(zero)
-
-    def send(block, slot):
-        owner = slot // 2
-        chip = owner // 2
-        dx = (chip // RING - here[0] + RING) % RING
-        dy = (chip % RING - here[1] + RING) % RING
-        second = slot % 2
-        place = jnp.where(second == 0, dx * RING + dy, dy * RING + dx) * 2 + owner % 2
-
-        @pl.when(second == here[2])
-        def _():
-            pltpu.make_async_copy(block, keep_hbm.at[place], keep_sem.at[0]).start()
-
-        @pl.when(second != here[2])
-        def _():
-            pltpu.make_async_copy(block, swap_hbm.at[place], swap_sem.at[0]).start()
-
-    @pl.loop(0, 2 * half)
-    def _(slot):
-        named[slot] = 0
-
-    @pl.loop(0, count)
-    def _(i):
-        for n1 in range(BLOCKS):
-            for n2 in range(BLOCKS):
-                named[slots[n1, n2, i]] = 1
-
-    @pl.loop(0, 2 * half)
-    def _(slot):
-        @pl.when(named[slot] == 0)
-        def _():
-            send(zero, slot)
+        start_row(remote, i, i, *arrays)
+
+    keep[...] = jnp.zeros_like(keep)
+    swap[...] = jnp.zeros_like(swap)
 
     @pl.loop(0, count)
     def _(i):
         wait_row(i, peers_hbm, far, sems)
-        image = row_image(local, match, i, a_buf, own, far, rhs)
+        image = row_image(local, match, i, i, a_buf, own, far, rhs)
         mine = jnp.concatenate([own[i, n] for n in range(BLOCKS)], axis=1)
         partial = lax.dot_general(mine, image, (((0,), (0,)), ((), ())), preferred_element_type=jnp.float32)
         for n1 in range(BLOCKS):
             for n2 in range(BLOCKS):
                 block = partial[n1 * width : (n1 + 1) * width, n2 * width : (n2 + 1) * width]
-                result[i, n1 * BLOCKS + n2] = block.astype(jnp.bfloat16)
-                send(result.at[i, n1 * BLOCKS + n2], slots[n1, n2, i])
-
-    pltpu.make_async_copy(keep_hbm, keep_hbm, keep_sem.at[0]).wait()
-    pltpu.make_async_copy(swap_hbm, swap_hbm, swap_sem.at[0]).wait()
+                block = block.astype(jnp.bfloat16)
+                slot = slots[n1, n2, i]
+                owner = slot // 2
+                chip = owner // 2
+                dx = (chip // RING - here[0] + RING) % RING
+                dy = (chip % RING - here[1] + RING) % RING
+                second = slot % 2
+                place = jnp.where(second == 0, dx * RING + dy, dy * RING + dx) * 2 + owner % 2
+
+                @pl.when(second == here[2])
+                def _():
+                    keep[place] = block
+
+                @pl.when(second != here[2])
+                def _():
+                    swap[place] = block
 
 
 def galerkin(tables, slots, here, operator, rows, received, low, high):
@@ -274,16 +279,10 @@
     return pl.pallas_call(
         galerkin_kernel,
         in_specs=[SMEM] * 5 + [VMEM] * 2 + [ANY] * 3,
-        out_specs=[ANY] * 2,
+        out_specs=[VMEM] * 2,
         out_shape=(shape(half, width, width), shape(half, width, width)),
-        scratch_shapes=[
-            far, rhs,
-            pltpu.VMEM((count, BLOCKS * BLOCKS, width, width), jnp.bfloat16),
-            pltpu.VMEM((width, width), jnp.bfloat16),
-            pltpu.SMEM((2 * half,), jnp.int32),
-            sems, single, single,
-        ],
-        compiler_params=PARAMS,
+        scratch_shapes=[far, rhs, sems],
+        compiler_params=pltpu.CompilerParams(vmem_limit_bytes=30 << 20),
         name="galerkin_rows",
     )(*tables, slots, here, operator, rows, received, low, high)
 
@@ -316,8 +315,11 @@
     outgoing, low, high, here = lax.optimization_barrier((outgoing, low, high, here))
     received = lax.all_to_all(outgoing, GY, split_axis=0, concat_axis=0, tiled=True)
     for smooth_pass in range(2):
-        rows, outgoing, up, down = smooth(tables, peer, slab, operator_blocks, inverse_diagonal, rows, received, low, high)
+        operands = (operator_blocks, inverse_diagonal, rows, received, low, high)
+        up, down = slab_rows(tables, slab, *operands)
+        up, down, operands = lax.optimization_barrier((up, down, operands))
         low, high = shifted(up, "gx", 1), shifted(down, "gx", -1)
+        rows, outgoing = smooth(tables, peer, *operands)
         outgoing, low, high = lax.optimization_barrier((outgoing, low, high))
         received = lax.all_to_all(outgoing, GY, split_axis=0, concat_axis=0, tiled=True)
     keep, swap = galerkin(tables, slots, here, operator_blocks, rows, received, low, high)

time: 450 us -> 426 us (0.947)
  waiting for transfers between devices: 66.3 us -> 48.9 us
  Pallas kernels: 47.5 us -> 40.7 us
    ppermute x6, waiting for transfers between devices: 24 us -> 6.61 us  [shifted(): lax.ppermute(value, axis, [(source, source + steps) for source in range(f...]
    pallas_call x1, Pallas kernels: 25 us -> 10.8 us  [galerkin(): pl.pallas_call(galerkin_kernel, in_specs=[SMEM] * 5 + [VMEM] * 2 + [ANY]...]
    pallas_call x2 -> x4, Pallas kernels: 20.1 us -> 27.5 us  [the longest x2 20.5 us: smooth(): pl.pallas_call(smooth_kernel, in_specs=[SMEM] * 4 + [VMEM] * 3 + [ANY] *...]
  transfers between devices with their start and end apart: 14 -> 14, of which waited for: 14 -> 10; matrix products, arithmetic and copies ran while one was open for 0% -> 0% of each run, Pallas kernels for 0% -> 5%
where the time goes in v5:
time: 426 us; the launch traced here: 424 us
  blocking collectives  304 us (71%)
  waiting for transfers between devices  48.9 us (11%)
  Pallas kernels  40.7 us (10%)
  starting transfers between devices  22.3 us (5%)
  other arithmetic  4.65 us (1%)
    all_to_all x3, blocking collectives, body(): lax.all_to_all(outgoing, GY, split_axis=0, concat_axis=0, tiled=True)  304 us
    ppermute x6, waiting for transfers between devices, around(): return lax.ppermute(value, GY, pairs)  33.9 us
    pallas_call x2, Pallas kernels, smooth(): pl.pallas_call(smooth_kernel, in_specs=[SMEM] * 4 + [VMEM] * 3 + [ANY] *...  20.5 us
    ppermute x6, starting transfers between devices, shifted(): lax.ppermute(value, axis, [(source, source + steps) for source in range(f...  15.6 us
    pallas_call x1, Pallas kernels, galerkin(): pl.pallas_call(galerkin_kernel, in_specs=[SMEM] * 5 + [VMEM] * 2 + [ANY]...  10.8 us
  transfers between devices with their start and end apart: 14, of which 10 were waited for; matrix products, arithmetic and copies ran while one was open for 0% of the time, Pallas kernels for 5%

profile of v5, /device:TPU:0, one launch (start us, length us, event | category | flops | bytes accessed | tf_op | source)
XLA Modules:
  0.0 424.3 jit_solution(9026455254523780330)
XLA Ops:
  0.6 0.0 copy-start
  0.6 1.6 copy-done
  2.2 0.0 copy-start.7
  2.2 0.7 copy-done.7
  2.9 0.7 pick_rows.1
  3.5 3.9 collective-permute-start
  7.5 1.3 collective-permute-start.1
  8.8 0.0 copy-done.1
  8.8 0.0 copy-done.9
  8.8 0.0 slice-start
  8.8 1.8 pack_rows.1
  10.6 0.1 pad_add_fusion.here
  10.7 0.0 copy-start.6
  10.7 0.0 copy-start.8
  10.7 2.3 collective-permute-done.low_hbm
  13.0 4.3 %collective-permute-done.1.high_hbm = bf16[1,2,256,256]{3,2,1,0:T(8,128)(2,1)S(1)} collective-permute-done((bf16[1,2,256,256]{3,2,1,0:T(8,128)(2,1)S(1)}, bf16[1,2,256,256]{3,2,1,0:T(8,128)(2,1)S(1)}, u32[]{:S(2)}, u32[]{:S(2)}) %collective-permute-start.1) | collective-permute-done | bytes 262176 | tf_op jit(solution)/shard_map/ppermute | solution.py:24
  17.3 102.7 %all_to_all.15.peers_hbm = bf16[32,2,256,256]{3,2,1,0:T(8,128)(2,1)} all-to-all(bf16[32,2,256,256]{3,2,1,0:T(8,128)(2,1)S(1)} %pack_rows.1), channel_id=1, replica_groups=mesh['gx'=4,'x'=4,'y'=4,'c'=2] {'x','y','c'}, dimensions={0} | all-to-all | bytes 16777216 | tf_op jit(solution)/shard_map/all_to_all | solution.py:316
  120.0 0.0 slice-done
  120.0 0.0 slice-done.1
  120.0 0.0 copy-done.2
  120.0 0.0 copy-done.4
  120.0 0.0 copy-done.5
  120.0 0.0 copy-done.6
  120.0 0.0 copy-done.8
  120.0 3.5 slab_rows.2
  123.6 3.7 collective-permute-start.2
  127.2 1.3 collective-permute-start.3
  128.5 10.4 %smooth_rows.2 = (bf16[8,2,256,256]{3,2,1,0:T(8,128)(2,1)S(1)}, bf16[32,2,256,256]{3,2,1,0:T(8,128)(2,1)}) custom-call(s32[2,8]{1,0:T(2,128)S(1)} %bitcast.20, s32[4,8]{1,0:T(4,128)S(1)} %bitcast.15, s32[6,2,8]{2,1,0:T(2,128)S(1)} %bitcast.10, s32[1,32]{1,0:T(1,128)S(1)} %copy-done.9, bf16[8,6,256,256]{3,2,1,0:T(8,128)(2,1)S(1)} %bitcast.8, ...), custom_call_target="tpu_custom_call" | custom-call | flops 3758096384 | bytes 29360128 | tf_op jit(solution)/shard_map/smooth_rows/pallas_call | solution.py:218
  138.9 0.0 collective-permute-done.2.low_hbm
  138.9 0.0 collective-permute-done.3.high_hbm
  138.9 100.4 %all_to_all.16.peers_hbm = bf16[32,2,256,256]{3,2,1,0:T(8,128)(2,1)} all-to-all(bf16[32,2,256,256]{3,2,1,0:T(8,128)(2,1)} %get-tuple-element.57), channel_id=1, replica_groups=mesh['gx'=4,'x'=4,'y'=4,'c'=2] {'x','y','c'}, dimensions={0} | all-to-all | bytes 16777216 | tf_op jit(solution)/shard_map/all_to_all | solution.py:324
  239.3 3.5 slab_rows.3
  242.9 4.1 collective-permute-start.4
  247.0 1.3 collective-permute-start.5
  248.3 10.1 %smooth_rows.3 = (bf16[8,2,256,256]{3,2,1,0:T(8,128)(2,1)}, bf16[32,2,256,256]{3,2,1,0:T(8,128)(2,1)}) custom-call(s32[2,8]{1,0:T(2,128)S(1)} %bitcast.22, s32[4,8]{1,0:T(4,128)S(1)} %bitcast.17, s32[6,2,8]{2,1,0:T(2,128)S(1)} %bitcast.12, s32[1,32]{1,0:T(1,128)S(1)} %copy-done.9, bf16[8,6,256,256]{3,2,1,0:T(8,128)(2,1)S(1)} %bitcast.8, ...), custom_call_target="tpu_custom_call" | custom-call | flops 3758096384 | bytes 29360128 | tf_op jit(solution)/shard_map/smooth_rows/pallas_call | solution.py:218
  258.4 0.0 collective-permute-done.4.low_hbm
  258.4 0.0 collective-permute-done.5.high_hbm
  258.4 0.0 copy-start.3
  258.5 0.0 copy-start.10
  258.5 100.5 %all_to_all.17.peers_hbm = bf16[32,2,256,256]{3,2,1,0:T(8,128)(2,1)} all-to-all(bf16[32,2,256,256]{3,2,1,0:T(8,128)(2,1)} %get-tuple-element.73), channel_id=1, replica_groups=mesh['gx'=4,'x'=4,'y'=4,'c'=2] {'x','y','c'}, dimensions={0} | all-to-all | bytes 16777216 | tf_op jit(solution)/shard_map/all_to_all | solution.py:324
  359.0 0.0 copy-done.3
  359.0 0.0 copy-done.10
  359.0 10.8 %galerkin_rows.1 = (bf16[32,256,256]{2,1,0:T(8,128)(2,1)S(1)}, bf16[32,256,256]{2,1,0:T(8,128)(2,1)S(1)}) custom-call(s32[2,8]{1,0:T(2,128)S(1)} %bitcast.23, s32[4,8]{1,0:T(4,128)S(1)} %bitcast.18, s32[6,2,8]{2,1,0:T(2,128)S(1)} %bitcast.13, s32[2,2,8]{2,1,0:T(2,128)S(1)} %bitcast.24, s32[3]{0:T(128)S(1)} %pad_add_fusion.here, ...), custom_call_target="tpu_custom_call" | custom-call | tf_op jit(solution)/shard_map/galerkin_rows/pallas_call | solution.py:279
  369.8 0.2 collective-permute-start.6
  370.1 7.0 %collective-permute-done.6 = bf16[32,256,256]{2,1,0:T(8,128)(2,1)S(1)} collective-permute-done((bf16[32,256,256]{2,1,0:T(8,128)(2,1)S(1)}, bf16[32,256,256]{2,1,0:T(8,128)(2,1)S(1)}, u32[]{:S(2)}, u32[]{:S(2)}) %collective-permute-start.6) | collective-permute-done | bytes 4194336 | tf_op jit(solution)/shard_map/ppermute | solution.py:326
  377.1 1.3 add_convert_fusion.3
  378.3 1.3 collective-permute-start.9
  379.6 0.5 collective-permute-start.8
  380.1 1.0 collective-permute-start.7
  381.2 12.0 %collective-permute-done.9 = bf16[8,256,256]{2,1,0:T(8,128)(2,1)S(1)} collective-permute-done((bf16[8,256,256]{2,1,0:T(8,128)(2,1)S(1)}, bf16[8,256,256]{2,1,0:T(8,128)(2,1)S(1)}, u32[]{:S(2)}, u32[]{:S(2)}) %collective-permute-start.9) | collective-permute-done | bytes 1048608 | tf_op jit(solution)/shard_map/ppermute | solution.py:34
  393.2 2.9 collective-permute-done.8
  396.0 11.1 %collective-permute-done.7 = bf16[8,256,256]{2,1,0:T(8,128)(2,1)S(1)} collective-permute-done((bf16[8,256,256]{2,1,0:T(8,128)(2,1)S(1)}, bf16[8,256,256]{2,1,0:T(8,128)(2,1)S(1)}, u32[]{:S(2)}, u32[]{:S(2)}) %collective-permute-start.7) | collective-permute-done | bytes 1048608 | tf_op jit(solution)/shard_map/ppermute | solution.py:34
  407.2 1.0 copy-done.11
  408.1 1.2 add_convert_fusion.7
  409.3 0.0 collective-permute-start.10
  409.4 3.2 collective-permute-start.12
  412.6 0.3 collective-permute-start.11
  412.9 4.3 %collective-permute-done.10 = bf16[2,256,256]{2,1,0:T(8,128)(2,1)S(1)} collective-permute-done((bf16[2,256,256]{2,1,0:T(8,128)(2,1)}, bf16[2,256,256]{2,1,0:T(8,128)(2,1)S(1)}, u32[]{:S(2)}, u32[]{:S(2)}) %collective-permute-start.10) | collective-permute-done | bytes 262176 | tf_op jit(solution)/shard_map/ppermute | solution.py:34
  417.1 2.5 collective-permute-done.12
  419.6 1.2 collective-permute-done.11
  420.8 1.3 add_convert_fusion.4
  422.1 0.1 collective-permute-start.13
  422.2 1.3 collective-permute-done.13
  423.6 0.7 pad_maximum_fusion
  (10 shorter events, 0.1 us)
Async XLA Ops:
  0.6 1.6 copy-start
  2.2 0.7 copy-start.7
  2.9 5.9 %copy-start.1 = (bf16[8,2,256,256]{3,2,1,0:T(8,128)(2,1)S(1)}, bf16[8,2,256,256]{3,2,1,0:T(8,128)(2,1)}, u32[]{:S(2)}) copy-start(bf16[8,2,256,256]{3,2,1,0:T(8,128)(2,1)} %own.2) | copy-start | bytes 6291460
  2.9 5.9 %copy-start.9 = (s32[1,32]{1,0:T(1,128)S(1)}, s32[1,32]{1,0:T(1,128)}, u32[]{:S(2)}) copy-start(s32[1,32]{1,0:T(1,128)} %peer.5) | copy-start | bytes 388
  3.5 9.5 %collective-permute-start = (bf16[1,2,256,256]{3,2,1,0:T(8,128)(2,1)S(1)}, bf16[1,2,256,256]{3,2,1,0:T(8,128)(2,1)S(1)}, u32[]{:S(2)}, u32[]{:S(2)}) collective-permute-start(bf16[1,2,256,256]{3,2,1,0:T(8,128)(2,1)S(1)} %get-tuple-element.40), channel_id=1, source_target_pairs={{0,32},{32,64},{64,96},{1,33},{33,65},{65,97},{2,34},{34,66},{66,9... | collective-permute-start | bytes 786440 | tf_op jit(solution)/shard_map/ppermute | solution.py:24
  7.5 9.8 %collective-permute-start.1 = (bf16[1,2,256,256]{3,2,1,0:T(8,128)(2,1)S(1)}, bf16[1,2,256,256]{3,2,1,0:T(8,128)(2,1)S(1)}, u32[]{:S(2)}, u32[]{:S(2)}) collective-permute-start(bf16[1,2,256,256]{3,2,1,0:T(8,128)(2,1)S(1)} %get-tuple-element.41), channel_id=1, source_target_pairs={{32,0},{64,32},{96,64},{33,1},{65,33},{97,65},{34,2},{66,34},{98,6... | collective-permute-start | bytes 786440 | tf_op jit(solution)/shard_map/ppermute | solution.py:24
  8.8 111.2 %slice-start = ((s8[6291456]{0:T(1024)(128)(4,1)}), s8[4194304]{0:T(1024)(128)(4,1)S(1)}, s32[]{:S(2)}) async-start(s8[6291456]{0:T(1024)(128)(4,1)} %bitcast.7), calls=%async_computation.3 | async-start | bytes 8388608
  10.7 109.3 %slice-start.1 = ((s8[6291456]{0:T(1024)(128)(4,1)}), s8[2097152]{0:T(1024)(128)(4,1)S(1)}, s32[]{:S(2)}) async-start(s8[6291456]{0:T(1024)(128)(4,1)} %bitcast.7), calls=%async_computation.4 | async-start | bytes 4194304
  10.7 109.3 %copy-start.2 = (bf16[8,256,256]{2,1,0:T(8,128)(2,1)S(1)}, bf16[8,256,256]{2,1,0:T(8,128)(2,1)}, u32[]{:S(2)}) copy-start(bf16[8,256,256]{2,1,0:T(8,128)(2,1)} %d_buf.5) | copy-start | bytes 3145732
  10.7 109.3 %copy-start.4 = (s32[8,6,2]{0,2,1:T(2,128)S(1)}, s32[8,6,2]{0,2,1:T(2,128)}, u32[]{:S(2)}) copy-start(s32[8,6,2]{0,2,1:T(2,128)} %param.12) | copy-start | bytes 1156
  10.7 109.3 %copy-start.5 = (s32[8,4]{0,1:T(4,128)S(1)}, s32[8,4]{0,1:T(4,128)}, u32[]{:S(2)}) copy-start(s32[8,4]{0,1:T(4,128)} %param.11) | copy-start | bytes 388
  10.7 109.3 %copy-start.6 = (s32[8,2]{0,1:T(2,128)S(1)}, s32[8,2]{0,1:T(2,128)}, u32[]{:S(2)}) copy-start(s32[8,2]{0,1:T(2,128)} %param.10) | copy-start | bytes 196
  10.7 109.3 %copy-start.8 = (s32[1,2]{1,0:T(1,128)S(1)}, s32[1,2]{1,0:T(1,128)}, u32[]{:S(2)}) copy-start(s32[1,2]{1,0:T(1,128)} %slab.5) | copy-start | bytes 28
  123.6 15.3 %collective-permute-start.2 = (bf16[1,2,256,256]{3,2,1,0:T(8,128)(2,1)S(1)}, bf16[1,2,256,256]{3,2,1,0:T(8,128)(2,1)S(1)}, u32[]{:S(2)}, u32[]{:S(2)}) collective-permute-start(bf16[1,2,256,256]{3,2,1,0:T(8,128)(2,1)S(1)} %get-tuple-element.55), channel_id=1, source_target_pairs={{0,32},{32,64},{64,96},{1,33},{33,65},{65,97},{2,34},{34,66},{66,9... | collective-permute-start | bytes 786440 | tf_op jit(solution)/shard_map/ppermute | solution.py:24
  127.2 11.7 %collective-permute-start.3 = (bf16[1,2,256,256]{3,2,1,0:T(8,128)(2,1)S(1)}, bf16[1,2,256,256]{3,2,1,0:T(8,128)(2,1)S(1)}, u32[]{:S(2)}, u32[]{:S(2)}) collective-permute-start(bf16[1,2,256,256]{3,2,1,0:T(8,128)(2,1)S(1)} %get-tuple-element.56), channel_id=1, source_target_pairs={{32,0},{64,32},{96,64},{33,1},{65,33},{97,65},{34,2},{66,34},{98,6... | collective-permute-start | bytes 786440 | tf_op jit(solution)/shard_map/ppermute | solution.py:24
  242.9 15.6 %collective-permute-start.4 = (bf16[1,2,256,256]{3,2,1,0:T(8,128)(2,1)S(1)}, bf16[1,2,256,256]{3,2,1,0:T(8,128)(2,1)S(1)}, u32[]{:S(2)}, u32[]{:S(2)}) collective-permute-start(bf16[1,2,256,256]{3,2,1,0:T(8,128)(2,1)S(1)} %get-tuple-element.71), channel_id=1, source_target_pairs={{0,32},{32,64},{64,96},{1,33},{33,65},{65,97},{2,34},{34,66},{66,9... | collective-permute-start | bytes 786440 | tf_op jit(solution)/shard_map/ppermute | solution.py:24
  247.0 11.5 %collective-permute-start.5 = (bf16[1,2,256,256]{3,2,1,0:T(8,128)(2,1)S(1)}, bf16[1,2,256,256]{3,2,1,0:T(8,128)(2,1)S(1)}, u32[]{:S(2)}, u32[]{:S(2)}) collective-permute-start(bf16[1,2,256,256]{3,2,1,0:T(8,128)(2,1)S(1)} %get-tuple-element.72), channel_id=1, source_target_pairs={{32,0},{64,32},{96,64},{33,1},{65,33},{97,65},{34,2},{66,34},{98,6... | collective-permute-start | bytes 786440 | tf_op jit(solution)/shard_map/ppermute | solution.py:24
  258.4 100.6 %copy-start.3 = (bf16[8,2,256,256]{3,2,1,0:T(8,128)(2,1)S(1)}, bf16[8,2,256,256]{3,2,1,0:T(8,128)(2,1)}, u32[]{:S(2)}) copy-start(bf16[8,2,256,256]{3,2,1,0:T(8,128)(2,1)} %get-tuple-element.38.own) | copy-start | bytes 6291460
  258.5 100.6 %copy-start.10 = (s32[8,2,2]{0,2,1:T(2,128)S(1)}, s32[8,2,2]{0,2,1:T(2,128)}, u32[]{:S(2)}) copy-start(s32[8,2,2]{0,2,1:T(2,128)} %param.17) | copy-start | bytes 388
  369.8 7.2 %collective-permute-start.6 = (bf16[32,256,256]{2,1,0:T(8,128)(2,1)S(1)}, bf16[32,256,256]{2,1,0:T(8,128)(2,1)S(1)}, u32[]{:S(2)}, u32[]{:S(2)}) collective-permute-start(bf16[32,256,256]{2,1,0:T(8,128)(2,1)S(1)} %get-tuple-element.77), channel_id=1, source_target_pairs={{0,1},{1,0},{2,3},{3,2},{4,5},{5,4},{6,7},{7,6},{8,9},{9,8},{10,11... | collective-permute-start | bytes 12582920 | tf_op jit(solution)/shard_map/ppermute | solution.py:326
  378.3 14.9 %collective-permute-start.9 = (bf16[8,256,256]{2,1,0:T(8,128)(2,1)S(1)}, bf16[8,256,256]{2,1,0:T(8,128)(2,1)S(1)}, u32[]{:S(2)}, u32[]{:S(2)}) collective-permute-start(bf16[8,256,256]{2,1,0:T(8,128)(2,1)S(1)} %get-tuple-element.79), channel_id=1, source_target_pairs={{0,24},{1,7},{2,26},{3,1},{4,28},{5,3},{6,30},{7,5},{8,0},{9,15},{... | collective-permute-start | bytes 3145736 | tf_op jit(solution)/shard_map/ppermute | solution.py:34
  379.6 16.4 %collective-permute-start.8 = (bf16[8,256,256]{2,1,0:T(8,128)(2,1)S(1)}, bf16[8,256,256]{2,1,0:T(8,128)(2,1)S(1)}, u32[]{:S(2)}, u32[]{:S(2)}) collective-permute-start(bf16[8,256,256]{2,1,0:T(8,128)(2,1)S(1)} %get-tuple-element.80), channel_id=1, source_target_pairs={{0,16},{1,5},{2,18},{3,7},{4,20},{5,1},{6,22},{7,3},{8,24},{9,13},... | collective-permute-start | bytes 3145736 | tf_op jit(solution)/shard_map/ppermute | solution.py:34
  380.1 27.0 %collective-permute-start.7 = (bf16[8,256,256]{2,1,0:T(8,128)(2,1)S(1)}, bf16[8,256,256]{2,1,0:T(8,128)(2,1)S(1)}, u32[]{:S(2)}, u32[]{:S(2)}) collective-permute-start(bf16[8,256,256]{2,1,0:T(8,128)(2,1)S(1)} %get-tuple-element.81), channel_id=1, source_target_pairs={{0,8},{1,3},{2,10},{3,5},{4,12},{5,7},{6,14},{7,1},{8,16},{9,11},{... | collective-permute-start | bytes 3145736 | tf_op jit(solution)/shard_map/ppermute | solution.py:34
  407.2 1.0 copy-start.11
  409.3 7.8 %collective-permute-start.10 = (bf16[2,256,256]{2,1,0:T(8,128)(2,1)}, bf16[2,256,256]{2,1,0:T(8,128)(2,1)S(1)}, u32[]{:S(2)}, u32[]{:S(2)}) collective-permute-start(bf16[2,256,256]{2,1,0:T(8,128)(2,1)} %get-tuple-element.82), channel_id=1, source_target_pairs={{0,2},{1,9},{2,4},{3,11},{4,6},{5,13},{6,0},{7,15},{8,10},{9,17},{... | collective-permute-start | bytes 786440 | tf_op jit(solution)/shard_map/ppermute | solution.py:34
  409.4 10.2 %collective-permute-start.12 = (bf16[2,256,256]{2,1,0:T(8,128)(2,1)}, bf16[2,256,256]{2,1,0:T(8,128)(2,1)}, u32[]{:S(2)}, u32[]{:S(2)}) collective-permute-start(bf16[2,256,256]{2,1,0:T(8,128)(2,1)} %get-tuple-element.83), channel_id=1, source_target_pairs={{0,6},{1,25},{2,0},{3,27},{4,2},{5,29},{6,4},{7,31},{8,14},{9,1},{... | collective-permute-start | bytes 786440 | tf_op jit(solution)/shard_map/ppermute | solution.py:34
  412.6 8.2 %collective-permute-start.11 = (bf16[2,256,256]{2,1,0:T(8,128)(2,1)}, bf16[2,256,256]{2,1,0:T(8,128)(2,1)}, u32[]{:S(2)}, u32[]{:S(2)}) collective-permute-start(bf16[2,256,256]{2,1,0:T(8,128)(2,1)} %get-tuple-element.84), channel_id=1, source_target_pairs={{0,4},{1,17},{2,6},{3,19},{4,0},{5,21},{6,2},{7,23},{8,12},{9,25},... | collective-permute-start | bytes 786440 | tf_op jit(solution)/shard_map/ppermute | solution.py:34
  422.1 1.4 collective-permute-start.13

commit v6 on v5

--- a/solution.py
+++ b/solution.py
@@ -94,27 +94,40 @@
     )(peer, rows)
 
 
-def start_row(remote, i, slot, peers_hbm, low_hbm, high_hbm, far, sems, first, count):
+def wanted_blocks(match, i, k):
+    for m in range(BLOCKS):
+        needed = match[LOCAL + k, 0, i] == m
+        for n in range(1, BLOCKS):
+            needed = needed | (match[LOCAL + k, n, i] == m)
+        yield m, needed
+
+
+def start_row(remote, match, i, slot, peers_hbm, low_hbm, high_hbm, far, sems, first, count):
     for k in range(LINKS - LOCAL):
         column = remote[k, i]
-        place = (far.at[slot, k], sems.at[slot, k])
-
-        @pl.when(column < first + count)
-        def _():
-            pltpu.make_async_copy(peers_hbm.at[jnp.maximum(column - first, 0)], *place).start()
-
-        @pl.when(column == first + count)
-        def _():
-            pltpu.make_async_copy(low_hbm.at[0], *place).start()
-
-        @pl.when(column > first + count)
-        def _():
-            pltpu.make_async_copy(high_hbm.at[0], *place).start()
-
-
-def wait_row(i, peers_hbm, far, sems):
+        for m, needed in wanted_blocks(match, i, k):
+            place = (far.at[slot, k, m], sems.at[slot, k, m])
+
+            @pl.when(needed & (column < first + count))
+            def _():
+                pltpu.make_async_copy(peers_hbm.at[jnp.maximum(column - first, 0), m], *place).start()
+
+            @pl.when(needed & (column == first + count))
+            def _():
+                pltpu.make_async_copy(low_hbm.at[0, m], *place).start()
+
+            @pl.when(needed & (column > first + count))
+            def _():
+                pltpu.make_async_copy(high_hbm.at[0, m], *place).start()
+
+
+def wait_row(match, i, slot, peers_hbm, far, sems):
     for k in range(LINKS - LOCAL):
-        pltpu.make_async_copy(peers_hbm.at[0], far.at[i, k], sems.at[i, k]).wait()
+        for m, needed in wanted_blocks(match, i, k):
+
+            @pl.when(needed)
+            def _():
+                pltpu.make_async_copy(peers_hbm.at[0, m], far.at[slot, k, m], sems.at[slot, k, m]).wait()
 
 
 def row_image(local, match, i, slot, a_buf, own, far, rhs):
@@ -150,9 +163,9 @@
 ):
     arrays = (peers_hbm, low_hbm, high_hbm, far, sems, own.shape[0], peers_hbm.shape[0])
     for j in range(2):
-        start_row(remote, slab[0, j], j, *arrays)
+        start_row(remote, match, slab[0, j], j, *arrays)
     for j, out in enumerate((up, down)):
-        wait_row(j, peers_hbm, far, sems)
+        wait_row(match, slab[0, j], j, peers_hbm, far, sems)
         for n, value in enumerate(new_row(local, match, slab[0, j], j, a_buf, d_buf, own, far, rhs)):
             out[0, n] = value
 
@@ -170,11 +183,11 @@
 
     @pl.loop(0, count)
     def _(i):
-        start_row(remote, i, i, *arrays)
+        start_row(remote, match, i, i, *arrays)
 
     @pl.loop(0, count)
     def _(i):
-        wait_row(i, peers_hbm, far, sems)
+        wait_row(match, i, i, peers_hbm, far, sems)
         for n, value in enumerate(new_row(local, match, i, i, a_buf, d_buf, own, far, rhs)):
             new[i, n] = value
         pltpu.make_async_copy(new.at[i], rows_hbm.at[i], rows_sem.at[0]).start()
@@ -192,7 +205,7 @@
     return [
         pltpu.VMEM((count, LINKS - LOCAL, BLOCKS, width, width), jnp.bfloat16),
         pltpu.VMEM((LINKS * width, BLOCKS * width), jnp.bfloat16),
-        pltpu.SemaphoreType.DMA((count, LINKS - LOCAL)),
+        pltpu.SemaphoreType.DMA((count, LINKS - LOCAL, BLOCKS)),
         pltpu.SemaphoreType.DMA((1,)),
     ]
 
@@ -230,24 +243,24 @@
 def galerkin_kernel(
     local, remote, match, slots, here,
     a_buf, own, peers_hbm, low_hbm, high_hbm,
-    keep, swap,
-    far, rhs,
-    sems,
+    *refs,
 ):
+    keeps, swaps = refs[:RING], refs[RING : 2 * RING]
+    far, rhs, sems = refs[2 * RING :]
     count, width = own.shape[0], own.shape[-1]
     peers = peers_hbm.shape[0]
     arrays = (peers_hbm, low_hbm, high_hbm, far, sems, count, peers)
 
     @pl.loop(0, count)
     def _(i):
-        start_row(remote, i, i, *arrays)
-
-    keep[...] = jnp.zeros_like(keep)
-    swap[...] = jnp.zeros_like(swap)
+        start_row(remote, match, i, i, *arrays)
+
+    for out in keeps + swaps:
+        out[...] = jnp.zeros_like(out)
 
     @pl.loop(0, count)
     def _(i):
-        wait_row(i, peers_hbm, far, sems)
+        wait_row(match, i, i, peers_hbm, far, sems)
         image = row_image(local, match, i, i, a_buf, own, far, rhs)
         mine = jnp.concatenate([own[i, n] for n in range(BLOCKS)], axis=1)
         partial = lax.dot_general(mine, image, (((0,), (0,)), ((), ())), preferred_element_type=jnp.float32)
@@ -261,26 +274,27 @@
                 dx = (chip // RING - here[0] + RING) % RING
                 dy = (chip % RING - here[1] + RING) % RING
                 second = slot % 2
-                place = jnp.where(second == 0, dx * RING + dy, dy * RING + dx) * 2 + owner % 2
-
-                @pl.when(second == here[2])
-                def _():
-                    keep[place] = block
-
-                @pl.when(second != here[2])
-                def _():
-                    swap[place] = block
+                step = jnp.where(second == 0, dx, dy)
+                place = jnp.where(second == 0, dy, dx) * 2 + owner % 2
+                for j in range(RING):
+
+                    @pl.when((second == here[2]) & (step == j))
+                    def _():
+                        keeps[j][place] = block
+
+                    @pl.when((second != here[2]) & (step == j))
+                    def _():
+                        swaps[j][place] = block
 
 
 def galerkin(tables, slots, here, operator, rows, received, low, high):
     count, _, width, _ = operator.shape
-    half = RING * RING * BLOCKS
     far, rhs, sems, single = row_scratch(count, width)
     return pl.pallas_call(
         galerkin_kernel,
         in_specs=[SMEM] * 5 + [VMEM] * 2 + [ANY] * 3,
-        out_specs=[VMEM] * 2,
-        out_shape=(shape(half, width, width), shape(half, width, width)),
+        out_specs=[VMEM] * (2 * RING),
+        out_shape=[shape(2 * RING, width, width)] * (2 * RING),
         scratch_shapes=[far, rhs, sems],
         compiler_params=pltpu.CompilerParams(vmem_limit_bytes=30 << 20),
         name="galerkin_rows",
@@ -322,10 +336,10 @@
         rows, outgoing = smooth(tables, peer, *operands)
         outgoing, low, high = lax.optimization_barrier((outgoing, low, high))
         received = lax.all_to_all(outgoing, GY, split_axis=0, concat_axis=0, tiled=True)
-    keep, swap = galerkin(tables, slots, here, operator_blocks, rows, received, low, high)
-    other = lax.ppermute(swap, "c", [(0, 1), (1, 0)])
-    group = keep.shape[0] // RING
-    parts = [add((keep[group * j : group * j + group], other[group * j : group * j + group])) for j in range(RING)]
+    parts = galerkin(tables, slots, here, operator_blocks, rows, received, low, high)
+    keeps, swaps = parts[:RING], parts[RING:]
+    others = [lax.ppermute(swap, "c", [(0, 1), (1, 0)]) for swap in swaps]
+    parts = [add(pair) for pair in zip(keeps, others)]
     for swapped in range(2):
         terms = [parts[0], *[around(parts[s], s, swapped) for s in range(1, RING)]]
         group = max(terms[0].shape[0] // RING, 2)

time: 426 us -> 427 us (level)
  waiting for transfers between devices: 48.9 us -> 42 us
  Pallas kernels: 40.7 us -> 46.3 us
    ppermute x1 -> x4, waiting for transfers between devices: 7 us -> 2.59 us  [body(): others = [lax.ppermute(swap, 'c', [(0, 1), (1, 0)]) for swap in swaps]]
  transfers between devices with their start and end apart: 14 -> 17, of which waited for: 10 -> 11; matrix products, arithmetic and copies ran while one was open for 0% -> 0% of each run, Pallas kernels for 5% -> 6%
where the time goes in v6:
time: 427 us; the launch traced here: 425 us
  blocking collectives  304 us (71%)
  Pallas kernels  46.3 us (11%)
  waiting for transfers between devices  42 us (10%)
  starting transfers between devices  24.6 us (6%)
  other arithmetic  4.53 us (1%)
    all_to_all x3, blocking collectives, body(): lax.all_to_all(outgoing, GY, split_axis=0, concat_axis=0, tiled=True)  304 us
    ppermute x6, waiting for transfers between devices, around(): return lax.ppermute(value, GY, pairs)  31.4 us
    pallas_call x2, Pallas kernels, smooth(): pl.pallas_call(smooth_kernel, in_specs=[SMEM] * 4 + [VMEM] * 3 + [ANY] *...  22.3 us
    ppermute x6, starting transfers between devices, shifted(): lax.ppermute(value, axis, [(source, source + steps) for source in range(f...  16.5 us
    pallas_call x1, Pallas kernels, galerkin(): pl.pallas_call(galerkin_kernel, in_specs=[SMEM] * 5 + [VMEM] * 2 + [ANY]...  14.4 us
  transfers between devices with their start and end apart: 17, of which 11 were waited for; matrix products, arithmetic and copies ran while one was open for 0% of the time, Pallas kernels for 6%

profile of v6, /device:TPU:0, one launch (start us, length us, event | category | flops | bytes accessed | tf_op | source)
XLA Modules:
  0.0 425.3 jit_solution(18067291346417402367)
XLA Ops:
  0.6 0.0 copy-start
  0.6 1.6 copy-done
  2.2 0.7 copy-done.7
  2.9 0.7 pick_rows.1
  3.5 3.9 collective-permute-start
  7.5 1.3 collective-permute-start.1
  8.8 0.0 copy-done.1
  8.8 0.0 slice-start
  8.8 1.8 pack_rows.1
  10.6 0.1 pad_add_fusion.here
  10.7 0.0 copy-start.6
  10.7 0.0 copy-start.8
  10.7 2.3 collective-permute-done.low_hbm
  13.0 4.3 %collective-permute-done.1.high_hbm = bf16[1,2,256,256]{3,2,1,0:T(8,128)(2,1)S(1)} collective-permute-done((bf16[1,2,256,256]{3,2,1,0:T(8,128)(2,1)S(1)}, bf16[1,2,256,256]{3,2,1,0:T(8,128)(2,1)S(1)}, u32[]{:S(2)}, u32[]{:S(2)}) %collective-permute-start.1) | collective-permute-done | bytes 262176 | tf_op jit(solution)/shard_map/ppermute | solution.py:24
  17.3 102.7 %all_to_all.15.peers_hbm = bf16[32,2,256,256]{3,2,1,0:T(8,128)(2,1)} all-to-all(bf16[32,2,256,256]{3,2,1,0:T(8,128)(2,1)S(1)} %pack_rows.1), channel_id=1, replica_groups=mesh['gx'=4,'x'=4,'y'=4,'c'=2] {'x','y','c'}, dimensions={0} | all-to-all | bytes 16777216 | tf_op jit(solution)/shard_map/all_to_all | solution.py:330
  120.0 0.0 slice-done.1
  120.0 3.6 slab_rows.2
  123.6 3.7 collective-permute-start.2
  127.3 1.3 collective-permute-start.3
  128.6 11.3 %smooth_rows.2 = (bf16[8,2,256,256]{3,2,1,0:T(8,128)(2,1)S(1)}, bf16[32,2,256,256]{3,2,1,0:T(8,128)(2,1)}) custom-call(s32[2,8]{1,0:T(2,128)S(1)} %bitcast.20, s32[4,8]{1,0:T(4,128)S(1)} %bitcast.15, s32[6,2,8]{2,1,0:T(2,128)S(1)} %bitcast.10, s32[1,32]{1,0:T(1,128)S(1)} %copy-done.9, bf16[8,6,256,256]{3,2,1,0:T(8,128)(2,1)S(1)} %bitcast.8, ...), custom_call_target="tpu_custom_call" | custom-call | flops 3758096384 | bytes 29360128 | tf_op jit(solution)/shard_map/smooth_rows/pallas_call | solution.py:231
  139.9 0.0 collective-permute-done.2.low_hbm
  139.9 0.0 collective-permute-done.3.high_hbm
  139.9 100.4 %all_to_all.16.peers_hbm = bf16[32,2,256,256]{3,2,1,0:T(8,128)(2,1)} all-to-all(bf16[32,2,256,256]{3,2,1,0:T(8,128)(2,1)} %get-tuple-element.63), channel_id=1, replica_groups=mesh['gx'=4,'x'=4,'y'=4,'c'=2] {'x','y','c'}, dimensions={0} | all-to-all | bytes 16777216 | tf_op jit(solution)/shard_map/all_to_all | solution.py:338
  240.4 3.6 slab_rows.3
  243.9 5.0 %collective-permute-start.4 = (bf16[1,2,256,256]{3,2,1,0:T(8,128)(2,1)S(1)}, bf16[1,2,256,256]{3,2,1,0:T(8,128)(2,1)S(1)}, u32[]{:S(2)}, u32[]{:S(2)}) collective-permute-start(bf16[1,2,256,256]{3,2,1,0:T(8,128)(2,1)S(1)} %get-tuple-element.77), channel_id=1, source_target_pairs={{0,32},{32,64},{64,96},{1,33},{33,65},{65,97},{2,34},{34,66},{66,9... | collective-permute-start | bytes 786440 | tf_op jit(solution)/shard_map/ppermute | solution.py:24
  248.9 1.3 collective-permute-start.5
  250.2 11.1 %smooth_rows.3 = (bf16[8,2,256,256]{3,2,1,0:T(8,128)(2,1)}, bf16[32,2,256,256]{3,2,1,0:T(8,128)(2,1)}) custom-call(s32[2,8]{1,0:T(2,128)S(1)} %bitcast.22, s32[4,8]{1,0:T(4,128)S(1)} %bitcast.17, s32[6,2,8]{2,1,0:T(2,128)S(1)} %bitcast.12, s32[1,32]{1,0:T(1,128)S(1)} %copy-done.9, bf16[8,6,256,256]{3,2,1,0:T(8,128)(2,1)S(1)} %bitcast.8, ...), custom_call_target="tpu_custom_call" | custom-call | flops 3758096384 | bytes 29360128 | tf_op jit(solution)/shard_map/smooth_rows/pallas_call | solution.py:231
  261.3 0.0 collective-permute-done.4.low_hbm
  261.3 0.0 collective-permute-done.5.high_hbm
  261.3 0.0 copy-start.3
  261.3 0.0 copy-start.10
  261.3 100.6 %all_to_all.17.peers_hbm = bf16[32,2,256,256]{3,2,1,0:T(8,128)(2,1)} all-to-all(bf16[32,2,256,256]{3,2,1,0:T(8,128)(2,1)} %get-tuple-element.79), channel_id=1, replica_groups=mesh['gx'=4,'x'=4,'y'=4,'c'=2] {'x','y','c'}, dimensions={0} | all-to-all | bytes 16777216 | tf_op jit(solution)/shard_map/all_to_all | solution.py:338
  361.9 0.0 copy-done.10
  361.9 14.4 %galerkin_rows.1 = (bf16[8,256,256]{2,1,0:T(8,128)(2,1)S(1)}, bf16[8,256,256]{2,1,0:T(8,128)(2,1)S(1)}, bf16[8,256,256]{2,1,0:T(8,128)(2,1)S(1)}, bf16[8,256,256...) custom-call(s32[2,8]{1,0:T(2,128)S(1)} %bitcast.23, ...), custom_call_target="tpu_custom_call" | custom-call | tf_op jit(solution)/shard_map/galerkin_rows/pallas_call | solution.py:293
  376.3 0.1 collective-permute-start.7
  376.4 0.5 collective-permute-start.9
  376.9 0.1 collective-permute-start.11
  377.0 0.4 collective-permute-start.6
  377.4 1.6 collective-permute-done.7
  379.1 0.3 add_convert_fusion.2
  379.3 0.3 collective-permute-start.8
  379.6 0.9 collective-permute-done.9
  380.6 0.3 add_convert_fusion.1
  380.8 2.4 collective-permute-start.10
  383.2 0.0 collective-permute-done.11
  383.3 0.3 add_convert_fusion
  383.5 0.7 collective-permute-start.12
  384.2 0.0 collective-permute-done.6
  384.2 0.3 add_convert_fusion.3
  384.5 11.1 %collective-permute-done.8 = bf16[8,256,256]{2,1,0:T(8,128)(2,1)S(1)} collective-permute-done((bf16[8,256,256]{2,1,0:T(8,128)(2,1)S(1)}, bf16[8,256,256]{2,1,0:T(8,128)(2,1)S(1)}, u32[]{:S(2)}, u32[]{:S(2)}) %collective-permute-start.8) | collective-permute-done | bytes 1048608 | tf_op jit(solution)/shard_map/ppermute | solution.py:34
  395.6 11.3 %collective-permute-done.10 = bf16[8,256,256]{2,1,0:T(8,128)(2,1)S(1)} collective-permute-done((bf16[8,256,256]{2,1,0:T(8,128)(2,1)S(1)}, bf16[8,256,256]{2,1,0:T(8,128)(2,1)S(1)}, u32[]{:S(2)}, u32[]{:S(2)}) %collective-permute-start.10) | collective-permute-done | bytes 1048608 | tf_op jit(solution)/shard_map/ppermute | solution.py:34
  406.9 1.2 collective-permute-done.12
  408.1 1.0 copy-done.11
  409.1 1.2 add_convert_fusion.7
  410.3 0.0 collective-permute-start.13
  410.3 3.2 collective-permute-start.15
  413.5 0.3 collective-permute-start.14
  413.8 4.2 collective-permute-done.13
  418.1 2.5 collective-permute-done.15
  420.5 1.2 collective-permute-done.14
  421.7 1.3 add_convert_fusion.4
  423.1 0.1 collective-permute-start.16
  423.2 1.3 collective-permute-done.16
  424.5 0.7 pad_maximum_fusion
  (19 shorter events, 0.1 us)
Async XLA Ops:
  0.6 1.6 copy-start
  2.2 0.7 copy-start.7
  2.9 5.9 %copy-start.1 = (bf16[8,2,256,256]{3,2,1,0:T(8,128)(2,1)S(1)}, bf16[8,2,256,256]{3,2,1,0:T(8,128)(2,1)}, u32[]{:S(2)}) copy-start(bf16[8,2,256,256]{3,2,1,0:T(8,128)(2,1)} %own.2) | copy-start | bytes 6291460
  2.9 5.9 %copy-start.9 = (s32[1,32]{1,0:T(1,128)S(1)}, s32[1,32]{1,0:T(1,128)}, u32[]{:S(2)}) copy-start(s32[1,32]{1,0:T(1,128)} %peer.5) | copy-start | bytes 388
  3.5 9.5 %collective-permute-start = (bf16[1,2,256,256]{3,2,1,0:T(8,128)(2,1)S(1)}, bf16[1,2,256,256]{3,2,1,0:T(8,128)(2,1)S(1)}, u32[]{:S(2)}, u32[]{:S(2)}) collective-permute-start(bf16[1,2,256,256]{3,2,1,0:T(8,128)(2,1)S(1)} %get-tuple-element.46), channel_id=1, source_target_pairs={{0,32},{32,64},{64,96},{1,33},{33,65},{65,97},{2,34},{34,66},{66,9... | collective-permute-start | bytes 786440 | tf_op jit(solution)/shard_map/ppermute | solution.py:24
  7.5 9.8 %collective-permute-start.1 = (bf16[1,2,256,256]{3,2,1,0:T(8,128)(2,1)S(1)}, bf16[1,2,256,256]{3,2,1,0:T(8,128)(2,1)S(1)}, u32[]{:S(2)}, u32[]{:S(2)}) collective-permute-start(bf16[1,2,256,256]{3,2,1,0:T(8,128)(2,1)S(1)} %get-tuple-element.47), channel_id=1, source_target_pairs={{32,0},{64,32},{96,64},{33,1},{65,33},{97,65},{34,2},{66,34},{98,6... | collective-permute-start | bytes 786440 | tf_op jit(solution)/shard_map/ppermute | solution.py:24
  8.8 111.2 %slice-start = ((s8[6291456]{0:T(1024)(128)(4,1)}), s8[4194304]{0:T(1024)(128)(4,1)S(1)}, s32[]{:S(2)}) async-start(s8[6291456]{0:T(1024)(128)(4,1)} %bitcast.7), calls=%async_computation.3 | async-start | bytes 8388608
  10.7 109.3 %slice-start.1 = ((s8[6291456]{0:T(1024)(128)(4,1)}), s8[2097152]{0:T(1024)(128)(4,1)S(1)}, s32[]{:S(2)}) async-start(s8[6291456]{0:T(1024)(128)(4,1)} %bitcast.7), calls=%async_computation.4 | async-start | bytes 4194304
  10.7 109.3 %copy-start.2 = (bf16[8,256,256]{2,1,0:T(8,128)(2,1)S(1)}, bf16[8,256,256]{2,1,0:T(8,128)(2,1)}, u32[]{:S(2)}) copy-start(bf16[8,256,256]{2,1,0:T(8,128)(2,1)} %d_buf.5) | copy-start | bytes 3145732
  10.7 109.3 %copy-start.4 = (s32[8,6,2]{0,2,1:T(2,128)S(1)}, s32[8,6,2]{0,2,1:T(2,128)}, u32[]{:S(2)}) copy-start(s32[8,6,2]{0,2,1:T(2,128)} %param.12) | copy-start | bytes 1156
  10.7 109.3 %copy-start.5 = (s32[8,4]{0,1:T(4,128)S(1)}, s32[8,4]{0,1:T(4,128)}, u32[]{:S(2)}) copy-start(s32[8,4]{0,1:T(4,128)} %param.11) | copy-start | bytes 388
  10.7 109.3 %copy-start.6 = (s32[8,2]{0,1:T(2,128)S(1)}, s32[8,2]{0,1:T(2,128)}, u32[]{:S(2)}) copy-start(s32[8,2]{0,1:T(2,128)} %param.10) | copy-start | bytes 196
  10.7 109.3 %copy-start.8 = (s32[1,2]{1,0:T(1,128)S(1)}, s32[1,2]{1,0:T(1,128)}, u32[]{:S(2)}) copy-start(s32[1,2]{1,0:T(1,128)} %slab.5) | copy-start | bytes 28
  123.6 16.3 %collective-permute-start.2 = (bf16[1,2,256,256]{3,2,1,0:T(8,128)(2,1)S(1)}, bf16[1,2,256,256]{3,2,1,0:T(8,128)(2,1)S(1)}, u32[]{:S(2)}, u32[]{:S(2)}) collective-permute-start(bf16[1,2,256,256]{3,2,1,0:T(8,128)(2,1)S(1)} %get-tuple-element.61), channel_id=1, source_target_pairs={{0,32},{32,64},{64,96},{1,33},{33,65},{65,97},{2,34},{34,66},{66,9... | collective-permute-start | bytes 786440 | tf_op jit(solution)/shard_map/ppermute | solution.py:24
  127.3 12.6 %collective-permute-start.3 = (bf16[1,2,256,256]{3,2,1,0:T(8,128)(2,1)S(1)}, bf16[1,2,256,256]{3,2,1,0:T(8,128)(2,1)S(1)}, u32[]{:S(2)}, u32[]{:S(2)}) collective-permute-start(bf16[1,2,256,256]{3,2,1,0:T(8,128)(2,1)S(1)} %get-tuple-element.62), channel_id=1, source_target_pairs={{32,0},{64,32},{96,64},{33,1},{65,33},{97,65},{34,2},{66,34},{98,6... | collective-permute-start | bytes 786440 | tf_op jit(solution)/shard_map/ppermute | solution.py:24
  243.9 17.3 %collective-permute-start.4 = (bf16[1,2,256,256]{3,2,1,0:T(8,128)(2,1)S(1)}, bf16[1,2,256,256]{3,2,1,0:T(8,128)(2,1)S(1)}, u32[]{:S(2)}, u32[]{:S(2)}) collective-permute-start(bf16[1,2,256,256]{3,2,1,0:T(8,128)(2,1)S(1)} %get-tuple-element.77), channel_id=1, source_target_pairs={{0,32},{32,64},{64,96},{1,33},{33,65},{65,97},{2,34},{34,66},{66,9... | collective-permute-start | bytes 786440 | tf_op jit(solution)/shard_map/ppermute | solution.py:24
  248.9 12.4 %collective-permute-start.5 = (bf16[1,2,256,256]{3,2,1,0:T(8,128)(2,1)S(1)}, bf16[1,2,256,256]{3,2,1,0:T(8,128)(2,1)S(1)}, u32[]{:S(2)}, u32[]{:S(2)}) collective-permute-start(bf16[1,2,256,256]{3,2,1,0:T(8,128)(2,1)S(1)} %get-tuple-element.78), channel_id=1, source_target_pairs={{32,0},{64,32},{96,64},{33,1},{65,33},{97,65},{34,2},{66,34},{98,6... | collective-permute-start | bytes 786440 | tf_op jit(solution)/shard_map/ppermute | solution.py:24
  261.3 100.6 %copy-start.3 = (bf16[8,2,256,256]{3,2,1,0:T(8,128)(2,1)S(1)}, bf16[8,2,256,256]{3,2,1,0:T(8,128)(2,1)}, u32[]{:S(2)}) copy-start(bf16[8,2,256,256]{3,2,1,0:T(8,128)(2,1)} %get-tuple-element.44.own) | copy-start | bytes 6291460
  261.3 100.6 %copy-start.10 = (s32[8,2,2]{0,2,1:T(2,128)S(1)}, s32[8,2,2]{0,2,1:T(2,128)}, u32[]{:S(2)}) copy-start(s32[8,2,2]{0,2,1:T(2,128)} %param.17) | copy-start | bytes 388
  376.3 2.7 collective-permute-start.7
  376.4 4.1 collective-permute-start.9
  376.9 6.4 %collective-permute-start.11 = (bf16[8,256,256]{2,1,0:T(8,128)(2,1)S(1)}, bf16[8,256,256]{2,1,0:T(8,128)(2,1)S(1)}, u32[]{:S(2)}, u32[]{:S(2)}) collective-permute-start(bf16[8,256,256]{2,1,0:T(8,128)(2,1)S(1)} %get-tuple-element.89), channel_id=1, source_target_pairs={{0,1},{1,0},{2,3},{3,2},{4,5},{5,4},{6,7},{7,6},{8,9},{9,8},{10,11... | collective-permute-start | bytes 3145736 | tf_op jit(solution)/shard_map/ppermute | solution.py:341
  377.0 7.2 %collective-permute-start.6 = (bf16[8,256,256]{2,1,0:T(8,128)(2,1)S(1)}, bf16[8,256,256]{2,1,0:T(8,128)(2,1)S(1)}, u32[]{:S(2)}, u32[]{:S(2)}) collective-permute-start(bf16[8,256,256]{2,1,0:T(8,128)(2,1)S(1)} %get-tuple-element.83), channel_id=1, source_target_pairs={{0,1},{1,0},{2,3},{3,2},{4,5},{5,4},{6,7},{7,6},{8,9},{9,8},{10,11... | collective-permute-start | bytes 3145736 | tf_op jit(solution)/shard_map/ppermute | solution.py:341
  379.3 16.3 %collective-permute-start.8 = (bf16[8,256,256]{2,1,0:T(8,128)(2,1)S(1)}, bf16[8,256,256]{2,1,0:T(8,128)(2,1)S(1)}, u32[]{:S(2)}, u32[]{:S(2)}) collective-permute-start(bf16[8,256,256]{2,1,0:T(8,128)(2,1)S(1)} %add_convert_fusion.2), channel_id=1, source_target_pairs={{0,8},{1,3},{2,10},{3,5},{4,12},{5,7},{6,14},{7,1},{8,16},{9,11},{... | collective-permute-start | bytes 3145736 | tf_op jit(solution)/shard_map/ppermute | solution.py:34
  380.8 26.1 %collective-permute-start.10 = (bf16[8,256,256]{2,1,0:T(8,128)(2,1)S(1)}, bf16[8,256,256]{2,1,0:T(8,128)(2,1)S(1)}, u32[]{:S(2)}, u32[]{:S(2)}) collective-permute-start(bf16[8,256,256]{2,1,0:T(8,128)(2,1)S(1)} %add_convert_fusion.1), channel_id=1, source_target_pairs={{0,16},{1,5},{2,18},{3,7},{4,20},{5,1},{6,22},{7,3},{8,24},{9,13},... | collective-permute-start | bytes 3145736 | tf_op jit(solution)/shard_map/ppermute | solution.py:34
  383.5 24.6 %collective-permute-start.12 = (bf16[8,256,256]{2,1,0:T(8,128)(2,1)S(1)}, bf16[8,256,256]{2,1,0:T(8,128)(2,1)S(1)}, u32[]{:S(2)}, u32[]{:S(2)}) collective-permute-start(bf16[8,256,256]{2,1,0:T(8,128)(2,1)S(1)} %add_convert_fusion), channel_id=1, source_target_pairs={{0,24},{1,7},{2,26},{3,1},{4,28},{5,3},{6,30},{7,5},{8,0},{9,15},{... | collective-permute-start | bytes 3145736 | tf_op jit(solution)/shard_map/ppermute | solution.py:34
  408.1 1.0 copy-start.11
  410.3 7.8 %collective-permute-start.13 = (bf16[2,256,256]{2,1,0:T(8,128)(2,1)}, bf16[2,256,256]{2,1,0:T(8,128)(2,1)S(1)}, u32[]{:S(2)}, u32[]{:S(2)}) collective-permute-start(bf16[2,256,256]{2,1,0:T(8,128)(2,1)} %get-tuple-element.90), channel_id=1, source_target_pairs={{0,2},{1,9},{2,4},{3,11},{4,6},{5,13},{6,0},{7,15},{8,10},{9,17},{... | collective-permute-start | bytes 786440 | tf_op jit(solution)/shard_map/ppermute | solution.py:34
  410.3 10.2 %collective-permute-start.15 = (bf16[2,256,256]{2,1,0:T(8,128)(2,1)}, bf16[2,256,256]{2,1,0:T(8,128)(2,1)}, u32[]{:S(2)}, u32[]{:S(2)}) collective-permute-start(bf16[2,256,256]{2,1,0:T(8,128)(2,1)} %get-tuple-element.91), channel_id=1, source_target_pairs={{0,6},{1,25},{2,0},{3,27},{4,2},{5,29},{6,4},{7,31},{8,14},{9,1},{... | collective-permute-start | bytes 786440 | tf_op jit(solution)/shard_map/ppermute | solution.py:34
  413.5 8.2 %collective-permute-start.14 = (bf16[2,256,256]{2,1,0:T(8,128)(2,1)}, bf16[2,256,256]{2,1,0:T(8,128)(2,1)}, u32[]{:S(2)}, u32[]{:S(2)}) collective-permute-start(bf16[2,256,256]{2,1,0:T(8,128)(2,1)} %get-tuple-element.92), channel_id=1, source_target_pairs={{0,4},{1,17},{2,6},{3,19},{4,0},{5,21},{6,2},{7,23},{8,12},{9,25},... | collective-permute-start | bytes 786440 | tf_op jit(solution)/shard_map/ppermute | solution.py:34
  423.1 1.4 collective-permute-start.16

commit v7 on v5

--- a/solution.py
+++ b/solution.py
@@ -14,8 +14,9 @@
 RING = 4
 ANY = pl.BlockSpec(memory_space=pl.ANY)
 VMEM = pl.BlockSpec(memory_space=pltpu.VMEM)
+HBM = pl.BlockSpec(memory_space=pltpu.HBM)
 SMEM = pl.BlockSpec(memory_space=pltpu.SMEM)
-PARAMS = pltpu.CompilerParams(vmem_limit_bytes=40 << 20)
+PARAMS = pltpu.CompilerParams(vmem_limit_bytes=26 << 20)
 
 
 def shifted(value, axis, steps):
@@ -94,31 +95,9 @@
     )(peer, rows)
 
 
-def start_row(remote, i, slot, peers_hbm, low_hbm, high_hbm, far, sems, first, count):
-    for k in range(LINKS - LOCAL):
-        column = remote[k, i]
-        place = (far.at[slot, k], sems.at[slot, k])
-
-        @pl.when(column < first + count)
-        def _():
-            pltpu.make_async_copy(peers_hbm.at[jnp.maximum(column - first, 0)], *place).start()
-
-        @pl.when(column == first + count)
-        def _():
-            pltpu.make_async_copy(low_hbm.at[0], *place).start()
-
-        @pl.when(column > first + count)
-        def _():
-            pltpu.make_async_copy(high_hbm.at[0], *place).start()
-
-
-def wait_row(i, peers_hbm, far, sems):
-    for k in range(LINKS - LOCAL):
-        pltpu.make_async_copy(peers_hbm.at[0], far.at[i, k], sems.at[i, k]).wait()
-
-
-def row_image(local, match, i, slot, a_buf, own, far, rhs):
+def row_image(local, remote, match, i, a_buf, own, peers, low, high, rhs):
     width = own.shape[-1]
+    first, count = own.shape[0], peers.shape[0]
     for k in range(LINKS):
         for n in range(BLOCKS):
             wanted = match[k, n, i]
@@ -126,16 +105,19 @@
             if k < LOCAL:
                 block = own[local[k, i], there]
             else:
-                block = far[slot, k - LOCAL, there]
+                column = remote[k - LOCAL, i]
+                block = peers[jnp.clip(column - first, 0, count - 1), there]
+                block = jnp.where(column == first + count, low[0, there], block)
+                block = jnp.where(column > first + count, high[0, there], block)
             block = jnp.where(wanted < BLOCKS, block, jnp.zeros_like(block))
             rhs[k * width : (k + 1) * width, n * width : (n + 1) * width] = block
     lhs = jnp.concatenate([a_buf[i, k] for k in range(LINKS)], axis=1)
     return jnp.dot(lhs, rhs[...], preferred_element_type=jnp.float32).astype(jnp.bfloat16)
 
 
-def new_row(local, match, i, slot, a_buf, d_buf, own, far, rhs):
+def new_row(local, remote, match, i, a_buf, d_buf, own, peers, low, high, rhs):
     width = own.shape[-1]
-    image = row_image(local, match, i, slot, a_buf, own, far, rhs)
+    image = row_image(local, remote, match, i, a_buf, own, peers, low, high, rhs)
     update = jnp.dot(d_buf[i], image, preferred_element_type=jnp.float32)
     halves = [update[:, n * width : (n + 1) * width] for n in range(BLOCKS)]
     return [(own[i, n].astype(jnp.float32) - halves[n]).astype(jnp.bfloat16) for n in range(BLOCKS)]
@@ -143,58 +125,37 @@
 
 def slab_kernel(
     local, remote, match, slab,
-    a_buf, d_buf, own, peers_hbm, low_hbm, high_hbm,
+    a_buf, d_buf, own, peers, low, high,
     up, down,
-    far, rhs,
-    sems,
-):
-    arrays = (peers_hbm, low_hbm, high_hbm, far, sems, own.shape[0], peers_hbm.shape[0])
-    for j in range(2):
-        start_row(remote, slab[0, j], j, *arrays)
+    rhs,
+):
     for j, out in enumerate((up, down)):
-        wait_row(j, peers_hbm, far, sems)
-        for n, value in enumerate(new_row(local, match, slab[0, j], j, a_buf, d_buf, own, far, rhs)):
+        for n, value in enumerate(new_row(local, remote, match, slab[0, j], a_buf, d_buf, own, peers, low, high, rhs)):
             out[0, n] = value
 
 
 def smooth_kernel(
     local, remote, match, peer,
-    a_buf, d_buf, own, peers_hbm, low_hbm, high_hbm,
-    rows_hbm, out_hbm,
-    far, new, rhs,
-    sems, rows_sem, out_sem,
-):
-    count = own.shape[0]
-    peers = out_hbm.shape[0]
-    arrays = (peers_hbm, low_hbm, high_hbm, far, sems, count, peers)
-
-    @pl.loop(0, count)
+    a_buf, d_buf, own, peers, low, high,
+    new, out_hbm,
+    rhs,
+    out_sem,
+):
+    @pl.loop(0, own.shape[0])
     def _(i):
-        start_row(remote, i, i, *arrays)
-
-    @pl.loop(0, count)
-    def _(i):
-        wait_row(i, peers_hbm, far, sems)
-        for n, value in enumerate(new_row(local, match, i, i, a_buf, d_buf, own, far, rhs)):
+        for n, value in enumerate(new_row(local, remote, match, i, a_buf, d_buf, own, peers, low, high, rhs)):
             new[i, n] = value
-        pltpu.make_async_copy(new.at[i], rows_hbm.at[i], rows_sem.at[0]).start()
-        for q in range(peers):
+        for q in range(out_hbm.shape[0]):
 
             @pl.when(peer[0, q] == i)
             def _():
                 pltpu.make_async_copy(new.at[i], out_hbm.at[q], out_sem.at[0]).start()
 
-    pltpu.make_async_copy(rows_hbm, rows_hbm, rows_sem.at[0]).wait()
     pltpu.make_async_copy(out_hbm, out_hbm, out_sem.at[0]).wait()
 
 
-def row_scratch(count, width):
-    return [
-        pltpu.VMEM((count, LINKS - LOCAL, BLOCKS, width, width), jnp.bfloat16),
-        pltpu.VMEM((LINKS * width, BLOCKS * width), jnp.bfloat16),
-        pltpu.SemaphoreType.DMA((count, LINKS - LOCAL)),
-        pltpu.SemaphoreType.DMA((1,)),
-    ]
+def operand_scratch(width):
+    return pltpu.VMEM((LINKS * width, BLOCKS * width), jnp.bfloat16)
 
 
 def slab_rows(tables, slab, operator, inverse, rows, received, low, high):
@@ -202,10 +163,10 @@
     one = shape(1, *rows.shape[1:])
     return pl.pallas_call(
         slab_kernel,
-        in_specs=[SMEM] * 4 + [VMEM] * 3 + [ANY] * 3,
+        in_specs=[SMEM] * 4 + [VMEM] * 6,
         out_specs=[VMEM] * 2,
         out_shape=(one, one),
-        scratch_shapes=row_scratch(2, width)[:3],
+        scratch_shapes=[operand_scratch(width)],
         compiler_params=PARAMS,
         name="slab_rows",
     )(*tables, slab, operator, inverse, rows, received, low, high)
@@ -213,14 +174,13 @@
 
 def smooth(tables, peer, operator, inverse, rows, received, low, high):
     count, _, width, _ = operator.shape
-    far, rhs, sems, single = row_scratch(count, width)
     flops = 2 * count * (LINKS + 1) * BLOCKS * width**3
     return pl.pallas_call(
         smooth_kernel,
-        in_specs=[SMEM] * 4 + [VMEM] * 3 + [ANY] * 3,
-        out_specs=[ANY] * 2,
+        in_specs=[SMEM] * 4 + [VMEM] * 6,
+        out_specs=[VMEM, HBM],
         out_shape=(shape(*rows.shape), shape(*received.shape)),
-        scratch_shapes=[far, pltpu.VMEM(rows.shape, jnp.bfloat16), rhs, sems, single, single],
+        scratch_shapes=[operand_scratch(width), pltpu.SemaphoreType.DMA((1,))],
         cost_estimate=pl.CostEstimate(flops=flops, transcendentals=0, bytes_accessed=28 << 20),
         compiler_params=PARAMS,
         name="smooth_rows",
@@ -229,60 +189,42 @@
 
 def galerkin_kernel(
     local, remote, match, slots, here,
-    a_buf, own, peers_hbm, low_hbm, high_hbm,
-    keep, swap,
-    far, rhs,
-    sems,
-):
-    count, width = own.shape[0], own.shape[-1]
-    peers = peers_hbm.shape[0]
-    arrays = (peers_hbm, low_hbm, high_hbm, far, sems, count, peers)
-
-    @pl.loop(0, count)
+    a_buf, own, peers, low, high,
+    sums,
+    rhs,
+):
+    width = own.shape[-1]
+    sums[...] = jnp.zeros_like(sums)
+
+    @pl.loop(0, own.shape[0])
     def _(i):
-        start_row(remote, i, i, *arrays)
-
-    keep[...] = jnp.zeros_like(keep)
-    swap[...] = jnp.zeros_like(swap)
-
-    @pl.loop(0, count)
-    def _(i):
-        wait_row(i, peers_hbm, far, sems)
-        image = row_image(local, match, i, i, a_buf, own, far, rhs)
+        image = row_image(local, remote, match, i, a_buf, own, peers, low, high, rhs)
         mine = jnp.concatenate([own[i, n] for n in range(BLOCKS)], axis=1)
         partial = lax.dot_general(mine, image, (((0,), (0,)), ((), ())), preferred_element_type=jnp.float32)
         for n1 in range(BLOCKS):
             for n2 in range(BLOCKS):
-                block = partial[n1 * width : (n1 + 1) * width, n2 * width : (n2 + 1) * width]
-                block = block.astype(jnp.bfloat16)
                 slot = slots[n1, n2, i]
                 owner = slot // 2
                 chip = owner // 2
                 dx = (chip // RING - here[0] + RING) % RING
                 dy = (chip % RING - here[1] + RING) % RING
                 second = slot % 2
-                place = jnp.where(second == 0, dx * RING + dy, dy * RING + dx) * 2 + owner % 2
-
-                @pl.when(second == here[2])
-                def _():
-                    keep[place] = block
-
-                @pl.when(second != here[2])
-                def _():
-                    swap[place] = block
+                step = jnp.where(second == 0, dx, dy)
+                place = jnp.where(second == 0, dy, dx) * 2 + owner % 2
+                group = jnp.where(second == here[2], 0, RING) + step
+                block = partial[n1 * width : (n1 + 1) * width, n2 * width : (n2 + 1) * width]
+                sums[group, place] = block.astype(jnp.bfloat16)
 
 
 def galerkin(tables, slots, here, operator, rows, received, low, high):
-    count, _, width, _ = operator.shape
-    half = RING * RING * BLOCKS
-    far, rhs, sems, single = row_scratch(count, width)
+    width = operator.shape[-1]
     return pl.pallas_call(
         galerkin_kernel,
-        in_specs=[SMEM] * 5 + [VMEM] * 2 + [ANY] * 3,
-        out_specs=[VMEM] * 2,
-        out_shape=(shape(half, width, width), shape(half, width, width)),
-        scratch_shapes=[far, rhs, sems],
-        compiler_params=pltpu.CompilerParams(vmem_limit_bytes=30 << 20),
+        in_specs=[SMEM] * 5 + [VMEM] * 5,
+        out_specs=VMEM,
+        out_shape=shape(2 * RING, 2 * RING, width, width),
+        scratch_shapes=[operand_scratch(width)],
+        compiler_params=PARAMS,
         name="galerkin_rows",
     )(*tables, slots, here, operator, rows, received, low, high)
 
@@ -322,10 +264,16 @@
         rows, outgoing = smooth(tables, peer, *operands)
         outgoing, low, high = lax.optimization_barrier((outgoing, low, high))
         received = lax.all_to_all(outgoing, GY, split_axis=0, concat_axis=0, tiled=True)
-    keep, swap = galerkin(tables, slots, here, operator_blocks, rows, received, low, high)
-    other = lax.ppermute(swap, "c", [(0, 1), (1, 0)])
-    group = keep.shape[0] // RING
-    parts = [add((keep[group * j : group * j + group], other[group * j : group * j + group])) for j in range(RING)]
+    sums = galerkin(tables, slots, here, operator_blocks, rows, received, low, high)
+    others = [lax.ppermute(sums[RING + j], "c", [(0, 1), (1, 0)]) for j in range(RING)]
+    parts = [None] * RING
+    ready = None
+    for j in (1, 2, 3, 0):
+        other = others[j]
+        if ready is not None:
+            other, parts[ready] = lax.optimization_barrier((other, parts[ready]))
+        parts[j] = add((sums[j], other))
+        ready = j
     for swapped in range(2):
         terms = [parts[0], *[around(parts[s], s, swapped) for s in range(1, RING)]]
         group = max(terms[0].shape[0] // RING, 2)

time: 426 us -> 416 us (0.977)
  waiting for transfers between devices: 48.9 us -> 42.9 us
  transfers between devices with their start and end apart: 14 -> 17, of which waited for: 10 -> 11; matrix products, arithmetic and copies ran while one was open for 0% -> 0% of each run, Pallas kernels for 5% -> 6%
where the time goes in v7:
time: 416 us; the launch traced here: 415 us
  blocking collectives  301 us (72%)
  waiting for transfers between devices  42.9 us (10%)
  Pallas kernels  37.3 us (9%)
  starting transfers between devices  24.4 us (6%)
  other arithmetic  4.59 us (1%)
    all_to_all x3, blocking collectives, body(): lax.all_to_all(outgoing, GY, split_axis=0, concat_axis=0, tiled=True)  301 us
    ppermute x6, waiting for transfers between devices, around(): return lax.ppermute(value, GY, pairs)  30.9 us
    pallas_call x2, Pallas kernels, smooth(): pl.pallas_call(smooth_kernel, in_specs=[SMEM] * 4 + [VMEM] * 6, out_specs...  21.8 us
    ppermute x6, starting transfers between devices, shifted(): lax.ppermute(value, axis, [(source, source + steps) for source in range(f...  16 us
    pallas_call x1, Pallas kernels, galerkin(): pl.pallas_call(galerkin_kernel, in_specs=[SMEM] * 5 + [VMEM] * 5, out_spe...  8.4 us
  transfers between devices with their start and end apart: 17, of which 11 were waited for; matrix products, arithmetic and copies ran while one was open for 0% of the time, Pallas kernels for 6%

profile of v7, /device:TPU:0, one launch (start us, length us, event | category | flops | bytes accessed | tf_op | source)
XLA Modules:
  0.0 414.9 jit_solution(11349302244152342937)
XLA Ops:
  0.6 1.6 copy-done
  2.2 0.7 copy-done.7
  2.9 0.7 pick_rows.1
  3.5 3.9 collective-permute-start
  7.5 1.3 collective-permute-start.1
  8.8 0.0 slice-start
  8.8 1.8 pack_rows.1
  10.6 0.1 pad_add_fusion.here
  10.7 0.0 copy-start.6
  10.7 0.0 copy-start.8
  10.7 2.3 collective-permute-done.low
  13.0 4.3 %collective-permute-done.1.high = bf16[1,2,256,256]{3,2,1,0:T(8,128)(2,1)S(1)} collective-permute-done((bf16[1,2,256,256]{3,2,1,0:T(8,128)(2,1)S(1)}, bf16[1,2,256,256]{3,2,1,0:T(8,128)(2,1)S(1)}, u32[]{:S(2)}, u32[]{:S(2)}) %collective-permute-start.1) | collective-permute-done | bytes 262176 | tf_op jit(solution)/shard_map/ppermute | solution.py:25
  17.3 102.6 %all_to_all.15.peers = bf16[32,2,256,256]{3,2,1,0:T(8,128)(2,1)S(1)} all-to-all(bf16[32,2,256,256]{3,2,1,0:T(8,128)(2,1)S(1)} %pack_rows.1), channel_id=1, replica_groups=mesh['gx'=4,'x'=4,'y'=4,'c'=2] {'x','y','c'}, dimensions={0} | all-to-all | bytes 16777216 | tf_op jit(solution)/shard_map/all_to_all | solution.py:258
  119.9 0.0 copy-done.4
  119.9 0.0 copy-done.5
  119.9 0.0 copy-done.6
  119.9 2.3 slab_rows.2
  122.2 3.7 collective-permute-start.2
  125.9 1.3 collective-permute-start.3
  127.2 10.2 %smooth_rows.2 = (bf16[8,2,256,256]{3,2,1,0:T(8,128)(2,1)S(1)}, bf16[32,2,256,256]{3,2,1,0:T(8,128)(2,1)S(1)}) custom-call(s32[2,8]{1,0:T(2,128)S(1)} %bitcast.48, s32[4,8]{1,0:T(4,128)S(1)} %bitcast.43, s32[6,2,8]{2,1,0:T(2,128)S(1)} %bitcast.38, s32[1,32]{1,0:T(1,128)S(1)} %copy-done.9, bf16[8,6,256,256]{3,2,1,0:T(8,128)(2,1)S(1)} %bitcast.36, ...), custom_call_target="tpu_custom_call" | custom-call | flops 3758096384 | bytes 29360128 | tf_op jit(solution)/shard_map/smooth_rows/pallas_call | solution.py:178
  137.4 0.0 collective-permute-done.2.low
  137.5 0.0 collective-permute-done.3.high
  137.5 99.3 %all_to_all.16.peers = bf16[32,2,256,256]{3,2,1,0:T(8,128)(2,1)S(1)} all-to-all(bf16[32,2,256,256]{3,2,1,0:T(8,128)(2,1)S(1)} %get-tuple-element.61), channel_id=1, replica_groups=mesh['gx'=4,'x'=4,'y'=4,'c'=2] {'x','y','c'}, dimensions={0} | all-to-all | bytes 16777216 | tf_op jit(solution)/shard_map/all_to_all | solution.py:266
  236.8 2.3 slab_rows.3
  239.1 4.6 %collective-permute-start.4 = (bf16[1,2,256,256]{3,2,1,0:T(8,128)(2,1)S(1)}, bf16[1,2,256,256]{3,2,1,0:T(8,128)(2,1)S(1)}, u32[]{:S(2)}, u32[]{:S(2)}) collective-permute-start(bf16[1,2,256,256]{3,2,1,0:T(8,128)(2,1)S(1)} %get-tuple-element.75), channel_id=1, source_target_pairs={{0,32},{32,64},{64,96},{1,33},{33,65},{65,97},{2,34},{34,66},{66,9... | collective-permute-start | bytes 786440 | tf_op jit(solution)/shard_map/ppermute | solution.py:25
  243.7 1.3 collective-permute-start.5
  245.0 11.6 %smooth_rows.3 = (bf16[8,2,256,256]{3,2,1,0:T(8,128)(2,1)}, bf16[32,2,256,256]{3,2,1,0:T(8,128)(2,1)S(1)}) custom-call(s32[2,8]{1,0:T(2,128)S(1)} %bitcast.50, s32[4,8]{1,0:T(4,128)S(1)} %bitcast.45, s32[6,2,8]{2,1,0:T(2,128)S(1)} %bitcast.40, s32[1,32]{1,0:T(1,128)S(1)} %copy-done.9, bf16[8,6,256,256]{3,2,1,0:T(8,128)(2,1)S(1)} %bitcast.36, ...), custom_call_target="tpu_custom_call" | custom-call | flops 3758096384 | bytes 29360128 | tf_op jit(solution)/shard_map/smooth_rows/pallas_call | solution.py:178
  256.6 0.0 collective-permute-done.4.low
  256.6 0.0 collective-permute-done.5.high
  256.6 0.0 copy-start.3
  256.6 0.0 copy-start.10
  256.6 99.4 %all_to_all.17.peers = bf16[32,2,256,256]{3,2,1,0:T(8,128)(2,1)S(1)} all-to-all(bf16[32,2,256,256]{3,2,1,0:T(8,128)(2,1)S(1)} %get-tuple-element.77), channel_id=1, replica_groups=mesh['gx'=4,'x'=4,'y'=4,'c'=2] {'x','y','c'}, dimensions={0} | all-to-all | bytes 16777216 | tf_op jit(solution)/shard_map/all_to_all | solution.py:266
  356.1 8.4 %galerkin_rows.1 = bf16[8,8,256,256]{3,2,1,0:T(8,128)(2,1)S(1)} custom-call(s32[2,8]{1,0:T(2,128)S(1)} %bitcast.51, s32[4,8]{1,0:T(4,128)S(1)} %bitcast.46, s32[6,2,8]{2,1,0:T(2,128)S(1)} %bitcast.41, s32[2,2,8]{2,1,0:T(2,128)S(1)} %bitcast.52, s32[3]{0:T(128)S(1)} %pad_add_fusion.here, bf16[8,6,256,256]{3,2,1,0:T(8,128)(2,1)S(1)} %bitcast.36, ...), custom_call_target="tpu_custom_call" | custom-call | tf_op jit(solution)/shard_map/galerkin_rows/pallas_call | solution.py:221
  364.5 0.3 slice_bitcast_fusion
  364.8 0.5 collective-permute-start.9
  365.2 0.1 collective-permute-start.8
  365.4 0.4 collective-permute-start.7
  365.7 0.1 collective-permute-start.6
  365.9 1.6 collective-permute-done.9
  367.5 0.3 fusion
  367.8 1.2 collective-permute-done.8
  369.0 0.0 collective-permute-start.10
  369.0 0.3 fusion.1
  369.3 1.2 collective-permute-done.7
  370.5 2.0 collective-permute-start.11
  372.6 0.3 fusion.2
  372.9 0.0 collective-permute-done.6
  372.9 1.3 collective-permute-start.12
  374.2 0.3 fusion.3
  374.5 21.8 %collective-permute-done.10 = bf16[8,256,256]{2,1,0:T(8,128)(2,1)S(1)} collective-permute-done((bf16[8,256,256]{2,1,0:T(8,128)(2,1)S(1)}, bf16[8,256,256]{2,1,0:T(8,128)(2,1)S(1)}, u32[]{:S(2)}, u32[]{:S(2)}) %collective-permute-start.10) | collective-permute-done | bytes 1048608 | tf_op jit(solution)/shard_map/ppermute | solution.py:35
  396.3 0.0 collective-permute-done.11
  396.3 1.5 collective-permute-done.12
  397.7 1.0 copy-done.11
  398.7 1.2 add_convert_fusion.3
  399.9 0.5 collective-permute-start.13
  400.4 2.7 collective-permute-start.15
  403.2 0.6 collective-permute-start.14
  403.7 4.0 collective-permute-done.13
  407.7 2.5 collective-permute-done.15
  410.2 1.1 collective-permute-done.14
  411.3 1.3 add_convert_fusion
  412.7 0.1 collective-permute-start.16
  412.8 1.3 collective-permute-done.16
  414.2 0.7 pad_maximum_fusion
  (20 shorter events, 0.1 us)
Async XLA Ops:
  0.6 1.6 copy-start
  2.2 0.7 copy-start.7
  2.9 5.9 %copy-start.1 = (bf16[8,2,256,256]{3,2,1,0:T(8,128)(2,1)S(1)}, bf16[8,2,256,256]{3,2,1,0:T(8,128)(2,1)}, u32[]{:S(2)}) copy-start(bf16[8,2,256,256]{3,2,1,0:T(8,128)(2,1)} %own.2) | copy-start | bytes 6291460
  2.9 5.9 %copy-start.9 = (s32[1,32]{1,0:T(1,128)S(1)}, s32[1,32]{1,0:T(1,128)}, u32[]{:S(2)}) copy-start(s32[1,32]{1,0:T(1,128)} %peer.5) | copy-start | bytes 388
  3.5 9.5 %collective-permute-start = (bf16[1,2,256,256]{3,2,1,0:T(8,128)(2,1)S(1)}, bf16[1,2,256,256]{3,2,1,0:T(8,128)(2,1)S(1)}, u32[]{:S(2)}, u32[]{:S(2)}) collective-permute-start(bf16[1,2,256,256]{3,2,1,0:T(8,128)(2,1)S(1)} %get-tuple-element.44), channel_id=1, source_target_pairs={{0,32},{32,64},{64,96},{1,33},{33,65},{65,97},{2,34},{34,66},{66,9... | collective-permute-start | bytes 786440 | tf_op jit(solution)/shard_map/ppermute | solution.py:25
  7.5 9.8 %collective-permute-start.1 = (bf16[1,2,256,256]{3,2,1,0:T(8,128)(2,1)S(1)}, bf16[1,2,256,256]{3,2,1,0:T(8,128)(2,1)S(1)}, u32[]{:S(2)}, u32[]{:S(2)}) collective-permute-start(bf16[1,2,256,256]{3,2,1,0:T(8,128)(2,1)S(1)} %get-tuple-element.45), channel_id=1, source_target_pairs={{32,0},{64,32},{96,64},{33,1},{65,33},{97,65},{34,2},{66,34},{98,6... | collective-permute-start | bytes 786440 | tf_op jit(solution)/shard_map/ppermute | solution.py:25
  8.8 111.1 %slice-start = ((s8[6291456]{0:T(1024)(128)(4,1)}), s8[4194304]{0:T(1024)(128)(4,1)S(1)}, s32[]{:S(2)}) async-start(s8[6291456]{0:T(1024)(128)(4,1)} %bitcast.35), calls=%async_computation.3 | async-start | bytes 8388608
  10.7 109.2 %slice-start.1 = ((s8[6291456]{0:T(1024)(128)(4,1)}), s8[2097152]{0:T(1024)(128)(4,1)S(1)}, s32[]{:S(2)}) async-start(s8[6291456]{0:T(1024)(128)(4,1)} %bitcast.35), calls=%async_computation.4 | async-start | bytes 4194304
  10.7 109.2 %copy-start.2 = (bf16[8,256,256]{2,1,0:T(8,128)(2,1)S(1)}, bf16[8,256,256]{2,1,0:T(8,128)(2,1)}, u32[]{:S(2)}) copy-start(bf16[8,256,256]{2,1,0:T(8,128)(2,1)} %d_buf.5) | copy-start | bytes 3145732
  10.7 109.2 %copy-start.4 = (s32[8,6,2]{0,2,1:T(2,128)S(1)}, s32[8,6,2]{0,2,1:T(2,128)}, u32[]{:S(2)}) copy-start(s32[8,6,2]{0,2,1:T(2,128)} %param.12) | copy-start | bytes 1156
  10.7 109.2 %copy-start.5 = (s32[8,4]{0,1:T(4,128)S(1)}, s32[8,4]{0,1:T(4,128)}, u32[]{:S(2)}) copy-start(s32[8,4]{0,1:T(4,128)} %param.11) | copy-start | bytes 388
  10.7 109.2 %copy-start.6 = (s32[8,2]{0,1:T(2,128)S(1)}, s32[8,2]{0,1:T(2,128)}, u32[]{:S(2)}) copy-start(s32[8,2]{0,1:T(2,128)} %param.10) | copy-start | bytes 196
  10.7 109.2 %copy-start.8 = (s32[1,2]{1,0:T(1,128)S(1)}, s32[1,2]{1,0:T(1,128)}, u32[]{:S(2)}) copy-start(s32[1,2]{1,0:T(1,128)} %slab.5) | copy-start | bytes 28
  122.2 15.2 %collective-permute-start.2 = (bf16[1,2,256,256]{3,2,1,0:T(8,128)(2,1)S(1)}, bf16[1,2,256,256]{3,2,1,0:T(8,128)(2,1)S(1)}, u32[]{:S(2)}, u32[]{:S(2)}) collective-permute-start(bf16[1,2,256,256]{3,2,1,0:T(8,128)(2,1)S(1)} %get-tuple-element.59), channel_id=1, source_target_pairs={{0,32},{32,64},{64,96},{1,33},{33,65},{65,97},{2,34},{34,66},{66,9... | collective-permute-start | bytes 786440 | tf_op jit(solution)/shard_map/ppermute | solution.py:25
  125.9 11.5 %collective-permute-start.3 = (bf16[1,2,256,256]{3,2,1,0:T(8,128)(2,1)S(1)}, bf16[1,2,256,256]{3,2,1,0:T(8,128)(2,1)S(1)}, u32[]{:S(2)}, u32[]{:S(2)}) collective-permute-start(bf16[1,2,256,256]{3,2,1,0:T(8,128)(2,1)S(1)} %get-tuple-element.60), channel_id=1, source_target_pairs={{32,0},{64,32},{96,64},{33,1},{65,33},{97,65},{34,2},{66,34},{98,6... | collective-permute-start | bytes 786440 | tf_op jit(solution)/shard_map/ppermute | solution.py:25
  239.1 17.5 %collective-permute-start.4 = (bf16[1,2,256,256]{3,2,1,0:T(8,128)(2,1)S(1)}, bf16[1,2,256,256]{3,2,1,0:T(8,128)(2,1)S(1)}, u32[]{:S(2)}, u32[]{:S(2)}) collective-permute-start(bf16[1,2,256,256]{3,2,1,0:T(8,128)(2,1)S(1)} %get-tuple-element.75), channel_id=1, source_target_pairs={{0,32},{32,64},{64,96},{1,33},{33,65},{65,97},{2,34},{34,66},{66,9... | collective-permute-start | bytes 786440 | tf_op jit(solution)/shard_map/ppermute | solution.py:25
  243.7 12.9 %collective-permute-start.5 = (bf16[1,2,256,256]{3,2,1,0:T(8,128)(2,1)S(1)}, bf16[1,2,256,256]{3,2,1,0:T(8,128)(2,1)S(1)}, u32[]{:S(2)}, u32[]{:S(2)}) collective-permute-start(bf16[1,2,256,256]{3,2,1,0:T(8,128)(2,1)S(1)} %get-tuple-element.76), channel_id=1, source_target_pairs={{32,0},{64,32},{96,64},{33,1},{65,33},{97,65},{34,2},{66,34},{98,6... | collective-permute-start | bytes 786440 | tf_op jit(solution)/shard_map/ppermute | solution.py:25
  256.6 99.5 %copy-start.3 = (bf16[8,2,256,256]{3,2,1,0:T(8,128)(2,1)S(1)}, bf16[8,2,256,256]{3,2,1,0:T(8,128)(2,1)}, u32[]{:S(2)}) copy-start(bf16[8,2,256,256]{3,2,1,0:T(8,128)(2,1)} %get-tuple-element.42.own) | copy-start | bytes 6291460
  256.6 99.5 %copy-start.10 = (s32[8,2,2]{0,2,1:T(2,128)S(1)}, s32[8,2,2]{0,2,1:T(2,128)}, u32[]{:S(2)}) copy-start(s32[8,2,2]{0,2,1:T(2,128)} %param.17) | copy-start | bytes 388
  364.8 2.7 collective-permute-start.9
  365.2 3.8 collective-permute-start.8
  365.4 5.2 %collective-permute-start.7 = (bf16[8,256,256]{2,1,0:T(8,128)(2,1)S(1)}, bf16[8,256,256]{2,1,0:T(8,128)(2,1)S(1)}, u32[]{:S(2)}, u32[]{:S(2)}) collective-permute-start(bf16[8,256,256]{2,1,0:T(8,128)(2,1)S(1)} %get-tuple-element.88), channel_id=1, source_target_pairs={{0,1},{1,0},{2,3},{3,2},{4,5},{5,4},{6,7},{7,6},{8,9},{9,8},{10,11... | collective-permute-start | bytes 3145736 | tf_op jit(solution)/shard_map/ppermute | solution.py:268
  365.7 7.1 %collective-permute-start.6 = (bf16[8,256,256]{2,1,0:T(8,128)(2,1)S(1)}, bf16[8,256,256]{2,1,0:T(8,128)(2,1)S(1)}, u32[]{:S(2)}, u32[]{:S(2)}) collective-permute-start(bf16[8,256,256]{2,1,0:T(8,128)(2,1)S(1)} %get-tuple-element.89), channel_id=1, source_target_pairs={{0,1},{1,0},{2,3},{3,2},{4,5},{5,4},{6,7},{7,6},{8,9},{9,8},{10,11... | collective-permute-start | bytes 3145736 | tf_op jit(solution)/shard_map/ppermute | solution.py:268
  369.0 27.2 %collective-permute-start.10 = (bf16[8,256,256]{2,1,0:T(8,128)(2,1)S(1)}, bf16[8,256,256]{2,1,0:T(8,128)(2,1)S(1)}, u32[]{:S(2)}, u32[]{:S(2)}) collective-permute-start(bf16[8,256,256]{2,1,0:T(8,128)(2,1)S(1)} %fusion), channel_id=1, source_target_pairs={{0,8},{1,3},{2,10},{3,5},{4,12},{5,7},{6,14},{7,1},{8,16},{9,11},{... | collective-permute-start | bytes 3145736 | tf_op jit(solution)/shard_map/ppermute | solution.py:35
  370.5 25.7 %collective-permute-start.11 = (bf16[8,256,256]{2,1,0:T(8,128)(2,1)S(1)}, bf16[8,256,256]{2,1,0:T(8,128)(2,1)S(1)}, u32[]{:S(2)}, u32[]{:S(2)}) collective-permute-start(bf16[8,256,256]{2,1,0:T(8,128)(2,1)S(1)} %fusion.1), channel_id=1, source_target_pairs={{0,16},{1,5},{2,18},{3,7},{4,20},{5,1},{6,22},{7,3},{8,24},{9,13},... | collective-permute-start | bytes 3145736 | tf_op jit(solution)/shard_map/ppermute | solution.py:35
  372.9 24.9 %collective-permute-start.12 = (bf16[8,256,256]{2,1,0:T(8,128)(2,1)S(1)}, bf16[8,256,256]{2,1,0:T(8,128)(2,1)S(1)}, u32[]{:S(2)}, u32[]{:S(2)}) collective-permute-start(bf16[8,256,256]{2,1,0:T(8,128)(2,1)S(1)} %fusion.2), channel_id=1, source_target_pairs={{0,24},{1,7},{2,26},{3,1},{4,28},{5,3},{6,30},{7,5},{8,0},{9,15},{... | collective-permute-start | bytes 3145736 | tf_op jit(solution)/shard_map/ppermute | solution.py:35
  397.7 1.0 copy-start.11
  399.9 7.8 %collective-permute-start.13 = (bf16[2,256,256]{2,1,0:T(8,128)(2,1)}, bf16[2,256,256]{2,1,0:T(8,128)(2,1)S(1)}, u32[]{:S(2)}, u32[]{:S(2)}) collective-permute-start(bf16[2,256,256]{2,1,0:T(8,128)(2,1)} %get-tuple-element.90), channel_id=1, source_target_pairs={{0,2},{1,9},{2,4},{3,11},{4,6},{5,13},{6,0},{7,15},{8,10},{9,17},{... | collective-permute-start | bytes 786440 | tf_op jit(solution)/shard_map/ppermute | solution.py:35
  400.4 9.8 %collective-permute-start.15 = (bf16[2,256,256]{2,1,0:T(8,128)(2,1)}, bf16[2,256,256]{2,1,0:T(8,128)(2,1)}, u32[]{:S(2)}, u32[]{:S(2)}) collective-permute-start(bf16[2,256,256]{2,1,0:T(8,128)(2,1)} %get-tuple-element.91), channel_id=1, source_target_pairs={{0,6},{1,25},{2,0},{3,27},{4,2},{5,29},{6,4},{7,31},{8,14},{9,1},{... | collective-permute-start | bytes 786440 | tf_op jit(solution)/shard_map/ppermute | solution.py:35
  403.2 8.2 %collective-permute-start.14 = (bf16[2,256,256]{2,1,0:T(8,128)(2,1)}, bf16[2,256,256]{2,1,0:T(8,128)(2,1)}, u32[]{:S(2)}, u32[]{:S(2)}) collective-permute-start(bf16[2,256,256]{2,1,0:T(8,128)(2,1)} %get-tuple-element.92), channel_id=1, source_target_pairs={{0,4},{1,17},{2,6},{3,19},{4,0},{5,21},{6,2},{7,23},{8,12},{9,25},... | collective-permute-start | bytes 786440 | tf_op jit(solution)/shard_map/ppermute | solution.py:35
  412.7 1.4 collective-permute-start.16

commit v8 on v7

--- a/solution.py
+++ b/solution.py
@@ -14,7 +14,6 @@
 RING = 4
 ANY = pl.BlockSpec(memory_space=pl.ANY)
 VMEM = pl.BlockSpec(memory_space=pltpu.VMEM)
-HBM = pl.BlockSpec(memory_space=pltpu.HBM)
 SMEM = pl.BlockSpec(memory_space=pltpu.SMEM)
 PARAMS = pltpu.CompilerParams(vmem_limit_bytes=26 << 20)
 
@@ -137,21 +136,22 @@
 def smooth_kernel(
     local, remote, match, peer,
     a_buf, d_buf, own, peers, low, high,
-    new, out_hbm,
-    rhs,
-    out_sem,
+    rows_hbm, out_hbm,
+    new, rhs,
+    rows_sem, out_sems,
 ):
     @pl.loop(0, own.shape[0])
     def _(i):
         for n, value in enumerate(new_row(local, remote, match, i, a_buf, d_buf, own, peers, low, high, rhs)):
             new[i, n] = value
-        for q in range(out_hbm.shape[0]):
-
-            @pl.when(peer[0, q] == i)
-            def _():
-                pltpu.make_async_copy(new.at[i], out_hbm.at[q], out_sem.at[0]).start()
-
-    pltpu.make_async_copy(out_hbm, out_hbm, out_sem.at[0]).wait()
+        pltpu.make_async_copy(new.at[i], rows_hbm.at[i], rows_sem.at[0]).start()
+
+    copies = [pltpu.make_async_copy(new.at[peer[0, q]], out_hbm.at[q], out_sems.at[q]) for q in range(out_hbm.shape[0])]
+    for copy in copies:
+        copy.start()
+    pltpu.make_async_copy(rows_hbm, rows_hbm, rows_sem.at[0]).wait()
+    for copy in copies:
+        copy.wait()
 
 
 def operand_scratch(width):
@@ -178,9 +178,14 @@
     return pl.pallas_call(
         smooth_kernel,
         in_specs=[SMEM] * 4 + [VMEM] * 6,
-        out_specs=[VMEM, HBM],
+        out_specs=[ANY, ANY],
         out_shape=(shape(*rows.shape), shape(*received.shape)),
-        scratch_shapes=[operand_scratch(width), pltpu.SemaphoreType.DMA((1,))],
+        scratch_shapes=[
+            pltpu.VMEM(rows.shape, jnp.bfloat16),
+            operand_scratch(width),
+            pltpu.SemaphoreType.DMA((1,)),
+            pltpu.SemaphoreType.DMA((received.shape[0],)),
+        ],
         cost_estimate=pl.CostEstimate(flops=flops, transcendentals=0, bytes_accessed=28 << 20),
         compiler_params=PARAMS,
         name="smooth_rows",
@@ -278,6 +283,7 @@
         terms = [parts[0], *[around(parts[s], s, swapped) for s in range(1, RING)]]
         group = max(terms[0].shape[0] // RING, 2)
         parts = [add([term[j : j + group] for term in terms]) for j in range(0, terms[0].shape[0], group)]
+        parts = lax.optimization_barrier(parts)
     total = parts[0]
     core = lax.axis_index("c") == 0
     mine = jnp.where(core, total[:1], total[1:])

time: 416 us -> 409 us (0.983)
  Pallas kernels: 37.3 us -> 32 us
    pallas_call x2, Pallas kernels: 21.8 us -> 16.6 us  [smooth(): pl.pallas_call(smooth_kernel, in_specs=[SMEM] * 4 + [VMEM] * 6, out_specs...]
  transfers between devices with their start and end apart: 17 -> 17, of which waited for: 11 -> 12; matrix products, arithmetic and copies ran while one was open for 0% -> 0% of each run, Pallas kernels for 6% -> 5%
where the time goes in v8:
time: 409 us; the launch traced here: 407 us
  blocking collectives  301 us (74%)
  waiting for transfers between devices  43.3 us (11%)
  Pallas kernels  32 us (8%)
  starting transfers between devices  25 us (6%)
    all_to_all x3, blocking collectives, body(): lax.all_to_all(outgoing, GY, split_axis=0, concat_axis=0, tiled=True)  301 us
    ppermute x6, waiting for transfers between devices, around(): return lax.ppermute(value, GY, pairs)  30.1 us
    pallas_call x2, Pallas kernels, smooth(): pl.pallas_call(smooth_kernel, in_specs=[SMEM] * 4 + [VMEM] * 6, out_specs...  16.6 us
    ppermute x6, starting transfers between devices, shifted(): lax.ppermute(value, axis, [(source, source + steps) for source in range(f...  16 us
    pallas_call x1, Pallas kernels, galerkin(): pl.pallas_call(galerkin_kernel, in_specs=[SMEM] * 5 + [VMEM] * 5, out_spe...  8.54 us
  transfers between devices with their start and end apart: 17, of which 12 were waited for; matrix products, arithmetic and copies ran while one was open for 0% of the time, Pallas kernels for 5%

profile of v8, /device:TPU:0, one launch (start us, length us, event | category | flops | bytes accessed | tf_op | source)
XLA Modules:
  0.0 407.3 jit_solution(11822073828932612522)
XLA Ops:
  0.6 0.0 copy-start
  0.6 1.6 copy-done
  2.2 0.7 copy-done.7
  2.9 0.7 pick_rows.1
  3.5 3.9 collective-permute-start
  7.5 1.3 collective-permute-start.1
  8.8 0.0 copy-done.1
  8.8 0.0 copy-done.9
  8.8 0.0 slice-start
  8.8 1.8 pack_rows.1
  10.6 0.1 pad_add_fusion.here
  10.7 0.0 copy-start.6
  10.7 0.0 copy-start.8
  10.7 2.3 collective-permute-done.low
  13.0 4.3 %collective-permute-done.1.high = bf16[1,2,256,256]{3,2,1,0:T(8,128)(2,1)S(1)} collective-permute-done((bf16[1,2,256,256]{3,2,1,0:T(8,128)(2,1)S(1)}, bf16[1,2,256,256]{3,2,1,0:T(8,128)(2,1)S(1)}, u32[]{:S(2)}, u32[]{:S(2)}) %collective-permute-start.1) | collective-permute-done | bytes 262176 | tf_op jit(solution)/shard_map/ppermute | solution.py:24
  17.3 102.6 %all_to_all.15.peers = bf16[32,2,256,256]{3,2,1,0:T(8,128)(2,1)S(1)} all-to-all(bf16[32,2,256,256]{3,2,1,0:T(8,128)(2,1)S(1)} %pack_rows.1), channel_id=1, replica_groups=mesh['gx'=4,'x'=4,'y'=4,'c'=2] {'x','y','c'}, dimensions={0} | all-to-all | bytes 16777216 | tf_op jit(solution)/shard_map/all_to_all | solution.py:263
  119.9 0.0 slice-done
  119.9 0.0 slice-done.1
  119.9 0.0 copy-done.2
  119.9 2.3 slab_rows.2
  122.2 3.7 collective-permute-start.2
  125.9 1.3 collective-permute-start.3
  127.2 8.6 %smooth_rows.2 = (bf16[8,2,256,256]{3,2,1,0:T(8,128)(2,1)S(1)}, bf16[32,2,256,256]{3,2,1,0:T(8,128)(2,1)S(1)}) custom-call(s32[2,8]{1,0:T(2,128)S(1)} %bitcast.48, s32[4,8]{1,0:T(4,128)S(1)} %bitcast.43, s32[6,2,8]{2,1,0:T(2,128)S(1)} %bitcast.38, s32[1,32]{1,0:T(1,128)S(1)} %copy-done.9, bf16[8,6,256,256]{3,2,1,0:T(8,128)(2,1)S(1)} %bitcast.36, ...), custom_call_target="tpu_custom_call" | custom-call | flops 3758096384 | bytes 29360128 | tf_op jit(solution)/shard_map/smooth_rows/pallas_call | solution.py:178
  135.8 0.0 collective-permute-done.2.low
  135.8 0.3 collective-permute-done.3.high
  136.1 99.0 %all_to_all.16.peers = bf16[32,2,256,256]{3,2,1,0:T(8,128)(2,1)S(1)} all-to-all(bf16[32,2,256,256]{3,2,1,0:T(8,128)(2,1)S(1)} %get-tuple-element.65), channel_id=1, replica_groups=mesh['gx'=4,'x'=4,'y'=4,'c'=2] {'x','y','c'}, dimensions={0} | all-to-all | bytes 16777216 | tf_op jit(solution)/shard_map/all_to_all | solution.py:271
  235.1 2.2 slab_rows.3
  237.3 4.6 %collective-permute-start.4 = (bf16[1,2,256,256]{3,2,1,0:T(8,128)(2,1)S(1)}, bf16[1,2,256,256]{3,2,1,0:T(8,128)(2,1)S(1)}, u32[]{:S(2)}, u32[]{:S(2)}) collective-permute-start(bf16[1,2,256,256]{3,2,1,0:T(8,128)(2,1)S(1)} %get-tuple-element.79), channel_id=1, source_target_pairs={{0,32},{32,64},{64,96},{1,33},{33,65},{65,97},{2,34},{34,66},{66,9... | collective-permute-start | bytes 786440 | tf_op jit(solution)/shard_map/ppermute | solution.py:24
  241.9 1.3 collective-permute-start.5
  243.2 8.0 %smooth_rows.3 = (bf16[8,2,256,256]{3,2,1,0:T(8,128)(2,1)}, bf16[32,2,256,256]{3,2,1,0:T(8,128)(2,1)S(1)}) custom-call(s32[2,8]{1,0:T(2,128)S(1)} %bitcast.50, s32[4,8]{1,0:T(4,128)S(1)} %bitcast.45, s32[6,2,8]{2,1,0:T(2,128)S(1)} %bitcast.40, s32[1,32]{1,0:T(1,128)S(1)} %copy-done.9, bf16[8,6,256,256]{3,2,1,0:T(8,128)(2,1)S(1)} %bitcast.36, ...), custom_call_target="tpu_custom_call" | custom-call | flops 3758096384 | bytes 29360128 | tf_op jit(solution)/shard_map/smooth_rows/pallas_call | solution.py:178
  251.2 0.0 collective-permute-done.4.low
  251.2 0.9 collective-permute-done.5.high
  252.1 99.1 %all_to_all.17.peers = bf16[32,2,256,256]{3,2,1,0:T(8,128)(2,1)S(1)} all-to-all(bf16[32,2,256,256]{3,2,1,0:T(8,128)(2,1)S(1)} %get-tuple-element.81), channel_id=1, replica_groups=mesh['gx'=4,'x'=4,'y'=4,'c'=2] {'x','y','c'}, dimensions={0} | all-to-all | bytes 16777216 | tf_op jit(solution)/shard_map/all_to_all | solution.py:271
  351.2 8.5 %galerkin_rows.1 = bf16[8,8,256,256]{3,2,1,0:T(8,128)(2,1)S(1)} custom-call(s32[2,8]{1,0:T(2,128)S(1)} %bitcast.51, s32[4,8]{1,0:T(4,128)S(1)} %bitcast.46, s32[6,2,8]{2,1,0:T(2,128)S(1)} %bitcast.41, s32[2,2,8]{2,1,0:T(2,128)S(1)} %bitcast.52, s32[3]{0:T(128)S(1)} %pad_add_fusion.here, bf16[8,6,256,256]{3,2,1,0:T(8,128)(2,1)S(1)} %bitcast.36, ...), custom_call_target="tpu_custom_call" | custom-call | tf_op jit(solution)/shard_map/galerkin_rows/pallas_call | solution.py:226
  359.8 0.3 slice_bitcast_fusion
  360.1 0.5 collective-permute-start.9
  360.5 0.1 collective-permute-start.8
  360.7 0.4 collective-permute-start.7
  361.0 0.1 collective-permute-start.6
  361.2 1.6 collective-permute-done.9
  362.8 0.3 fusion
  363.1 1.2 collective-permute-done.8
  364.3 0.0 collective-permute-start.10
  364.3 0.3 fusion.1
  364.6 1.2 collective-permute-done.7
  365.8 2.0 collective-permute-start.11
  367.8 0.3 fusion.2
  368.2 0.0 collective-permute-done.6
  368.2 1.3 collective-permute-start.12
  369.4 0.3 fusion.3
  369.8 21.8 %collective-permute-done.10 = bf16[8,256,256]{2,1,0:T(8,128)(2,1)S(1)} collective-permute-done((bf16[8,256,256]{2,1,0:T(8,128)(2,1)S(1)}, bf16[8,256,256]{2,1,0:T(8,128)(2,1)S(1)}, u32[]{:S(2)}, u32[]{:S(2)}) %collective-permute-start.10) | collective-permute-done | bytes 1048608 | tf_op jit(solution)/shard_map/ppermute | solution.py:34
  391.6 0.0 collective-permute-done.11
  391.6 1.5 collective-permute-done.12
  393.0 0.6 add_convert_fusion.1
  393.6 0.6 collective-permute-start.13
  394.2 2.5 collective-permute-start.14
  396.7 1.4 collective-permute-start.15
  398.1 6.0 %collective-permute-done.13 = bf16[2,256,256]{2,1,0:T(8,128)(2,1)S(1)} collective-permute-done((bf16[2,256,256]{2,1,0:T(8,128)(2,1)S(1)}, bf16[2,256,256]{2,1,0:T(8,128)(2,1)S(1)}, u32[]{:S(2)}, u32[]{:S(2)}) %collective-permute-start.13) | collective-permute-done | bytes 262176 | tf_op jit(solution)/shard_map/ppermute | solution.py:34
  404.1 0.0 collective-permute-done.14
  404.1 0.9 collective-permute-done.15
  405.0 0.1 add_convert_fusion
  405.1 0.1 collective-permute-start.16
  405.2 1.3 collective-permute-done.16
  406.6 0.7 pad_maximum_fusion
  (18 shorter events, 0.1 us)
Async XLA Ops:
  0.6 1.6 copy-start
  2.2 0.7 copy-start.7
  2.9 5.9 %copy-start.1 = (bf16[8,2,256,256]{3,2,1,0:T(8,128)(2,1)S(1)}, bf16[8,2,256,256]{3,2,1,0:T(8,128)(2,1)}, u32[]{:S(2)}) copy-start(bf16[8,2,256,256]{3,2,1,0:T(8,128)(2,1)} %own.2) | copy-start | bytes 6291460
  2.9 5.9 %copy-start.9 = (s32[1,32]{1,0:T(1,128)S(1)}, s32[1,32]{1,0:T(1,128)}, u32[]{:S(2)}) copy-start(s32[1,32]{1,0:T(1,128)} %peer.5) | copy-start | bytes 388
  3.5 9.5 %collective-permute-start = (bf16[1,2,256,256]{3,2,1,0:T(8,128)(2,1)S(1)}, bf16[1,2,256,256]{3,2,1,0:T(8,128)(2,1)S(1)}, u32[]{:S(2)}, u32[]{:S(2)}) collective-permute-start(bf16[1,2,256,256]{3,2,1,0:T(8,128)(2,1)S(1)} %get-tuple-element.48), channel_id=1, source_target_pairs={{0,32},{32,64},{64,96},{1,33},{33,65},{65,97},{2,34},{34,66},{66,9... | collective-permute-start | bytes 786440 | tf_op jit(solution)/shard_map/ppermute | solution.py:24
  7.5 9.8 %collective-permute-start.1 = (bf16[1,2,256,256]{3,2,1,0:T(8,128)(2,1)S(1)}, bf16[1,2,256,256]{3,2,1,0:T(8,128)(2,1)S(1)}, u32[]{:S(2)}, u32[]{:S(2)}) collective-permute-start(bf16[1,2,256,256]{3,2,1,0:T(8,128)(2,1)S(1)} %get-tuple-element.49), channel_id=1, source_target_pairs={{32,0},{64,32},{96,64},{33,1},{65,33},{97,65},{34,2},{66,34},{98,6... | collective-permute-start | bytes 786440 | tf_op jit(solution)/shard_map/ppermute | solution.py:24
  8.8 111.1 %slice-start = ((s8[6291456]{0:T(1024)(128)(4,1)}), s8[4194304]{0:T(1024)(128)(4,1)S(1)}, s32[]{:S(2)}) async-start(s8[6291456]{0:T(1024)(128)(4,1)} %bitcast.35), calls=%async_computation.3 | async-start | bytes 8388608
  10.7 109.2 %slice-start.1 = ((s8[6291456]{0:T(1024)(128)(4,1)}), s8[2097152]{0:T(1024)(128)(4,1)S(1)}, s32[]{:S(2)}) async-start(s8[6291456]{0:T(1024)(128)(4,1)} %bitcast.35), calls=%async_computation.4 | async-start | bytes 4194304
  10.7 109.2 %copy-start.2 = (bf16[8,256,256]{2,1,0:T(8,128)(2,1)S(1)}, bf16[8,256,256]{2,1,0:T(8,128)(2,1)}, u32[]{:S(2)}) copy-start(bf16[8,256,256]{2,1,0:T(8,128)(2,1)} %d_buf.5) | copy-start | bytes 3145732
  10.7 109.2 %copy-start.4 = (s32[8,6,2]{0,2,1:T(2,128)S(1)}, s32[8,6,2]{0,2,1:T(2,128)}, u32[]{:S(2)}) copy-start(s32[8,6,2]{0,2,1:T(2,128)} %param.12) | copy-start | bytes 1156
  10.7 109.2 %copy-start.5 = (s32[8,4]{0,1:T(4,128)S(1)}, s32[8,4]{0,1:T(4,128)}, u32[]{:S(2)}) copy-start(s32[8,4]{0,1:T(4,128)} %param.11) | copy-start | bytes 388
  10.7 109.2 %copy-start.6 = (s32[8,2]{0,1:T(2,128)S(1)}, s32[8,2]{0,1:T(2,128)}, u32[]{:S(2)}) copy-start(s32[8,2]{0,1:T(2,128)} %param.10) | copy-start | bytes 196
  10.7 109.2 %copy-start.8 = (s32[1,2]{1,0:T(1,128)S(1)}, s32[1,2]{1,0:T(1,128)}, u32[]{:S(2)}) copy-start(s32[1,2]{1,0:T(1,128)} %slab.5) | copy-start | bytes 28
  122.2 13.6 %collective-permute-start.2 = (bf16[1,2,256,256]{3,2,1,0:T(8,128)(2,1)S(1)}, bf16[1,2,256,256]{3,2,1,0:T(8,128)(2,1)S(1)}, u32[]{:S(2)}, u32[]{:S(2)}) collective-permute-start(bf16[1,2,256,256]{3,2,1,0:T(8,128)(2,1)S(1)} %get-tuple-element.63), channel_id=1, source_target_pairs={{0,32},{32,64},{64,96},{1,33},{33,65},{65,97},{2,34},{34,66},{66,9... | collective-permute-start | bytes 786440 | tf_op jit(solution)/shard_map/ppermute | solution.py:24
  125.9 10.2 %collective-permute-start.3 = (bf16[1,2,256,256]{3,2,1,0:T(8,128)(2,1)S(1)}, bf16[1,2,256,256]{3,2,1,0:T(8,128)(2,1)S(1)}, u32[]{:S(2)}, u32[]{:S(2)}) collective-permute-start(bf16[1,2,256,256]{3,2,1,0:T(8,128)(2,1)S(1)} %get-tuple-element.64), channel_id=1, source_target_pairs={{32,0},{64,32},{96,64},{33,1},{65,33},{97,65},{34,2},{66,34},{98,6... | collective-permute-start | bytes 786440 | tf_op jit(solution)/shard_map/ppermute | solution.py:24
  237.3 13.9 %collective-permute-start.4 = (bf16[1,2,256,256]{3,2,1,0:T(8,128)(2,1)S(1)}, bf16[1,2,256,256]{3,2,1,0:T(8,128)(2,1)S(1)}, u32[]{:S(2)}, u32[]{:S(2)}) collective-permute-start(bf16[1,2,256,256]{3,2,1,0:T(8,128)(2,1)S(1)} %get-tuple-element.79), channel_id=1, source_target_pairs={{0,32},{32,64},{64,96},{1,33},{33,65},{65,97},{2,34},{34,66},{66,9... | collective-permute-start | bytes 786440 | tf_op jit(solution)/shard_map/ppermute | solution.py:24
  241.9 10.2 %collective-permute-start.5 = (bf16[1,2,256,256]{3,2,1,0:T(8,128)(2,1)S(1)}, bf16[1,2,256,256]{3,2,1,0:T(8,128)(2,1)S(1)}, u32[]{:S(2)}, u32[]{:S(2)}) collective-permute-start(bf16[1,2,256,256]{3,2,1,0:T(8,128)(2,1)S(1)} %get-tuple-element.80), channel_id=1, source_target_pairs={{32,0},{64,32},{96,64},{33,1},{65,33},{97,65},{34,2},{66,34},{98,6... | collective-permute-start | bytes 786440 | tf_op jit(solution)/shard_map/ppermute | solution.py:24
  252.1 99.1 %copy-start.3 = (bf16[8,2,256,256]{3,2,1,0:T(8,128)(2,1)S(1)}, bf16[8,2,256,256]{3,2,1,0:T(8,128)(2,1)}, u32[]{:S(2)}) copy-start(bf16[8,2,256,256]{3,2,1,0:T(8,128)(2,1)} %get-tuple-element.46.own) | copy-start | bytes 6291460
  252.1 99.1 %copy-start.10 = (s32[8,2,2]{0,2,1:T(2,128)S(1)}, s32[8,2,2]{0,2,1:T(2,128)}, u32[]{:S(2)}) copy-start(s32[8,2,2]{0,2,1:T(2,128)} %param.17) | copy-start | bytes 388
  360.1 2.7 collective-permute-start.9
  360.5 3.8 collective-permute-start.8
  360.7 5.2 %collective-permute-start.7 = (bf16[8,256,256]{2,1,0:T(8,128)(2,1)S(1)}, bf16[8,256,256]{2,1,0:T(8,128)(2,1)S(1)}, u32[]{:S(2)}, u32[]{:S(2)}) collective-permute-start(bf16[8,256,256]{2,1,0:T(8,128)(2,1)S(1)} %get-tuple-element.96), channel_id=1, source_target_pairs={{0,1},{1,0},{2,3},{3,2},{4,5},{5,4},{6,7},{7,6},{8,9},{9,8},{10,11... | collective-permute-start | bytes 3145736 | tf_op jit(solution)/shard_map/ppermute | solution.py:273
  361.0 7.1 %collective-permute-start.6 = (bf16[8,256,256]{2,1,0:T(8,128)(2,1)S(1)}, bf16[8,256,256]{2,1,0:T(8,128)(2,1)S(1)}, u32[]{:S(2)}, u32[]{:S(2)}) collective-permute-start(bf16[8,256,256]{2,1,0:T(8,128)(2,1)S(1)} %get-tuple-element.97), channel_id=1, source_target_pairs={{0,1},{1,0},{2,3},{3,2},{4,5},{5,4},{6,7},{7,6},{8,9},{9,8},{10,11... | collective-permute-start | bytes 3145736 | tf_op jit(solution)/shard_map/ppermute | solution.py:273
  364.3 27.2 %collective-permute-start.10 = (bf16[8,256,256]{2,1,0:T(8,128)(2,1)S(1)}, bf16[8,256,256]{2,1,0:T(8,128)(2,1)S(1)}, u32[]{:S(2)}, u32[]{:S(2)}) collective-permute-start(bf16[8,256,256]{2,1,0:T(8,128)(2,1)S(1)} %fusion), channel_id=1, source_target_pairs={{0,8},{1,3},{2,10},{3,5},{4,12},{5,7},{6,14},{7,1},{8,16},{9,11},{... | collective-permute-start | bytes 3145736 | tf_op jit(solution)/shard_map/ppermute | solution.py:34
  365.8 25.7 %collective-permute-start.11 = (bf16[8,256,256]{2,1,0:T(8,128)(2,1)S(1)}, bf16[8,256,256]{2,1,0:T(8,128)(2,1)S(1)}, u32[]{:S(2)}, u32[]{:S(2)}) collective-permute-start(bf16[8,256,256]{2,1,0:T(8,128)(2,1)S(1)} %fusion.1), channel_id=1, source_target_pairs={{0,16},{1,5},{2,18},{3,7},{4,20},{5,1},{6,22},{7,3},{8,24},{9,13},... | collective-permute-start | bytes 3145736 | tf_op jit(solution)/shard_map/ppermute | solution.py:34
  368.2 24.9 %collective-permute-start.12 = (bf16[8,256,256]{2,1,0:T(8,128)(2,1)S(1)}, bf16[8,256,256]{2,1,0:T(8,128)(2,1)S(1)}, u32[]{:S(2)}, u32[]{:S(2)}) collective-permute-start(bf16[8,256,256]{2,1,0:T(8,128)(2,1)S(1)} %fusion.2), channel_id=1, source_target_pairs={{0,24},{1,7},{2,26},{3,1},{4,28},{5,3},{6,30},{7,5},{8,0},{9,15},{... | collective-permute-start | bytes 3145736 | tf_op jit(solution)/shard_map/ppermute | solution.py:34
  393.6 10.5 %collective-permute-start.13 = (bf16[2,256,256]{2,1,0:T(8,128)(2,1)S(1)}, bf16[2,256,256]{2,1,0:T(8,128)(2,1)S(1)}, u32[]{:S(2)}, u32[]{:S(2)}) collective-permute-start(bf16[2,256,256]{2,1,0:T(8,128)(2,1)S(1)} %get-tuple-element.91), channel_id=1, source_target_pairs={{0,2},{1,9},{2,4},{3,11},{4,6},{5,13},{6,0},{7,15},{8,10},{9,17},{... | collective-permute-start | bytes 786440 | tf_op jit(solution)/shard_map/ppermute | solution.py:34
  394.2 9.9 %collective-permute-start.14 = (bf16[2,256,256]{2,1,0:T(8,128)(2,1)S(1)}, bf16[2,256,256]{2,1,0:T(8,128)(2,1)S(1)}, u32[]{:S(2)}, u32[]{:S(2)}) collective-permute-start(bf16[2,256,256]{2,1,0:T(8,128)(2,1)S(1)} %get-tuple-element.92), channel_id=1, source_target_pairs={{0,4},{1,17},{2,6},{3,19},{4,0},{5,21},{6,2},{7,23},{8,12},{9,25},... | collective-permute-start | bytes 786440 | tf_op jit(solution)/shard_map/ppermute | solution.py:34
  396.7 8.3 %collective-permute-start.15 = (bf16[2,256,256]{2,1,0:T(8,128)(2,1)S(1)}, bf16[2,256,256]{2,1,0:T(8,128)(2,1)S(1)}, u32[]{:S(2)}, u32[]{:S(2)}) collective-permute-start(bf16[2,256,256]{2,1,0:T(8,128)(2,1)S(1)} %get-tuple-element.93), channel_id=1, source_target_pairs={{0,6},{1,25},{2,0},{3,27},{4,2},{5,29},{6,4},{7,31},{8,14},{9,1},{... | collective-permute-start | bytes 786440 | tf_op jit(solution)/shard_map/ppermute | solution.py:34
  405.1 1.4 collective-permute-start.16

commit v9 on v8

--- a/solution.py
+++ b/solution.py
@@ -58,7 +58,7 @@
         out_specs=[ANY, ANY],
         out_shape=(one, one),
         scratch_shapes=[pltpu.VMEM((2, *rows.shape[1:]), jnp.bfloat16), pltpu.SemaphoreType.DMA((4,))],
-        compiler_params=PARAMS,
+        compiler_params=pltpu.CompilerParams(vmem_limit_bytes=56 << 20),
         name="pick_rows",
     )(slab, rows)
 
@@ -129,7 +129,7 @@
     rhs,
 ):
     for j, out in enumerate((up, down)):
-        for n, value in enumerate(new_row(local, remote, match, slab[0, j], a_buf, d_buf, own, peers, low, high, rhs)):
+        for n, value in enumerate(new_row(local, remote, match, slab[0, j], a_buf, d_buf, own, peers, low, high, rhs.at[0])):
             out[0, n] = value
 
 
@@ -140,11 +140,14 @@
     new, rhs,
     rows_sem, out_sems,
 ):
-    @pl.loop(0, own.shape[0])
-    def _(i):
-        for n, value in enumerate(new_row(local, remote, match, i, a_buf, d_buf, own, peers, low, high, rhs)):
-            new[i, n] = value
-        pltpu.make_async_copy(new.at[i], rows_hbm.at[i], rows_sem.at[0]).start()
+    @pl.loop(0, own.shape[0], step=2)
+    def _(start):
+        for lane in range(2):
+            i = start + lane
+            for n, value in enumerate(new_row(local, remote, match, i, a_buf, d_buf, own, peers, low, high, rhs.at[lane])):
+                new[i, n] = value
+        for lane in range(2):
+            pltpu.make_async_copy(new.at[start + lane], rows_hbm.at[start + lane], rows_sem.at[0]).start()
 
     copies = [pltpu.make_async_copy(new.at[peer[0, q]], out_hbm.at[q], out_sems.at[q]) for q in range(out_hbm.shape[0])]
     for copy in copies:
@@ -155,7 +158,7 @@
 
 
 def operand_scratch(width):
-    return pltpu.VMEM((LINKS * width, BLOCKS * width), jnp.bfloat16)
+    return pltpu.VMEM((2, LINKS * width, BLOCKS * width), jnp.bfloat16)
 
 
 def slab_rows(tables, slab, operator, inverse, rows, received, low, high):
@@ -201,24 +204,26 @@
     width = own.shape[-1]
     sums[...] = jnp.zeros_like(sums)
 
-    @pl.loop(0, own.shape[0])
-    def _(i):
-        image = row_image(local, remote, match, i, a_buf, own, peers, low, high, rhs)
-        mine = jnp.concatenate([own[i, n] for n in range(BLOCKS)], axis=1)
-        partial = lax.dot_general(mine, image, (((0,), (0,)), ((), ())), preferred_element_type=jnp.float32)
-        for n1 in range(BLOCKS):
-            for n2 in range(BLOCKS):
-                slot = slots[n1, n2, i]
-                owner = slot // 2
-                chip = owner // 2
-                dx = (chip // RING - here[0] + RING) % RING
-                dy = (chip % RING - here[1] + RING) % RING
-                second = slot % 2
-                step = jnp.where(second == 0, dx, dy)
-                place = jnp.where(second == 0, dy, dx) * 2 + owner % 2
-                group = jnp.where(second == here[2], 0, RING) + step
-                block = partial[n1 * width : (n1 + 1) * width, n2 * width : (n2 + 1) * width]
-                sums[group, place] = block.astype(jnp.bfloat16)
+    @pl.loop(0, own.shape[0], step=2)
+    def _(start):
+        for lane in range(2):
+            i = start + lane
+            image = row_image(local, remote, match, i, a_buf, own, peers, low, high, rhs.at[lane])
+            mine = jnp.concatenate([own[i, n] for n in range(BLOCKS)], axis=1)
+            partial = lax.dot_general(mine, image, (((0,), (0,)), ((), ())), preferred_element_type=jnp.float32)
+            for n1 in range(BLOCKS):
+                for n2 in range(BLOCKS):
+                    slot = slots[n1, n2, i]
+                    owner = slot // 2
+                    chip = owner // 2
+                    dx = (chip // RING - here[0] + RING) % RING
+                    dy = (chip % RING - here[1] + RING) % RING
+                    second = slot % 2
+                    step = jnp.where(second == 0, dx, dy)
+                    place = jnp.where(second == 0, dy, dx) * 2 + owner % 2
+                    group = jnp.where(second == here[2], 0, RING) + step
+                    block = partial[n1 * width : (n1 + 1) * width, n2 * width : (n2 + 1) * width]
+                    sums[group, place] = block.astype(jnp.bfloat16)
 
 
 def galerkin(tables, slots, here, operator, rows, received, low, high):

time: 409 us -> 408 us (level)
  transfers between devices with their start and end apart: 17 -> 17, of which waited for: 12 -> 12; matrix products, arithmetic and copies ran while one was open for 0% -> 0% of each run, Pallas kernels for 5% -> 4%
where the time goes in v9:
time: 408 us; the launch traced here: 406 us
  blocking collectives  301 us (74%)
  waiting for transfers between devices  44.1 us (11%)
  Pallas kernels  32.8 us (8%)
  starting transfers between devices  24.5 us (6%)
    all_to_all x3, blocking collectives, body(): lax.all_to_all(outgoing, GY, split_axis=0, concat_axis=0, tiled=True)  301 us
    ppermute x6, waiting for transfers between devices, around(): return lax.ppermute(value, GY, pairs)  30.1 us
    pallas_call x2, Pallas kernels, smooth(): pl.pallas_call(smooth_kernel, in_specs=[SMEM] * 4 + [VMEM] * 6, out_specs...  15.9 us
    ppermute x6, starting transfers between devices, shifted(): lax.ppermute(value, axis, [(source, source + steps) for source in range(f...  15.7 us
    ppermute x6, waiting for transfers between devices, shifted(): lax.ppermute(value, axis, [(source, source + steps) for source in range(f...  8.64 us
  transfers between devices with their start and end apart: 17, of which 12 were waited for; matrix products, arithmetic and copies ran while one was open for 0% of the time, Pallas kernels for 4%

profile of v9, /device:TPU:0, one launch (start us, length us, event | category | flops | bytes accessed | tf_op | source)
XLA Modules:
  0.0 406.2 jit_solution(3126395765187689547)
XLA Ops:
  0.6 0.0 copy-start
  0.6 2.6 pick_rows.1
  3.2 3.9 collective-permute-start
  7.2 1.3 collective-permute-start.1
  8.5 0.0 copy-done
  8.5 0.0 copy-done.7
  8.5 0.0 slice-start
  8.5 1.8 pack_rows.1
  10.3 0.1 pad_add_fusion.here
  10.4 0.0 copy-start.5
  10.4 0.0 copy-start.6
  10.4 2.6 collective-permute-done.low
  13.0 4.2 %collective-permute-done.1.high = bf16[1,2,256,256]{3,2,1,0:T(8,128)(2,1)S(1)} collective-permute-done((bf16[1,2,256,256]{3,2,1,0:T(8,128)(2,1)}, bf16[1,2,256,256]{3,2,1,0:T(8,128)(2,1)S(1)}, u32[]{:S(2)}, u32[]{:S(2)}) %collective-permute-start.1) | collective-permute-done | bytes 262176 | tf_op jit(solution)/shard_map/ppermute | solution.py:24
  17.2 102.6 %all_to_all.15.peers = bf16[32,2,256,256]{3,2,1,0:T(8,128)(2,1)S(1)} all-to-all(bf16[32,2,256,256]{3,2,1,0:T(8,128)(2,1)S(1)} %pack_rows.1), channel_id=1, replica_groups=mesh['gx'=4,'x'=4,'y'=4,'c'=2] {'x','y','c'}, dimensions={0} | all-to-all | bytes 16777216 | tf_op jit(solution)/shard_map/all_to_all | solution.py:268
  119.8 0.0 copy-done.1
  119.8 0.0 copy-done.3
  119.8 0.0 copy-done.4
  119.8 0.0 copy-done.5
  119.8 0.0 copy-done.6
  119.8 2.3 slab_rows.2
  122.1 3.7 collective-permute-start.2
  125.8 1.3 collective-permute-start.3
  127.1 8.2 %smooth_rows.2 = (bf16[8,2,256,256]{3,2,1,0:T(8,128)(2,1)S(1)}, bf16[32,2,256,256]{3,2,1,0:T(8,128)(2,1)S(1)}) custom-call(s32[2,8]{1,0:T(2,128)S(1)} %bitcast.48, s32[4,8]{1,0:T(4,128)S(1)} %bitcast.43, s32[6,2,8]{2,1,0:T(2,128)S(1)} %bitcast.38, s32[1,32]{1,0:T(1,128)S(1)} %copy-done.7, bf16[8,6,256,256]{3,2,1,0:T(8,128)(2,1)S(1)} %bitcast.36, ...), custom_call_target="tpu_custom_call" | custom-call | flops 3758096384 | bytes 29360128 | tf_op jit(solution)/shard_map/smooth_rows/pallas_call | solution.py:181
  135.3 0.0 collective-permute-done.2.low
  135.3 0.6 collective-permute-done.3.high
  136.0 99.0 %all_to_all.16.peers = bf16[32,2,256,256]{3,2,1,0:T(8,128)(2,1)S(1)} all-to-all(bf16[32,2,256,256]{3,2,1,0:T(8,128)(2,1)S(1)} %get-tuple-element.65), channel_id=1, replica_groups=mesh['gx'=4,'x'=4,'y'=4,'c'=2] {'x','y','c'}, dimensions={0} | all-to-all | bytes 16777216 | tf_op jit(solution)/shard_map/all_to_all | solution.py:276
  235.0 2.2 slab_rows.3
  237.2 4.2 %collective-permute-start.4 = (bf16[1,2,256,256]{3,2,1,0:T(8,128)(2,1)S(1)}, bf16[1,2,256,256]{3,2,1,0:T(8,128)(2,1)S(1)}, u32[]{:S(2)}, u32[]{:S(2)}) collective-permute-start(bf16[1,2,256,256]{3,2,1,0:T(8,128)(2,1)S(1)} %get-tuple-element.79), channel_id=1, source_target_pairs={{0,32},{32,64},{64,96},{1,33},{33,65},{65,97},{2,34},{34,66},{66,9... | collective-permute-start | bytes 786440 | tf_op jit(solution)/shard_map/ppermute | solution.py:24
  241.4 1.3 collective-permute-start.5
  242.7 7.7 %smooth_rows.3 = (bf16[8,2,256,256]{3,2,1,0:T(8,128)(2,1)}, bf16[32,2,256,256]{3,2,1,0:T(8,128)(2,1)S(1)}) custom-call(s32[2,8]{1,0:T(2,128)S(1)} %bitcast.50, s32[4,8]{1,0:T(4,128)S(1)} %bitcast.45, s32[6,2,8]{2,1,0:T(2,128)S(1)} %bitcast.40, s32[1,32]{1,0:T(1,128)S(1)} %copy-done.7, bf16[8,6,256,256]{3,2,1,0:T(8,128)(2,1)S(1)} %bitcast.36, ...), custom_call_target="tpu_custom_call" | custom-call | flops 3758096384 | bytes 29360128 | tf_op jit(solution)/shard_map/smooth_rows/pallas_call | solution.py:181
  250.4 0.0 collective-permute-done.4.low
  250.4 1.2 collective-permute-done.5.high
  251.6 99.1 %all_to_all.17.peers = bf16[32,2,256,256]{3,2,1,0:T(8,128)(2,1)S(1)} all-to-all(bf16[32,2,256,256]{3,2,1,0:T(8,128)(2,1)S(1)} %get-tuple-element.81), channel_id=1, replica_groups=mesh['gx'=4,'x'=4,'y'=4,'c'=2] {'x','y','c'}, dimensions={0} | all-to-all | bytes 16777216 | tf_op jit(solution)/shard_map/all_to_all | solution.py:276
  350.7 8.1 %galerkin_rows.1 = bf16[8,8,256,256]{3,2,1,0:T(8,128)(2,1)S(1)} custom-call(s32[2,8]{1,0:T(2,128)S(1)} %bitcast.51, s32[4,8]{1,0:T(4,128)S(1)} %bitcast.46, s32[6,2,8]{2,1,0:T(2,128)S(1)} %bitcast.41, s32[2,2,8]{2,1,0:T(2,128)S(1)} %bitcast.52, s32[3]{0:T(128)S(1)} %pad_add_fusion.here, bf16[8,6,256,256]{3,2,1,0:T(8,128)(2,1)S(1)} %bitcast.36, ...), custom_call_target="tpu_custom_call" | custom-call | tf_op jit(solution)/shard_map/galerkin_rows/pallas_call | solution.py:231
  358.8 0.3 slice_bitcast_fusion
  359.1 0.5 collective-permute-start.9
  359.5 0.1 collective-permute-start.8
  359.7 0.4 collective-permute-start.7
  360.1 0.1 collective-permute-start.6
  360.2 1.6 collective-permute-done.9
  361.8 0.3 fusion
  362.1 1.2 collective-permute-done.8
  363.3 0.0 collective-permute-start.10
  363.3 0.3 fusion.1
  363.6 1.2 collective-permute-done.7
  364.8 1.9 collective-permute-start.11
  366.7 0.3 fusion.2
  367.0 0.0 collective-permute-done.6
  367.0 1.3 collective-permute-start.12
  368.3 0.3 fusion.3
  368.6 22.0 %collective-permute-done.10 = bf16[8,256,256]{2,1,0:T(8,128)(2,1)S(1)} collective-permute-done((bf16[8,256,256]{2,1,0:T(8,128)(2,1)S(1)}, bf16[8,256,256]{2,1,0:T(8,128)(2,1)S(1)}, u32[]{:S(2)}, u32[]{:S(2)}) %collective-permute-start.10) | collective-permute-done | bytes 1048608 | tf_op jit(solution)/shard_map/ppermute | solution.py:34
  390.6 0.0 collective-permute-done.11
  390.6 1.3 collective-permute-done.12
  391.9 0.6 add_convert_fusion.1
  392.5 0.6 collective-permute-start.13
  393.1 2.5 collective-permute-start.14
  395.5 1.4 collective-permute-start.15
  397.0 6.0 %collective-permute-done.13 = bf16[2,256,256]{2,1,0:T(8,128)(2,1)S(1)} collective-permute-done((bf16[2,256,256]{2,1,0:T(8,128)(2,1)S(1)}, bf16[2,256,256]{2,1,0:T(8,128)(2,1)S(1)}, u32[]{:S(2)}, u32[]{:S(2)}) %collective-permute-start.13) | collective-permute-done | bytes 262176 | tf_op jit(solution)/shard_map/ppermute | solution.py:34
  402.9 0.0 collective-permute-done.14
  402.9 0.9 collective-permute-done.15
  403.8 0.1 add_convert_fusion
  404.0 0.1 collective-permute-start.16
  404.1 1.3 collective-permute-done.16
  405.4 0.7 pad_maximum_fusion
  (14 shorter events, 0.1 us)
Async XLA Ops:
  0.6 7.8 %copy-start = (bf16[8,2,256,256]{3,2,1,0:T(8,128)(2,1)S(1)}, bf16[8,2,256,256]{3,2,1,0:T(8,128)(2,1)}, u32[]{:S(2)}) copy-start(bf16[8,2,256,256]{3,2,1,0:T(8,128)(2,1)} %own.2) | copy-start | bytes 6291460
  0.6 7.8 %copy-start.7 = (s32[1,32]{1,0:T(1,128)S(1)}, s32[1,32]{1,0:T(1,128)}, u32[]{:S(2)}) copy-start(s32[1,32]{1,0:T(1,128)} %peer.5) | copy-start | bytes 388
  3.2 9.8 %collective-permute-start = (bf16[1,2,256,256]{3,2,1,0:T(8,128)(2,1)}, bf16[1,2,256,256]{3,2,1,0:T(8,128)(2,1)S(1)}, u32[]{:S(2)}, u32[]{:S(2)}) collective-permute-start(bf16[1,2,256,256]{3,2,1,0:T(8,128)(2,1)} %get-tuple-element.48), channel_id=1, source_target_pairs={{0,32},{32,64},{64,96},{1,33},{33,65},{65,97},{2,34},{34,66},{66,9... | collective-permute-start | bytes 786440 | tf_op jit(solution)/shard_map/ppermute | solution.py:24
  7.2 10.0 %collective-permute-start.1 = (bf16[1,2,256,256]{3,2,1,0:T(8,128)(2,1)}, bf16[1,2,256,256]{3,2,1,0:T(8,128)(2,1)S(1)}, u32[]{:S(2)}, u32[]{:S(2)}) collective-permute-start(bf16[1,2,256,256]{3,2,1,0:T(8,128)(2,1)} %get-tuple-element.49), channel_id=1, source_target_pairs={{32,0},{64,32},{96,64},{33,1},{65,33},{97,65},{34,2},{66,34},{98,6... | collective-permute-start | bytes 786440 | tf_op jit(solution)/shard_map/ppermute | solution.py:24
  8.5 111.3 %slice-start = ((s8[6291456]{0:T(1024)(128)(4,1)}), s8[4194304]{0:T(1024)(128)(4,1)S(1)}, s32[]{:S(2)}) async-start(s8[6291456]{0:T(1024)(128)(4,1)} %bitcast.35), calls=%async_computation.3 | async-start | bytes 8388608
  10.4 109.4 %slice-start.1 = ((s8[6291456]{0:T(1024)(128)(4,1)}), s8[2097152]{0:T(1024)(128)(4,1)S(1)}, s32[]{:S(2)}) async-start(s8[6291456]{0:T(1024)(128)(4,1)} %bitcast.35), calls=%async_computation.4 | async-start | bytes 4194304
  10.4 109.4 %copy-start.1 = (bf16[8,256,256]{2,1,0:T(8,128)(2,1)S(1)}, bf16[8,256,256]{2,1,0:T(8,128)(2,1)}, u32[]{:S(2)}) copy-start(bf16[8,256,256]{2,1,0:T(8,128)(2,1)} %d_buf.5) | copy-start | bytes 3145732
  10.4 109.4 %copy-start.3 = (s32[8,6,2]{0,2,1:T(2,128)S(1)}, s32[8,6,2]{0,2,1:T(2,128)}, u32[]{:S(2)}) copy-start(s32[8,6,2]{0,2,1:T(2,128)} %param.12) | copy-start | bytes 1156
  10.4 109.4 %copy-start.4 = (s32[8,4]{0,1:T(4,128)S(1)}, s32[8,4]{0,1:T(4,128)}, u32[]{:S(2)}) copy-start(s32[8,4]{0,1:T(4,128)} %param.11) | copy-start | bytes 388
  10.4 109.4 %copy-start.5 = (s32[8,2]{0,1:T(2,128)S(1)}, s32[8,2]{0,1:T(2,128)}, u32[]{:S(2)}) copy-start(s32[8,2]{0,1:T(2,128)} %param.10) | copy-start | bytes 196
  10.4 109.4 %copy-start.6 = (s32[1,2]{1,0:T(1,128)S(1)}, s32[1,2]{1,0:T(1,128)}, u32[]{:S(2)}) copy-start(s32[1,2]{1,0:T(1,128)} %slab.5) | copy-start | bytes 28
  122.1 13.2 %collective-permute-start.2 = (bf16[1,2,256,256]{3,2,1,0:T(8,128)(2,1)S(1)}, bf16[1,2,256,256]{3,2,1,0:T(8,128)(2,1)S(1)}, u32[]{:S(2)}, u32[]{:S(2)}) collective-permute-start(bf16[1,2,256,256]{3,2,1,0:T(8,128)(2,1)S(1)} %get-tuple-element.63), channel_id=1, source_target_pairs={{0,32},{32,64},{64,96},{1,33},{33,65},{65,97},{2,34},{34,66},{66,9... | collective-permute-start | bytes 786440 | tf_op jit(solution)/shard_map/ppermute | solution.py:24
  125.8 10.2 %collective-permute-start.3 = (bf16[1,2,256,256]{3,2,1,0:T(8,128)(2,1)S(1)}, bf16[1,2,256,256]{3,2,1,0:T(8,128)(2,1)S(1)}, u32[]{:S(2)}, u32[]{:S(2)}) collective-permute-start(bf16[1,2,256,256]{3,2,1,0:T(8,128)(2,1)S(1)} %get-tuple-element.64), channel_id=1, source_target_pairs={{32,0},{64,32},{96,64},{33,1},{65,33},{97,65},{34,2},{66,34},{98,6... | collective-permute-start | bytes 786440 | tf_op jit(solution)/shard_map/ppermute | solution.py:24
  237.2 13.2 %collective-permute-start.4 = (bf16[1,2,256,256]{3,2,1,0:T(8,128)(2,1)S(1)}, bf16[1,2,256,256]{3,2,1,0:T(8,128)(2,1)S(1)}, u32[]{:S(2)}, u32[]{:S(2)}) collective-permute-start(bf16[1,2,256,256]{3,2,1,0:T(8,128)(2,1)S(1)} %get-tuple-element.79), channel_id=1, source_target_pairs={{0,32},{32,64},{64,96},{1,33},{33,65},{65,97},{2,34},{34,66},{66,9... | collective-permute-start | bytes 786440 | tf_op jit(solution)/shard_map/ppermute | solution.py:24
  241.4 10.2 %collective-permute-start.5 = (bf16[1,2,256,256]{3,2,1,0:T(8,128)(2,1)S(1)}, bf16[1,2,256,256]{3,2,1,0:T(8,128)(2,1)S(1)}, u32[]{:S(2)}, u32[]{:S(2)}) collective-permute-start(bf16[1,2,256,256]{3,2,1,0:T(8,128)(2,1)S(1)} %get-tuple-element.80), channel_id=1, source_target_pairs={{32,0},{64,32},{96,64},{33,1},{65,33},{97,65},{34,2},{66,34},{98,6... | collective-permute-start | bytes 786440 | tf_op jit(solution)/shard_map/ppermute | solution.py:24
  251.6 99.1 %copy-start.2 = (bf16[8,2,256,256]{3,2,1,0:T(8,128)(2,1)S(1)}, bf16[8,2,256,256]{3,2,1,0:T(8,128)(2,1)}, u32[]{:S(2)}) copy-start(bf16[8,2,256,256]{3,2,1,0:T(8,128)(2,1)} %get-tuple-element.46.own) | copy-start | bytes 6291460
  251.6 99.1 %copy-start.8 = (s32[8,2,2]{0,2,1:T(2,128)S(1)}, s32[8,2,2]{0,2,1:T(2,128)}, u32[]{:S(2)}) copy-start(s32[8,2,2]{0,2,1:T(2,128)} %param.17) | copy-start | bytes 388
  359.1 2.7 collective-permute-start.9
  359.5 3.8 collective-permute-start.8
  359.7 5.2 %collective-permute-start.7 = (bf16[8,256,256]{2,1,0:T(8,128)(2,1)S(1)}, bf16[8,256,256]{2,1,0:T(8,128)(2,1)S(1)}, u32[]{:S(2)}, u32[]{:S(2)}) collective-permute-start(bf16[8,256,256]{2,1,0:T(8,128)(2,1)S(1)} %get-tuple-element.96), channel_id=1, source_target_pairs={{0,1},{1,0},{2,3},{3,2},{4,5},{5,4},{6,7},{7,6},{8,9},{9,8},{10,11... | collective-permute-start | bytes 3145736 | tf_op jit(solution)/shard_map/ppermute | solution.py:278
  360.1 7.0 %collective-permute-start.6 = (bf16[8,256,256]{2,1,0:T(8,128)(2,1)S(1)}, bf16[8,256,256]{2,1,0:T(8,128)(2,1)S(1)}, u32[]{:S(2)}, u32[]{:S(2)}) collective-permute-start(bf16[8,256,256]{2,1,0:T(8,128)(2,1)S(1)} %get-tuple-element.97), channel_id=1, source_target_pairs={{0,1},{1,0},{2,3},{3,2},{4,5},{5,4},{6,7},{7,6},{8,9},{9,8},{10,11... | collective-permute-start | bytes 3145736 | tf_op jit(solution)/shard_map/ppermute | solution.py:278
  363.3 27.2 %collective-permute-start.10 = (bf16[8,256,256]{2,1,0:T(8,128)(2,1)S(1)}, bf16[8,256,256]{2,1,0:T(8,128)(2,1)S(1)}, u32[]{:S(2)}, u32[]{:S(2)}) collective-permute-start(bf16[8,256,256]{2,1,0:T(8,128)(2,1)S(1)} %fusion), channel_id=1, source_target_pairs={{0,8},{1,3},{2,10},{3,5},{4,12},{5,7},{6,14},{7,1},{8,16},{9,11},{... | collective-permute-start | bytes 3145736 | tf_op jit(solution)/shard_map/ppermute | solution.py:34
  364.8 25.7 %collective-permute-start.11 = (bf16[8,256,256]{2,1,0:T(8,128)(2,1)S(1)}, bf16[8,256,256]{2,1,0:T(8,128)(2,1)S(1)}, u32[]{:S(2)}, u32[]{:S(2)}) collective-permute-start(bf16[8,256,256]{2,1,0:T(8,128)(2,1)S(1)} %fusion.1), channel_id=1, source_target_pairs={{0,16},{1,5},{2,18},{3,7},{4,20},{5,1},{6,22},{7,3},{8,24},{9,13},... | collective-permute-start | bytes 3145736 | tf_op jit(solution)/shard_map/ppermute | solution.py:34
  367.0 24.9 %collective-permute-start.12 = (bf16[8,256,256]{2,1,0:T(8,128)(2,1)S(1)}, bf16[8,256,256]{2,1,0:T(8,128)(2,1)S(1)}, u32[]{:S(2)}, u32[]{:S(2)}) collective-permute-start(bf16[8,256,256]{2,1,0:T(8,128)(2,1)S(1)} %fusion.2), channel_id=1, source_target_pairs={{0,24},{1,7},{2,26},{3,1},{4,28},{5,3},{6,30},{7,5},{8,0},{9,15},{... | collective-permute-start | bytes 3145736 | tf_op jit(solution)/shard_map/ppermute | solution.py:34
  392.5 10.5 %collective-permute-start.13 = (bf16[2,256,256]{2,1,0:T(8,128)(2,1)S(1)}, bf16[2,256,256]{2,1,0:T(8,128)(2,1)S(1)}, u32[]{:S(2)}, u32[]{:S(2)}) collective-permute-start(bf16[2,256,256]{2,1,0:T(8,128)(2,1)S(1)} %get-tuple-element.91), channel_id=1, source_target_pairs={{0,2},{1,9},{2,4},{3,11},{4,6},{5,13},{6,0},{7,15},{8,10},{9,17},{... | collective-permute-start | bytes 786440 | tf_op jit(solution)/shard_map/ppermute | solution.py:34
  393.1 9.9 %collective-permute-start.14 = (bf16[2,256,256]{2,1,0:T(8,128)(2,1)S(1)}, bf16[2,256,256]{2,1,0:T(8,128)(2,1)S(1)}, u32[]{:S(2)}, u32[]{:S(2)}) collective-permute-start(bf16[2,256,256]{2,1,0:T(8,128)(2,1)S(1)} %get-tuple-element.92), channel_id=1, source_target_pairs={{0,4},{1,17},{2,6},{3,19},{4,0},{5,21},{6,2},{7,23},{8,12},{9,25},... | collective-permute-start | bytes 786440 | tf_op jit(solution)/shard_map/ppermute | solution.py:34
  395.5 8.3 %collective-permute-start.15 = (bf16[2,256,256]{2,1,0:T(8,128)(2,1)S(1)}, bf16[2,256,256]{2,1,0:T(8,128)(2,1)S(1)}, u32[]{:S(2)}, u32[]{:S(2)}) collective-permute-start(bf16[2,256,256]{2,1,0:T(8,128)(2,1)S(1)} %get-tuple-element.93), channel_id=1, source_target_pairs={{0,6},{1,25},{2,0},{3,27},{4,2},{5,29},{6,4},{7,31},{8,14},{9,1},{... | collective-permute-start | bytes 786440 | tf_op jit(solution)/shard_map/ppermute | solution.py:34
  404.0 1.4 collective-permute-start.16

commit v10 on v9

--- a/solution.py
+++ b/solution.py
@@ -278,7 +278,7 @@
     others = [lax.ppermute(sums[RING + j], "c", [(0, 1), (1, 0)]) for j in range(RING)]
     parts = [None] * RING
     ready = None
-    for j in (1, 2, 3, 0):
+    for j in (2, 1, 3, 0):
         other = others[j]
         if ready is not None:
             other, parts[ready] = lax.optimization_barrier((other, parts[ready]))

time: 408 us -> 407 us (level)
  transfers between devices with their start and end apart: 17 -> 17, of which waited for: 12 -> 11; matrix products, arithmetic and copies ran while one was open for 0% -> 0% of each run, Pallas kernels for 4% -> 4%
where the time goes in v10:
time: 407 us; the launch traced here: 405 us
  blocking collectives  301 us (74%)
  waiting for transfers between devices  41.4 us (10%)
  Pallas kernels  32.8 us (8%)
  starting transfers between devices  26.3 us (6%)
    all_to_all x3, blocking collectives, body(): lax.all_to_all(outgoing, GY, split_axis=0, concat_axis=0, tiled=True)  301 us
    ppermute x6, waiting for transfers between devices, around(): return lax.ppermute(value, GY, pairs)  28.5 us
    pallas_call x2, Pallas kernels, smooth(): pl.pallas_call(smooth_kernel, in_specs=[SMEM] * 4 + [VMEM] * 6, out_specs...  15.9 us
    ppermute x6, starting transfers between devices, shifted(): lax.ppermute(value, axis, [(source, source + steps) for source in range(f...  15.7 us
    ppermute x6, starting transfers between devices, around(): return lax.ppermute(value, GY, pairs)  9.41 us
    ppermute x6, waiting for transfers between devices, shifted(): lax.ppermute(value, axis, [(source, source + steps) for source in range(f...  8.65 us
  transfers between devices with their start and end apart: 17, of which 11 were waited for; matrix products, arithmetic and copies ran while one was open for 0% of the time, Pallas kernels for 4%

profile of v10, /device:TPU:0, one launch (start us, length us, event | category | flops | bytes accessed | tf_op | source)
XLA Modules:
  0.0 405.2 jit_solution(17691636780302811242)
XLA Ops:
  0.6 0.0 copy-start
  0.6 0.0 copy-start.7
  0.6 2.6 pick_rows.1
  3.2 3.9 collective-permute-start
  7.2 1.3 collective-permute-start.1
  8.5 0.0 copy-done
  8.5 0.0 copy-done.7
  8.5 0.0 slice-start
  8.5 1.8 pack_rows.1
  10.3 0.1 pad_add_fusion.here
  10.4 0.0 copy-start.5
  10.4 0.0 copy-start.6
  10.4 2.6 collective-permute-done.low
  13.0 4.2 %collective-permute-done.1.high = bf16[1,2,256,256]{3,2,1,0:T(8,128)(2,1)S(1)} collective-permute-done((bf16[1,2,256,256]{3,2,1,0:T(8,128)(2,1)}, bf16[1,2,256,256]{3,2,1,0:T(8,128)(2,1)S(1)}, u32[]{:S(2)}, u32[]{:S(2)}) %collective-permute-start.1) | collective-permute-done | bytes 262176 | tf_op jit(solution)/shard_map/ppermute | solution.py:24
  17.2 102.6 %all_to_all.15.peers = bf16[32,2,256,256]{3,2,1,0:T(8,128)(2,1)S(1)} all-to-all(bf16[32,2,256,256]{3,2,1,0:T(8,128)(2,1)S(1)} %pack_rows.1), channel_id=1, replica_groups=mesh['gx'=4,'x'=4,'y'=4,'c'=2] {'x','y','c'}, dimensions={0} | all-to-all | bytes 16777216 | tf_op jit(solution)/shard_map/all_to_all | solution.py:268
  119.8 0.0 slice-done
  119.8 0.0 slice-done.1
  119.8 0.0 copy-done.1
  119.8 2.3 slab_rows.2
  122.1 3.7 collective-permute-start.2
  125.8 1.3 collective-permute-start.3
  127.1 8.2 %smooth_rows.2 = (bf16[8,2,256,256]{3,2,1,0:T(8,128)(2,1)S(1)}, bf16[32,2,256,256]{3,2,1,0:T(8,128)(2,1)S(1)}) custom-call(s32[2,8]{1,0:T(2,128)S(1)} %bitcast.48, s32[4,8]{1,0:T(4,128)S(1)} %bitcast.43, s32[6,2,8]{2,1,0:T(2,128)S(1)} %bitcast.38, s32[1,32]{1,0:T(1,128)S(1)} %copy-done.7, bf16[8,6,256,256]{3,2,1,0:T(8,128)(2,1)S(1)} %bitcast.36, ...), custom_call_target="tpu_custom_call" | custom-call | flops 3758096384 | bytes 29360128 | tf_op jit(solution)/shard_map/smooth_rows/pallas_call | solution.py:181
  135.3 0.0 collective-permute-done.2.low
  135.3 0.7 collective-permute-done.3.high
  136.0 99.0 %all_to_all.16.peers = bf16[32,2,256,256]{3,2,1,0:T(8,128)(2,1)S(1)} all-to-all(bf16[32,2,256,256]{3,2,1,0:T(8,128)(2,1)S(1)} %get-tuple-element.65), channel_id=1, replica_groups=mesh['gx'=4,'x'=4,'y'=4,'c'=2] {'x','y','c'}, dimensions={0} | all-to-all | bytes 16777216 | tf_op jit(solution)/shard_map/all_to_all | solution.py:276
  235.0 2.2 slab_rows.3
  237.2 4.2 %collective-permute-start.4 = (bf16[1,2,256,256]{3,2,1,0:T(8,128)(2,1)S(1)}, bf16[1,2,256,256]{3,2,1,0:T(8,128)(2,1)S(1)}, u32[]{:S(2)}, u32[]{:S(2)}) collective-permute-start(bf16[1,2,256,256]{3,2,1,0:T(8,128)(2,1)S(1)} %get-tuple-element.79), channel_id=1, source_target_pairs={{0,32},{32,64},{64,96},{1,33},{33,65},{65,97},{2,34},{34,66},{66,9... | collective-permute-start | bytes 786440 | tf_op jit(solution)/shard_map/ppermute | solution.py:24
  241.4 1.3 collective-permute-start.5
  242.7 7.7 %smooth_rows.3 = (bf16[8,2,256,256]{3,2,1,0:T(8,128)(2,1)}, bf16[32,2,256,256]{3,2,1,0:T(8,128)(2,1)S(1)}) custom-call(s32[2,8]{1,0:T(2,128)S(1)} %bitcast.50, s32[4,8]{1,0:T(4,128)S(1)} %bitcast.45, s32[6,2,8]{2,1,0:T(2,128)S(1)} %bitcast.40, s32[1,32]{1,0:T(1,128)S(1)} %copy-done.7, bf16[8,6,256,256]{3,2,1,0:T(8,128)(2,1)S(1)} %bitcast.36, ...), custom_call_target="tpu_custom_call" | custom-call | flops 3758096384 | bytes 29360128 | tf_op jit(solution)/shard_map/smooth_rows/pallas_call | solution.py:181
  250.4 0.0 collective-permute-done.4.low
  250.4 1.2 collective-permute-done.5.high
  251.6 99.1 %all_to_all.17.peers = bf16[32,2,256,256]{3,2,1,0:T(8,128)(2,1)S(1)} all-to-all(bf16[32,2,256,256]{3,2,1,0:T(8,128)(2,1)S(1)} %get-tuple-element.81), channel_id=1, replica_groups=mesh['gx'=4,'x'=4,'y'=4,'c'=2] {'x','y','c'}, dimensions={0} | all-to-all | bytes 16777216 | tf_op jit(solution)/shard_map/all_to_all | solution.py:276
  350.7 0.0 copy-done.2
  350.7 8.1 %galerkin_rows.1 = bf16[8,8,256,256]{3,2,1,0:T(8,128)(2,1)S(1)} custom-call(s32[2,8]{1,0:T(2,128)S(1)} %bitcast.51, s32[4,8]{1,0:T(4,128)S(1)} %bitcast.46, s32[6,2,8]{2,1,0:T(2,128)S(1)} %bitcast.41, s32[2,2,8]{2,1,0:T(2,128)S(1)} %bitcast.52, s32[3]{0:T(128)S(1)} %pad_add_fusion.here, bf16[8,6,256,256]{3,2,1,0:T(8,128)(2,1)S(1)} %bitcast.36, ...), custom_call_target="tpu_custom_call" | custom-call | tf_op jit(solution)/shard_map/galerkin_rows/pallas_call | solution.py:231
  358.8 0.3 slice_bitcast_fusion
  359.1 0.5 collective-permute-start.9
  359.5 0.1 collective-permute-start.8
  359.7 0.4 collective-permute-start.7
  360.1 0.1 collective-permute-start.6
  360.2 1.6 collective-permute-done.9
  361.8 0.3 fusion
  362.1 1.2 collective-permute-done.8
  363.3 1.5 collective-permute-start.11
  364.9 0.3 fusion.1
  365.2 0.0 collective-permute-done.7
  365.2 0.9 collective-permute-start.10
  366.1 0.3 fusion.2
  366.4 0.0 collective-permute-done.6
  366.4 2.5 collective-permute-start.12
  368.9 0.3 fusion.3
  369.2 10.5 %collective-permute-done.11 = bf16[8,256,256]{2,1,0:T(8,128)(2,1)S(1)} collective-permute-done((bf16[8,256,256]{2,1,0:T(8,128)(2,1)S(1)}, bf16[8,256,256]{2,1,0:T(8,128)(2,1)S(1)}, u32[]{:S(2)}, u32[]{:S(2)}) %collective-permute-start.11) | collective-permute-done | bytes 1048608 | tf_op jit(solution)/shard_map/ppermute | solution.py:34
  379.7 11.1 %collective-permute-done.10 = bf16[8,256,256]{2,1,0:T(8,128)(2,1)S(1)} collective-permute-done((bf16[8,256,256]{2,1,0:T(8,128)(2,1)S(1)}, bf16[8,256,256]{2,1,0:T(8,128)(2,1)S(1)}, u32[]{:S(2)}, u32[]{:S(2)}) %collective-permute-start.10) | collective-permute-done | bytes 1048608 | tf_op jit(solution)/shard_map/ppermute | solution.py:34
  390.9 0.0 collective-permute-done.12
  390.9 0.6 add_convert_fusion.1
  391.5 0.6 collective-permute-start.13
  392.0 2.4 collective-permute-start.14
  394.5 1.4 collective-permute-start.15
  395.9 6.0 %collective-permute-done.13 = bf16[2,256,256]{2,1,0:T(8,128)(2,1)S(1)} collective-permute-done((bf16[2,256,256]{2,1,0:T(8,128)(2,1)S(1)}, bf16[2,256,256]{2,1,0:T(8,128)(2,1)S(1)}, u32[]{:S(2)}, u32[]{:S(2)}) %collective-permute-start.13) | collective-permute-done | bytes 262176 | tf_op jit(solution)/shard_map/ppermute | solution.py:34
  401.9 0.0 collective-permute-done.14
  401.9 0.9 collective-permute-done.15
  402.8 0.1 add_convert_fusion
  403.0 0.1 collective-permute-start.16
  403.1 1.3 collective-permute-done.16
  404.4 0.7 pad_maximum_fusion
  (14 shorter events, 0.1 us)
Async XLA Ops:
  0.6 7.8 %copy-start = (bf16[8,2,256,256]{3,2,1,0:T(8,128)(2,1)S(1)}, bf16[8,2,256,256]{3,2,1,0:T(8,128)(2,1)}, u32[]{:S(2)}) copy-start(bf16[8,2,256,256]{3,2,1,0:T(8,128)(2,1)} %own.2) | copy-start | bytes 6291460
  0.6 7.8 %copy-start.7 = (s32[1,32]{1,0:T(1,128)S(1)}, s32[1,32]{1,0:T(1,128)}, u32[]{:S(2)}) copy-start(s32[1,32]{1,0:T(1,128)} %peer.5) | copy-start | bytes 388
  3.2 9.8 %collective-permute-start = (bf16[1,2,256,256]{3,2,1,0:T(8,128)(2,1)}, bf16[1,2,256,256]{3,2,1,0:T(8,128)(2,1)S(1)}, u32[]{:S(2)}, u32[]{:S(2)}) collective-permute-start(bf16[1,2,256,256]{3,2,1,0:T(8,128)(2,1)} %get-tuple-element.48), channel_id=1, source_target_pairs={{0,32},{32,64},{64,96},{1,33},{33,65},{65,97},{2,34},{34,66},{66,9... | collective-permute-start | bytes 786440 | tf_op jit(solution)/shard_map/ppermute | solution.py:24
  7.2 10.0 %collective-permute-start.1 = (bf16[1,2,256,256]{3,2,1,0:T(8,128)(2,1)}, bf16[1,2,256,256]{3,2,1,0:T(8,128)(2,1)S(1)}, u32[]{:S(2)}, u32[]{:S(2)}) collective-permute-start(bf16[1,2,256,256]{3,2,1,0:T(8,128)(2,1)} %get-tuple-element.49), channel_id=1, source_target_pairs={{32,0},{64,32},{96,64},{33,1},{65,33},{97,65},{34,2},{66,34},{98,6... | collective-permute-start | bytes 786440 | tf_op jit(solution)/shard_map/ppermute | solution.py:24
  8.5 111.3 %slice-start = ((s8[6291456]{0:T(1024)(128)(4,1)}), s8[4194304]{0:T(1024)(128)(4,1)S(1)}, s32[]{:S(2)}) async-start(s8[6291456]{0:T(1024)(128)(4,1)} %bitcast.35), calls=%async_computation.3 | async-start | bytes 8388608
  10.4 109.4 %slice-start.1 = ((s8[6291456]{0:T(1024)(128)(4,1)}), s8[2097152]{0:T(1024)(128)(4,1)S(1)}, s32[]{:S(2)}) async-start(s8[6291456]{0:T(1024)(128)(4,1)} %bitcast.35), calls=%async_computation.4 | async-start | bytes 4194304
  10.4 109.4 %copy-start.1 = (bf16[8,256,256]{2,1,0:T(8,128)(2,1)S(1)}, bf16[8,256,256]{2,1,0:T(8,128)(2,1)}, u32[]{:S(2)}) copy-start(bf16[8,256,256]{2,1,0:T(8,128)(2,1)} %d_buf.5) | copy-start | bytes 3145732
  10.4 109.4 %copy-start.3 = (s32[8,6,2]{0,2,1:T(2,128)S(1)}, s32[8,6,2]{0,2,1:T(2,128)}, u32[]{:S(2)}) copy-start(s32[8,6,2]{0,2,1:T(2,128)} %param.12) | copy-start | bytes 1156
  10.4 109.4 %copy-start.4 = (s32[8,4]{0,1:T(4,128)S(1)}, s32[8,4]{0,1:T(4,128)}, u32[]{:S(2)}) copy-start(s32[8,4]{0,1:T(4,128)} %param.11) | copy-start | bytes 388
  10.4 109.4 %copy-start.5 = (s32[8,2]{0,1:T(2,128)S(1)}, s32[8,2]{0,1:T(2,128)}, u32[]{:S(2)}) copy-start(s32[8,2]{0,1:T(2,128)} %param.10) | copy-start | bytes 196
  10.4 109.4 %copy-start.6 = (s32[1,2]{1,0:T(1,128)S(1)}, s32[1,2]{1,0:T(1,128)}, u32[]{:S(2)}) copy-start(s32[1,2]{1,0:T(1,128)} %slab.5) | copy-start | bytes 28
  122.1 13.2 %collective-permute-start.2 = (bf16[1,2,256,256]{3,2,1,0:T(8,128)(2,1)S(1)}, bf16[1,2,256,256]{3,2,1,0:T(8,128)(2,1)S(1)}, u32[]{:S(2)}, u32[]{:S(2)}) collective-permute-start(bf16[1,2,256,256]{3,2,1,0:T(8,128)(2,1)S(1)} %get-tuple-element.63), channel_id=1, source_target_pairs={{0,32},{32,64},{64,96},{1,33},{33,65},{65,97},{2,34},{34,66},{66,9... | collective-permute-start | bytes 786440 | tf_op jit(solution)/shard_map/ppermute | solution.py:24
  125.8 10.2 %collective-permute-start.3 = (bf16[1,2,256,256]{3,2,1,0:T(8,128)(2,1)S(1)}, bf16[1,2,256,256]{3,2,1,0:T(8,128)(2,1)S(1)}, u32[]{:S(2)}, u32[]{:S(2)}) collective-permute-start(bf16[1,2,256,256]{3,2,1,0:T(8,128)(2,1)S(1)} %get-tuple-element.64), channel_id=1, source_target_pairs={{32,0},{64,32},{96,64},{33,1},{65,33},{97,65},{34,2},{66,34},{98,6... | collective-permute-start | bytes 786440 | tf_op jit(solution)/shard_map/ppermute | solution.py:24
  237.2 13.2 %collective-permute-start.4 = (bf16[1,2,256,256]{3,2,1,0:T(8,128)(2,1)S(1)}, bf16[1,2,256,256]{3,2,1,0:T(8,128)(2,1)S(1)}, u32[]{:S(2)}, u32[]{:S(2)}) collective-permute-start(bf16[1,2,256,256]{3,2,1,0:T(8,128)(2,1)S(1)} %get-tuple-element.79), channel_id=1, source_target_pairs={{0,32},{32,64},{64,96},{1,33},{33,65},{65,97},{2,34},{34,66},{66,9... | collective-permute-start | bytes 786440 | tf_op jit(solution)/shard_map/ppermute | solution.py:24
  241.4 10.2 %collective-permute-start.5 = (bf16[1,2,256,256]{3,2,1,0:T(8,128)(2,1)S(1)}, bf16[1,2,256,256]{3,2,1,0:T(8,128)(2,1)S(1)}, u32[]{:S(2)}, u32[]{:S(2)}) collective-permute-start(bf16[1,2,256,256]{3,2,1,0:T(8,128)(2,1)S(1)} %get-tuple-element.80), channel_id=1, source_target_pairs={{32,0},{64,32},{96,64},{33,1},{65,33},{97,65},{34,2},{66,34},{98,6... | collective-permute-start | bytes 786440 | tf_op jit(solution)/shard_map/ppermute | solution.py:24
  251.6 99.1 %copy-start.2 = (bf16[8,2,256,256]{3,2,1,0:T(8,128)(2,1)S(1)}, bf16[8,2,256,256]{3,2,1,0:T(8,128)(2,1)}, u32[]{:S(2)}) copy-start(bf16[8,2,256,256]{3,2,1,0:T(8,128)(2,1)} %get-tuple-element.46.own) | copy-start | bytes 6291460
  251.6 99.1 %copy-start.8 = (s32[8,2,2]{0,2,1:T(2,128)S(1)}, s32[8,2,2]{0,2,1:T(2,128)}, u32[]{:S(2)}) copy-start(s32[8,2,2]{0,2,1:T(2,128)} %param.17) | copy-start | bytes 388
  359.1 2.7 collective-permute-start.9
  359.5 3.8 collective-permute-start.8
  359.7 5.5 %collective-permute-start.7 = (bf16[8,256,256]{2,1,0:T(8,128)(2,1)S(1)}, bf16[8,256,256]{2,1,0:T(8,128)(2,1)S(1)}, u32[]{:S(2)}, u32[]{:S(2)}) collective-permute-start(bf16[8,256,256]{2,1,0:T(8,128)(2,1)S(1)} %get-tuple-element.96), channel_id=1, source_target_pairs={{0,1},{1,0},{2,3},{3,2},{4,5},{5,4},{6,7},{7,6},{8,9},{9,8},{10,11... | collective-permute-start | bytes 3145736 | tf_op jit(solution)/shard_map/ppermute | solution.py:278
  360.1 6.3 %collective-permute-start.6 = (bf16[8,256,256]{2,1,0:T(8,128)(2,1)S(1)}, bf16[8,256,256]{2,1,0:T(8,128)(2,1)S(1)}, u32[]{:S(2)}, u32[]{:S(2)}) collective-permute-start(bf16[8,256,256]{2,1,0:T(8,128)(2,1)S(1)} %get-tuple-element.97), channel_id=1, source_target_pairs={{0,1},{1,0},{2,3},{3,2},{4,5},{5,4},{6,7},{7,6},{8,9},{9,8},{10,11... | collective-permute-start | bytes 3145736 | tf_op jit(solution)/shard_map/ppermute | solution.py:278
  363.3 16.4 %collective-permute-start.11 = (bf16[8,256,256]{2,1,0:T(8,128)(2,1)S(1)}, bf16[8,256,256]{2,1,0:T(8,128)(2,1)S(1)}, u32[]{:S(2)}, u32[]{:S(2)}) collective-permute-start(bf16[8,256,256]{2,1,0:T(8,128)(2,1)S(1)} %fusion), channel_id=1, source_target_pairs={{0,16},{1,5},{2,18},{3,7},{4,20},{5,1},{6,22},{7,3},{8,24},{9,13},... | collective-permute-start | bytes 3145736 | tf_op jit(solution)/shard_map/ppermute | solution.py:34
  365.2 25.7 %collective-permute-start.10 = (bf16[8,256,256]{2,1,0:T(8,128)(2,1)S(1)}, bf16[8,256,256]{2,1,0:T(8,128)(2,1)S(1)}, u32[]{:S(2)}, u32[]{:S(2)}) collective-permute-start(bf16[8,256,256]{2,1,0:T(8,128)(2,1)S(1)} %fusion.1), channel_id=1, source_target_pairs={{0,8},{1,3},{2,10},{3,5},{4,12},{5,7},{6,14},{7,1},{8,16},{9,11},{... | collective-permute-start | bytes 3145736 | tf_op jit(solution)/shard_map/ppermute | solution.py:34
  366.4 24.5 %collective-permute-start.12 = (bf16[8,256,256]{2,1,0:T(8,128)(2,1)S(1)}, bf16[8,256,256]{2,1,0:T(8,128)(2,1)S(1)}, u32[]{:S(2)}, u32[]{:S(2)}) collective-permute-start(bf16[8,256,256]{2,1,0:T(8,128)(2,1)S(1)} %fusion.2), channel_id=1, source_target_pairs={{0,24},{1,7},{2,26},{3,1},{4,28},{5,3},{6,30},{7,5},{8,0},{9,15},{... | collective-permute-start | bytes 3145736 | tf_op jit(solution)/shard_map/ppermute | solution.py:34
  391.5 10.5 %collective-permute-start.13 = (bf16[2,256,256]{2,1,0:T(8,128)(2,1)S(1)}, bf16[2,256,256]{2,1,0:T(8,128)(2,1)S(1)}, u32[]{:S(2)}, u32[]{:S(2)}) collective-permute-start(bf16[2,256,256]{2,1,0:T(8,128)(2,1)S(1)} %get-tuple-element.91), channel_id=1, source_target_pairs={{0,2},{1,9},{2,4},{3,11},{4,6},{5,13},{6,0},{7,15},{8,10},{9,17},{... | collective-permute-start | bytes 786440 | tf_op jit(solution)/shard_map/ppermute | solution.py:34
  392.0 9.9 %collective-permute-start.14 = (bf16[2,256,256]{2,1,0:T(8,128)(2,1)S(1)}, bf16[2,256,256]{2,1,0:T(8,128)(2,1)S(1)}, u32[]{:S(2)}, u32[]{:S(2)}) collective-permute-start(bf16[2,256,256]{2,1,0:T(8,128)(2,1)S(1)} %get-tuple-element.92), channel_id=1, source_target_pairs={{0,4},{1,17},{2,6},{3,19},{4,0},{5,21},{6,2},{7,23},{8,12},{9,25},... | collective-permute-start | bytes 786440 | tf_op jit(solution)/shard_map/ppermute | solution.py:34
  394.5 8.3 %collective-permute-start.15 = (bf16[2,256,256]{2,1,0:T(8,128)(2,1)S(1)}, bf16[2,256,256]{2,1,0:T(8,128)(2,1)S(1)}, u32[]{:S(2)}, u32[]{:S(2)}) collective-permute-start(bf16[2,256,256]{2,1,0:T(8,128)(2,1)S(1)} %get-tuple-element.93), channel_id=1, source_target_pairs={{0,6},{1,25},{2,0},{3,27},{4,2},{5,29},{6,4},{7,31},{8,14},{9,1},{... | collective-permute-start | bytes 786440 | tf_op jit(solution)/shard_map/ppermute | solution.py:34
  403.0 1.4 collective-permute-start.16

commit v11 on v10

--- a/solution.py
+++ b/solution.py
@@ -129,7 +129,7 @@
     rhs,
 ):
     for j, out in enumerate((up, down)):
-        for n, value in enumerate(new_row(local, remote, match, slab[0, j], a_buf, d_buf, own, peers, low, high, rhs.at[0])):
+        for n, value in enumerate(new_row(local, remote, match, slab[0, j], a_buf, d_buf, own, peers, low, high, rhs.at[j])):
             out[0, n] = value
 
 
@@ -140,13 +140,13 @@
     new, rhs,
     rows_sem, out_sems,
 ):
-    @pl.loop(0, own.shape[0], step=2)
+    @pl.loop(0, own.shape[0], step=4)
     def _(start):
-        for lane in range(2):
+        for lane in range(4):
             i = start + lane
             for n, value in enumerate(new_row(local, remote, match, i, a_buf, d_buf, own, peers, low, high, rhs.at[lane])):
                 new[i, n] = value
-        for lane in range(2):
+        for lane in range(4):
             pltpu.make_async_copy(new.at[start + lane], rows_hbm.at[start + lane], rows_sem.at[0]).start()
 
     copies = [pltpu.make_async_copy(new.at[peer[0, q]], out_hbm.at[q], out_sems.at[q]) for q in range(out_hbm.shape[0])]
@@ -158,7 +158,7 @@
 
 
 def operand_scratch(width):
-    return pltpu.VMEM((2, LINKS * width, BLOCKS * width), jnp.bfloat16)
+    return pltpu.VMEM((4, LINKS * width, BLOCKS * width), jnp.bfloat16)
 
 
 def slab_rows(tables, slab, operator, inverse, rows, received, low, high):
@@ -204,9 +204,9 @@
     width = own.shape[-1]
     sums[...] = jnp.zeros_like(sums)
 
-    @pl.loop(0, own.shape[0], step=2)
+    @pl.loop(0, own.shape[0], step=4)
     def _(start):
-        for lane in range(2):
+        for lane in range(4):
             i = start + lane
             image = row_image(local, remote, match, i, a_buf, own, peers, low, high, rhs.at[lane])
             mine = jnp.concatenate([own[i, n] for n in range(BLOCKS)], axis=1)

time: 407 us -> 406 us (level)
  no operation moved by 1% of the time
where the time goes in v11:
time: 406 us; the launch traced here: 405 us
  blocking collectives  301 us (74%)
  waiting for transfers between devices  41.6 us (10%)
  Pallas kernels  32.3 us (8%)
  starting transfers between devices  26.1 us (6%)
    all_to_all x3, blocking collectives, body(): lax.all_to_all(outgoing, GY, split_axis=0, concat_axis=0, tiled=True)  301 us
    ppermute x6, waiting for transfers between devices, around(): return lax.ppermute(value, GY, pairs)  28.5 us
    pallas_call x2, Pallas kernels, smooth(): pl.pallas_call(smooth_kernel, in_specs=[SMEM] * 4 + [VMEM] * 6, out_specs...  15.6 us
    ppermute x6, starting transfers between devices, shifted(): lax.ppermute(value, axis, [(source, source + steps) for source in range(f...  15.5 us
    ppermute x6, starting transfers between devices, around(): return lax.ppermute(value, GY, pairs)  9.43 us
    ppermute x6, waiting for transfers between devices, shifted(): lax.ppermute(value, axis, [(source, source + steps) for source in range(f...  8.9 us
  transfers between devices with their start and end apart: 17, of which 11 were waited for; matrix products, arithmetic and copies ran while one was open for 0% of the time, Pallas kernels for 4%

profile of v11, /device:TPU:0, one launch (start us, length us, event | category | flops | bytes accessed | tf_op | source)
XLA Modules:
  0.0 404.7 jit_solution(18034817074082244159)
XLA Ops:
  0.6 0.0 copy-start
  0.6 0.0 copy-start.7
  0.6 2.6 pick_rows.1
  3.2 3.9 collective-permute-start
  7.2 1.3 collective-permute-start.1
  8.5 0.0 copy-done
  8.5 0.0 copy-done.7
  8.5 0.0 slice-start
  8.5 1.8 pack_rows.1
  10.3 0.1 pad_add_fusion.here
  10.4 0.0 copy-start.5
  10.4 0.0 copy-start.6
  10.4 2.6 collective-permute-done.low
  13.0 4.2 %collective-permute-done.1.high = bf16[1,2,256,256]{3,2,1,0:T(8,128)(2,1)S(1)} collective-permute-done((bf16[1,2,256,256]{3,2,1,0:T(8,128)(2,1)}, bf16[1,2,256,256]{3,2,1,0:T(8,128)(2,1)S(1)}, u32[]{:S(2)}, u32[]{:S(2)}) %collective-permute-start.1) | collective-permute-done | bytes 262176 | tf_op jit(solution)/shard_map/ppermute | solution.py:24
  17.2 102.6 %all_to_all.15.peers = bf16[32,2,256,256]{3,2,1,0:T(8,128)(2,1)S(1)} all-to-all(bf16[32,2,256,256]{3,2,1,0:T(8,128)(2,1)S(1)} %pack_rows.1), channel_id=1, replica_groups=mesh['gx'=4,'x'=4,'y'=4,'c'=2] {'x','y','c'}, dimensions={0} | all-to-all | bytes 16777216 | tf_op jit(solution)/shard_map/all_to_all | solution.py:268
  119.8 0.0 slice-done
  119.8 0.0 slice-done.1
  119.8 0.0 copy-done.1
  119.8 0.0 copy-done.3
  119.8 2.3 slab_rows.2
  122.1 3.7 collective-permute-start.2
  125.8 1.3 collective-permute-start.3
  127.1 8.0 %smooth_rows.2 = (bf16[8,2,256,256]{3,2,1,0:T(8,128)(2,1)S(1)}, bf16[32,2,256,256]{3,2,1,0:T(8,128)(2,1)S(1)}) custom-call(s32[2,8]{1,0:T(2,128)S(1)} %bitcast.48, s32[4,8]{1,0:T(4,128)S(1)} %bitcast.43, s32[6,2,8]{2,1,0:T(2,128)S(1)} %bitcast.38, s32[1,32]{1,0:T(1,128)S(1)} %copy-done.7, bf16[8,6,256,256]{3,2,1,0:T(8,128)(2,1)S(1)} %bitcast.36, ...), custom_call_target="tpu_custom_call" | custom-call | flops 3758096384 | bytes 29360128 | tf_op jit(solution)/shard_map/smooth_rows/pallas_call | solution.py:181
  135.1 0.0 collective-permute-done.2.low
  135.1 0.9 collective-permute-done.3.high
  136.0 99.0 %all_to_all.16.peers = bf16[32,2,256,256]{3,2,1,0:T(8,128)(2,1)S(1)} all-to-all(bf16[32,2,256,256]{3,2,1,0:T(8,128)(2,1)S(1)} %get-tuple-element.65), channel_id=1, replica_groups=mesh['gx'=4,'x'=4,'y'=4,'c'=2] {'x','y','c'}, dimensions={0} | all-to-all | bytes 16777216 | tf_op jit(solution)/shard_map/all_to_all | solution.py:276
  235.0 2.2 slab_rows.3
  237.2 4.0 collective-permute-start.4
  241.2 1.3 collective-permute-start.5
  242.5 7.7 %smooth_rows.3 = (bf16[8,2,256,256]{3,2,1,0:T(8,128)(2,1)}, bf16[32,2,256,256]{3,2,1,0:T(8,128)(2,1)S(1)}) custom-call(s32[2,8]{1,0:T(2,128)S(1)} %bitcast.50, s32[4,8]{1,0:T(4,128)S(1)} %bitcast.45, s32[6,2,8]{2,1,0:T(2,128)S(1)} %bitcast.40, s32[1,32]{1,0:T(1,128)S(1)} %copy-done.7, bf16[8,6,256,256]{3,2,1,0:T(8,128)(2,1)S(1)} %bitcast.36, ...), custom_call_target="tpu_custom_call" | custom-call | flops 3758096384 | bytes 29360128 | tf_op jit(solution)/shard_map/smooth_rows/pallas_call | solution.py:181
  250.2 0.0 collective-permute-done.4.low
  250.2 1.2 collective-permute-done.5.high
  251.4 99.1 %all_to_all.17.peers = bf16[32,2,256,256]{3,2,1,0:T(8,128)(2,1)S(1)} all-to-all(bf16[32,2,256,256]{3,2,1,0:T(8,128)(2,1)S(1)} %get-tuple-element.81), channel_id=1, replica_groups=mesh['gx'=4,'x'=4,'y'=4,'c'=2] {'x','y','c'}, dimensions={0} | all-to-all | bytes 16777216 | tf_op jit(solution)/shard_map/all_to_all | solution.py:276
  350.5 7.9 %galerkin_rows.1 = bf16[8,8,256,256]{3,2,1,0:T(8,128)(2,1)S(1)} custom-call(s32[2,8]{1,0:T(2,128)S(1)} %bitcast.51, s32[4,8]{1,0:T(4,128)S(1)} %bitcast.46, s32[6,2,8]{2,1,0:T(2,128)S(1)} %bitcast.41, s32[2,2,8]{2,1,0:T(2,128)S(1)} %bitcast.52, s32[3]{0:T(128)S(1)} %pad_add_fusion.here, bf16[8,6,256,256]{3,2,1,0:T(8,128)(2,1)S(1)} %bitcast.36, ...), custom_call_target="tpu_custom_call" | custom-call | tf_op jit(solution)/shard_map/galerkin_rows/pallas_call | solution.py:231
  358.4 0.3 slice_bitcast_fusion
  358.7 0.5 collective-permute-start.9
  359.1 0.1 collective-permute-start.8
  359.3 0.4 collective-permute-start.7
  359.6 0.1 collective-permute-start.6
  359.8 1.6 collective-permute-done.9
  361.4 0.3 fusion
  361.7 1.2 collective-permute-done.8
  362.9 1.6 collective-permute-start.11
  364.5 0.3 fusion.1
  364.8 0.0 collective-permute-done.7
  364.8 0.9 collective-permute-start.10
  365.7 0.3 fusion.2
  366.0 0.0 collective-permute-done.6
  366.0 2.5 collective-permute-start.12
  368.5 0.3 fusion.3
  368.8 10.5 %collective-permute-done.11 = bf16[8,256,256]{2,1,0:T(8,128)(2,1)S(1)} collective-permute-done((bf16[8,256,256]{2,1,0:T(8,128)(2,1)S(1)}, bf16[8,256,256]{2,1,0:T(8,128)(2,1)S(1)}, u32[]{:S(2)}, u32[]{:S(2)}) %collective-permute-start.11) | collective-permute-done | bytes 1048608 | tf_op jit(solution)/shard_map/ppermute | solution.py:34
  379.3 11.1 %collective-permute-done.10 = bf16[8,256,256]{2,1,0:T(8,128)(2,1)S(1)} collective-permute-done((bf16[8,256,256]{2,1,0:T(8,128)(2,1)S(1)}, bf16[8,256,256]{2,1,0:T(8,128)(2,1)S(1)}, u32[]{:S(2)}, u32[]{:S(2)}) %collective-permute-start.10) | collective-permute-done | bytes 1048608 | tf_op jit(solution)/shard_map/ppermute | solution.py:34
  390.5 0.0 collective-permute-done.12
  390.5 0.6 add_convert_fusion.1
  391.0 0.6 collective-permute-start.13
  391.6 2.4 collective-permute-start.14
  394.1 1.5 collective-permute-start.15
  395.5 6.0 %collective-permute-done.13 = bf16[2,256,256]{2,1,0:T(8,128)(2,1)S(1)} collective-permute-done((bf16[2,256,256]{2,1,0:T(8,128)(2,1)S(1)}, bf16[2,256,256]{2,1,0:T(8,128)(2,1)S(1)}, u32[]{:S(2)}, u32[]{:S(2)}) %collective-permute-start.13) | collective-permute-done | bytes 262176 | tf_op jit(solution)/shard_map/ppermute | solution.py:34
  401.5 0.0 collective-permute-done.14
  401.5 0.9 collective-permute-done.15
  402.4 0.1 add_convert_fusion
  402.6 0.1 collective-permute-start.16
  402.6 1.3 collective-permute-done.16
  404.0 0.7 pad_maximum_fusion
  (14 shorter events, 0.1 us)
Async XLA Ops:
  0.6 7.8 %copy-start = (bf16[8,2,256,256]{3,2,1,0:T(8,128)(2,1)S(1)}, bf16[8,2,256,256]{3,2,1,0:T(8,128)(2,1)}, u32[]{:S(2)}) copy-start(bf16[8,2,256,256]{3,2,1,0:T(8,128)(2,1)} %own.2) | copy-start | bytes 6291460
  0.6 7.8 %copy-start.7 = (s32[1,32]{1,0:T(1,128)S(1)}, s32[1,32]{1,0:T(1,128)}, u32[]{:S(2)}) copy-start(s32[1,32]{1,0:T(1,128)} %peer.5) | copy-start | bytes 388
  3.2 9.8 %collective-permute-start = (bf16[1,2,256,256]{3,2,1,0:T(8,128)(2,1)}, bf16[1,2,256,256]{3,2,1,0:T(8,128)(2,1)S(1)}, u32[]{:S(2)}, u32[]{:S(2)}) collective-permute-start(bf16[1,2,256,256]{3,2,1,0:T(8,128)(2,1)} %get-tuple-element.48), channel_id=1, source_target_pairs={{0,32},{32,64},{64,96},{1,33},{33,65},{65,97},{2,34},{34,66},{66,9... | collective-permute-start | bytes 786440 | tf_op jit(solution)/shard_map/ppermute | solution.py:24
  7.2 10.0 %collective-permute-start.1 = (bf16[1,2,256,256]{3,2,1,0:T(8,128)(2,1)}, bf16[1,2,256,256]{3,2,1,0:T(8,128)(2,1)S(1)}, u32[]{:S(2)}, u32[]{:S(2)}) collective-permute-start(bf16[1,2,256,256]{3,2,1,0:T(8,128)(2,1)} %get-tuple-element.49), channel_id=1, source_target_pairs={{32,0},{64,32},{96,64},{33,1},{65,33},{97,65},{34,2},{66,34},{98,6... | collective-permute-start | bytes 786440 | tf_op jit(solution)/shard_map/ppermute | solution.py:24
  8.5 111.3 %slice-start = ((s8[6291456]{0:T(1024)(128)(4,1)}), s8[4194304]{0:T(1024)(128)(4,1)S(1)}, s32[]{:S(2)}) async-start(s8[6291456]{0:T(1024)(128)(4,1)} %bitcast.35), calls=%async_computation.3 | async-start | bytes 8388608
  10.4 109.4 %slice-start.1 = ((s8[6291456]{0:T(1024)(128)(4,1)}), s8[2097152]{0:T(1024)(128)(4,1)S(1)}, s32[]{:S(2)}) async-start(s8[6291456]{0:T(1024)(128)(4,1)} %bitcast.35), calls=%async_computation.4 | async-start | bytes 4194304
  10.4 109.4 %copy-start.1 = (bf16[8,256,256]{2,1,0:T(8,128)(2,1)S(1)}, bf16[8,256,256]{2,1,0:T(8,128)(2,1)}, u32[]{:S(2)}) copy-start(bf16[8,256,256]{2,1,0:T(8,128)(2,1)} %d_buf.5) | copy-start | bytes 3145732
  10.4 109.4 %copy-start.3 = (s32[8,6,2]{0,2,1:T(2,128)S(1)}, s32[8,6,2]{0,2,1:T(2,128)}, u32[]{:S(2)}) copy-start(s32[8,6,2]{0,2,1:T(2,128)} %param.12) | copy-start | bytes 1156
  10.4 109.4 %copy-start.4 = (s32[8,4]{0,1:T(4,128)S(1)}, s32[8,4]{0,1:T(4,128)}, u32[]{:S(2)}) copy-start(s32[8,4]{0,1:T(4,128)} %param.11) | copy-start | bytes 388
  10.4 109.4 %copy-start.5 = (s32[8,2]{0,1:T(2,128)S(1)}, s32[8,2]{0,1:T(2,128)}, u32[]{:S(2)}) copy-start(s32[8,2]{0,1:T(2,128)} %param.10) | copy-start | bytes 196
  10.4 109.4 %copy-start.6 = (s32[1,2]{1,0:T(1,128)S(1)}, s32[1,2]{1,0:T(1,128)}, u32[]{:S(2)}) copy-start(s32[1,2]{1,0:T(1,128)} %slab.5) | copy-start | bytes 28
  122.1 13.0 %collective-permute-start.2 = (bf16[1,2,256,256]{3,2,1,0:T(8,128)(2,1)S(1)}, bf16[1,2,256,256]{3,2,1,0:T(8,128)(2,1)S(1)}, u32[]{:S(2)}, u32[]{:S(2)}) collective-permute-start(bf16[1,2,256,256]{3,2,1,0:T(8,128)(2,1)S(1)} %get-tuple-element.63), channel_id=1, source_target_pairs={{0,32},{32,64},{64,96},{1,33},{33,65},{65,97},{2,34},{34,66},{66,9... | collective-permute-start | bytes 786440 | tf_op jit(solution)/shard_map/ppermute | solution.py:24
  125.8 10.2 %collective-permute-start.3 = (bf16[1,2,256,256]{3,2,1,0:T(8,128)(2,1)S(1)}, bf16[1,2,256,256]{3,2,1,0:T(8,128)(2,1)S(1)}, u32[]{:S(2)}, u32[]{:S(2)}) collective-permute-start(bf16[1,2,256,256]{3,2,1,0:T(8,128)(2,1)S(1)} %get-tuple-element.64), channel_id=1, source_target_pairs={{32,0},{64,32},{96,64},{33,1},{65,33},{97,65},{34,2},{66,34},{98,6... | collective-permute-start | bytes 786440 | tf_op jit(solution)/shard_map/ppermute | solution.py:24
  237.2 13.0 %collective-permute-start.4 = (bf16[1,2,256,256]{3,2,1,0:T(8,128)(2,1)S(1)}, bf16[1,2,256,256]{3,2,1,0:T(8,128)(2,1)S(1)}, u32[]{:S(2)}, u32[]{:S(2)}) collective-permute-start(bf16[1,2,256,256]{3,2,1,0:T(8,128)(2,1)S(1)} %get-tuple-element.79), channel_id=1, source_target_pairs={{0,32},{32,64},{64,96},{1,33},{33,65},{65,97},{2,34},{34,66},{66,9... | collective-permute-start | bytes 786440 | tf_op jit(solution)/shard_map/ppermute | solution.py:24
  241.2 10.2 %collective-permute-start.5 = (bf16[1,2,256,256]{3,2,1,0:T(8,128)(2,1)S(1)}, bf16[1,2,256,256]{3,2,1,0:T(8,128)(2,1)S(1)}, u32[]{:S(2)}, u32[]{:S(2)}) collective-permute-start(bf16[1,2,256,256]{3,2,1,0:T(8,128)(2,1)S(1)} %get-tuple-element.80), channel_id=1, source_target_pairs={{32,0},{64,32},{96,64},{33,1},{65,33},{97,65},{34,2},{66,34},{98,6... | collective-permute-start | bytes 786440 | tf_op jit(solution)/shard_map/ppermute | solution.py:24
  251.4 99.1 %copy-start.2 = (bf16[8,2,256,256]{3,2,1,0:T(8,128)(2,1)S(1)}, bf16[8,2,256,256]{3,2,1,0:T(8,128)(2,1)}, u32[]{:S(2)}) copy-start(bf16[8,2,256,256]{3,2,1,0:T(8,128)(2,1)} %get-tuple-element.46.own) | copy-start | bytes 6291460
  251.4 99.1 %copy-start.8 = (s32[8,2,2]{0,2,1:T(2,128)S(1)}, s32[8,2,2]{0,2,1:T(2,128)}, u32[]{:S(2)}) copy-start(s32[8,2,2]{0,2,1:T(2,128)} %param.17) | copy-start | bytes 388
  358.7 2.7 collective-permute-start.9
  359.1 3.8 collective-permute-start.8
  359.3 5.5 %collective-permute-start.7 = (bf16[8,256,256]{2,1,0:T(8,128)(2,1)S(1)}, bf16[8,256,256]{2,1,0:T(8,128)(2,1)S(1)}, u32[]{:S(2)}, u32[]{:S(2)}) collective-permute-start(bf16[8,256,256]{2,1,0:T(8,128)(2,1)S(1)} %get-tuple-element.96), channel_id=1, source_target_pairs={{0,1},{1,0},{2,3},{3,2},{4,5},{5,4},{6,7},{7,6},{8,9},{9,8},{10,11... | collective-permute-start | bytes 3145736 | tf_op jit(solution)/shard_map/ppermute | solution.py:278
  359.6 6.3 %collective-permute-start.6 = (bf16[8,256,256]{2,1,0:T(8,128)(2,1)S(1)}, bf16[8,256,256]{2,1,0:T(8,128)(2,1)S(1)}, u32[]{:S(2)}, u32[]{:S(2)}) collective-permute-start(bf16[8,256,256]{2,1,0:T(8,128)(2,1)S(1)} %get-tuple-element.97), channel_id=1, source_target_pairs={{0,1},{1,0},{2,3},{3,2},{4,5},{5,4},{6,7},{7,6},{8,9},{9,8},{10,11... | collective-permute-start | bytes 3145736 | tf_op jit(solution)/shard_map/ppermute | solution.py:278
  362.9 16.4 %collective-permute-start.11 = (bf16[8,256,256]{2,1,0:T(8,128)(2,1)S(1)}, bf16[8,256,256]{2,1,0:T(8,128)(2,1)S(1)}, u32[]{:S(2)}, u32[]{:S(2)}) collective-permute-start(bf16[8,256,256]{2,1,0:T(8,128)(2,1)S(1)} %fusion), channel_id=1, source_target_pairs={{0,16},{1,5},{2,18},{3,7},{4,20},{5,1},{6,22},{7,3},{8,24},{9,13},... | collective-permute-start | bytes 3145736 | tf_op jit(solution)/shard_map/ppermute | solution.py:34
  364.8 25.7 %collective-permute-start.10 = (bf16[8,256,256]{2,1,0:T(8,128)(2,1)S(1)}, bf16[8,256,256]{2,1,0:T(8,128)(2,1)S(1)}, u32[]{:S(2)}, u32[]{:S(2)}) collective-permute-start(bf16[8,256,256]{2,1,0:T(8,128)(2,1)S(1)} %fusion.1), channel_id=1, source_target_pairs={{0,8},{1,3},{2,10},{3,5},{4,12},{5,7},{6,14},{7,1},{8,16},{9,11},{... | collective-permute-start | bytes 3145736 | tf_op jit(solution)/shard_map/ppermute | solution.py:34
  366.0 24.5 %collective-permute-start.12 = (bf16[8,256,256]{2,1,0:T(8,128)(2,1)S(1)}, bf16[8,256,256]{2,1,0:T(8,128)(2,1)S(1)}, u32[]{:S(2)}, u32[]{:S(2)}) collective-permute-start(bf16[8,256,256]{2,1,0:T(8,128)(2,1)S(1)} %fusion.2), channel_id=1, source_target_pairs={{0,24},{1,7},{2,26},{3,1},{4,28},{5,3},{6,30},{7,5},{8,0},{9,15},{... | collective-permute-start | bytes 3145736 | tf_op jit(solution)/shard_map/ppermute | solution.py:34
  391.0 10.5 %collective-permute-start.13 = (bf16[2,256,256]{2,1,0:T(8,128)(2,1)S(1)}, bf16[2,256,256]{2,1,0:T(8,128)(2,1)S(1)}, u32[]{:S(2)}, u32[]{:S(2)}) collective-permute-start(bf16[2,256,256]{2,1,0:T(8,128)(2,1)S(1)} %get-tuple-element.91), channel_id=1, source_target_pairs={{0,2},{1,9},{2,4},{3,11},{4,6},{5,13},{6,0},{7,15},{8,10},{9,17},{... | collective-permute-start | bytes 786440 | tf_op jit(solution)/shard_map/ppermute | solution.py:34
  391.6 9.9 %collective-permute-start.14 = (bf16[2,256,256]{2,1,0:T(8,128)(2,1)S(1)}, bf16[2,256,256]{2,1,0:T(8,128)(2,1)S(1)}, u32[]{:S(2)}, u32[]{:S(2)}) collective-permute-start(bf16[2,256,256]{2,1,0:T(8,128)(2,1)S(1)} %get-tuple-element.92), channel_id=1, source_target_pairs={{0,4},{1,17},{2,6},{3,19},{4,0},{5,21},{6,2},{7,23},{8,12},{9,25},... | collective-permute-start | bytes 786440 | tf_op jit(solution)/shard_map/ppermute | solution.py:34
  394.1 8.3 %collective-permute-start.15 = (bf16[2,256,256]{2,1,0:T(8,128)(2,1)S(1)}, bf16[2,256,256]{2,1,0:T(8,128)(2,1)S(1)}, u32[]{:S(2)}, u32[]{:S(2)}) collective-permute-start(bf16[2,256,256]{2,1,0:T(8,128)(2,1)S(1)} %get-tuple-element.93), channel_id=1, source_target_pairs={{0,6},{1,25},{2,0},{3,27},{4,2},{5,29},{6,4},{7,31},{8,14},{9,1},{... | collective-permute-start | bytes 786440 | tf_op jit(solution)/shard_map/ppermute | solution.py:34
  402.6 1.4 collective-permute-start.16
